TPU v7x, 32 devices: a whole 2x2x4 slice. The times are simulated.
32 devices in a mesh: ctx: 16 (over z, y, core), fsdp: 2 (over x).
Axes of the slice: x: 2, y: 2, z: 4, core: 2. Of those that a mesh axis runs over, the one named last changes fastest.
Arguments:
- tokens: bfloat16 [4096, 768], P(('fsdp', 'ctx')), may hold values from -6 to 6
- encoded: bfloat16 [4096, 768], P(('fsdp', 'ctx')), may hold values from -6 to 6
- cotangent: bfloat16 [4096, 768], P(('fsdp', 'ctx')), may hold values from -6 to 6
- tgt_lengths: int32 [2, 6], P('fsdp'), may hold values from 1 to 1984, 2048 in all within a row
- enc_lengths: int32 [2, 6], P('fsdp'), may hold values from 1 to 1984, 2048 in all within a row
- deal: int32 [2, 6], P('fsdp'), may hold values from 0 to 5, each once within a row
- ln_self: float32 [768], P('fsdp'), may hold values from 0.1 to 1.9
- ln_cross: float32 [768], P('fsdp'), may hold values from 0.1 to 1.9
- ln_ffn: float32 [768], P('fsdp'), may hold values from 0.1 to 1.9
- bias_table: float32 [32, 12], P('fsdp'), may hold values from -4 to 4
- self_query: float32 [768, 768], P('fsdp'), may hold values from -0.0546875 to 0.0546875
- self_key: float32 [768, 768], P('fsdp'), may hold values from -0.21875 to 0.21875
- self_value: float32 [768, 768], P('fsdp'), may hold values from -0.21875 to 0.21875
- self_output: float32 [768, 768], P('fsdp'), may hold values from -1.25 to 1.25
- cross_query: float32 [768, 768], P('fsdp'), may hold values from -0.0546875 to 0.0546875
- cross_key: float32 [768, 768], P('fsdp'), may hold values from -0.21875 to 0.21875
- cross_value: float32 [768, 768], P('fsdp'), may hold values from -0.21875 to 0.21875
- cross_output: float32 [768, 768], P('fsdp'), may hold values from -1.25 to 1.25
- ffn_inner: float32 [768, 3072], P('fsdp'), may hold values from -0.21875 to 0.21875
- ffn_outer: float32 [3072, 768], P('fsdp'), may hold values from -0.109375 to 0.109375
Outputs:
- output: float32 [4096, 768], P(('fsdp', 'ctx'))
- tokens_grad: float32 [4096, 768], P(('fsdp', 'ctx'))
- encoded_grad: float32 [4096, 768], P(('fsdp', 'ctx'))
- ln_self_grad: float32 [768], P('fsdp')
- ln_cross_grad: float32 [768], P('fsdp')
- ln_ffn_grad: float32 [768], P('fsdp')
- bias_table_grad: float32 [32, 12], P('fsdp')
- self_query_grad: float32 [768, 768], P('fsdp')
- self_key_grad: float32 [768, 768], P('fsdp')
- self_value_grad: float32 [768, 768], P('fsdp')
- self_output_grad: float32 [768, 768], P('fsdp')
- cross_query_grad: float32 [768, 768], P('fsdp')
- cross_key_grad: float32 [768, 768], P('fsdp')
- cross_value_grad: float32 [768, 768], P('fsdp')
- cross_output_grad: float32 [768, 768], P('fsdp')
- ffn_inner_grad: float32 [768, 3072], P('fsdp')
- ffn_outer_grad: float32 [3072, 768], P('fsdp')
Inputs may be any that keep to these rules, and one draw needn't show every extreme that they name: `tgt_lengths`: each row holds the lengths of the 6 target sequences of one group in packed order, summing to 2048; the longest is exactly 1984. `enc_lengths`: each row holds the lengths of the 6 encoder sequences of one group in packed order, summing to 2048; the longest is exactly 1984. `deal`: each row is a permutation of the 6 encoder sequences of the group.
All inputs are finite; a program needn't handle non-finite values.
Results may differ from a plain program's by a relative error of at most 0.03.
The roundings to bfloat16 on the way count: a program that leaves them out, or rounds other values in their place, can miss the bound.
Values may be sent and summed in bfloat16 or wider, within the bound.
No kernel may reach another device: no remote copies, remote signals or barrier semaphores. Data moves between devices by JAX's collectives and lax.ppermute only.
A program may use at most 192 MiB of HBM per device.

v0:
```python
import math

import jax
import jax.numpy as jnp
from jax import lax
from jax.sharding import PartitionSpec as P

HEADS = 12
HEAD_DIM = 64


EPS = 1e-06
NEG = -1e30
GELU_C = 0.7978845608028654
GELU_A = 0.044715


def shifted(value, axis, by):
    size = lax.axis_size(axis)
    return lax.ppermute(value, axis, [(i, (i + by) % size) for i in range(size)])


def from_behind(block, axis, distance):
    devices = range(lax.axis_size(axis))
    route = [(i - distance, i) for i in devices if i - distance in devices]
    return lax.ppermute(block, axis, route)


def bucket_edges():
    edges = []
    for level in range(1, 16):
        distance = 16
        while int(math.log(distance / 16.0) / math.log(8.0) * 16.0) < level:
            distance += 1
        edges.append(distance)
    return edges


def bucket_of(distance):
    clipped = jnp.maximum(distance, 0).astype(jnp.int32)
    large = jnp.full(clipped.shape, 16, jnp.int32)
    for edge in bucket_edges():
        large = large + (clipped >= edge).astype(jnp.int32)
    return jnp.where(clipped < 16, clipped, large)


def seg_ids(index, lengths):
    ends = jnp.cumsum(lengths).astype(jnp.int32)
    return jnp.sum((index[:, None] >= ends[None, :]).astype(jnp.int32), axis=1).astype(jnp.int32)


def rms_forward(value, gain):
    inverse = lax.rsqrt(jnp.mean(value * value, axis=-1, keepdims=True) + EPS)
    return (value * inverse * gain, inverse)


def rms_backward(value, inverse, gain, grad):
    scaled = grad * gain
    cubed = inverse * inverse * inverse
    dvalue = inverse * scaled - value * cubed * jnp.mean(scaled * value, axis=-1, keepdims=True)
    return (dvalue, jnp.sum(grad * value * inverse, axis=0))


def gelu_parts(value):
    tangent = jnp.tanh(GELU_C * (value + GELU_A * value * value * value))
    result = 0.5 * value * (1.0 + tangent)
    slope = 0.5 * (1.0 + tangent) + 0.5 * value * (1.0 - tangent * tangent) * GELU_C * (
        1.0 + 3.0 * GELU_A * value * value
    )
    return (result, slope)


def project(left, right):
    return jnp.dot(left, right, preferred_element_type=jnp.float32)


def weight_grad(left, right):
    return jnp.einsum("td,te->de", left, right, preferred_element_type=jnp.float32)


def back_project(grad, weight):
    return jnp.einsum("te,de->td", grad, weight, preferred_element_type=jnp.float32)


def heads_of(value):
    return value.reshape(value.shape[0], HEADS, HEAD_DIM)


def self_allowed(q_index, key_index, lengths):
    q_seg = seg_ids(q_index, lengths)
    key_seg = seg_ids(key_index, lengths)
    distance = q_index[:, None] - key_index[None, :]
    return ((q_seg[:, None] == key_seg[None, :]) & (distance >= 0), distance)


def cross_allowed(q_pair, enc_index, enc_sizes):
    return q_pair[:, None] == seg_ids(enc_index, enc_sizes)[None, :]


def bias_onehot(distance, buckets):
    return (
        bucket_of(distance)[:, :, None] == jnp.arange(buckets, dtype=jnp.int32)[None, None, :]
    ).astype(jnp.bfloat16)


def keep_state(state):
    return state


def masked_scores(query, keys, allowed, bias):
    scores = jnp.einsum("qhd,khd->hqk", query, keys, preferred_element_type=jnp.float32)
    if bias is not None:
        scores = scores + bias
    return jnp.where(allowed[None], scores, NEG)


def stats_step(state, query, keys, allowed, bias):
    peak, total = state
    scores = masked_scores(query, keys, allowed, bias)
    new_peak = jnp.maximum(peak, jnp.max(scores, axis=2))
    weights = jnp.where(allowed[None], jnp.exp(scores - new_peak[:, :, None]), 0.0)
    return (new_peak, total * jnp.exp(peak - new_peak) + jnp.sum(weights, axis=2))


def value_step(running, query, keys, values, allowed, bias, lse):
    scores = masked_scores(query, keys, allowed, bias)
    probs = jnp.where(allowed[None], jnp.exp(scores - lse[:, :, None]), 0.0).astype(jnp.bfloat16)
    return running + jnp.einsum("hqk,khd->hqd", probs, values, preferred_element_type=jnp.float32)


def fold_blocks(state, piece, start, block_fn):
    count = piece[0].shape[0]
    block = math.gcd(count, 512)
    if block == count:
        return block_fn(state, piece, start)

    def advance(current, offset):
        part = tuple((lax.dynamic_slice_in_dim(item, offset, block, 0) for item in piece))
        return (block_fn(current, part, start + offset), None)

    result, unused = lax.scan(advance, state, jnp.arange(count // block, dtype=jnp.int32) * block)
    return result


def grad_block(query, keys, values, dout, lse, delta, allowed, bias):
    scores = jnp.einsum("qhd,khd->hqk", query, keys, preferred_element_type=jnp.float32)
    if bias is not None:
        scores = scores + bias
    probs = jnp.where(allowed[None], jnp.exp(scores - lse[:, :, None]), 0.0)
    dvalues = jnp.einsum(
        "hqk,qhd->khd", probs.astype(jnp.bfloat16), dout, preferred_element_type=jnp.float32
    )
    dprobs = jnp.einsum("qhd,khd->hqk", dout, values, preferred_element_type=jnp.float32)
    dscores = (probs * (dprobs - delta[:, :, None])).astype(jnp.bfloat16)
    dquery = jnp.einsum("hqk,khd->qhd", dscores, keys, preferred_element_type=jnp.float32)
    dkeys = jnp.einsum("hqk,qhd->khd", dscores, query, preferred_element_type=jnp.float32)
    return (dquery, dkeys, dvalues, dscores)


def on_device(
    tokens,
    encoded,
    cotangent,
    tgt_lengths,
    enc_lengths,
    deal,
    ln_self,
    ln_cross,
    ln_ffn,
    bias_table,
    self_query,
    self_key,
    self_value,
    self_output,
    cross_query,
    cross_key,
    cross_value,
    cross_output,
    ffn_inner,
    ffn_outer,
):
    full = (
        lax.all_gather(ln_self.astype(jnp.bfloat16), "fsdp", axis=0, tiled=True),
        lax.all_gather(ln_cross.astype(jnp.bfloat16), "fsdp", axis=0, tiled=True),
        lax.all_gather(ln_ffn.astype(jnp.bfloat16), "fsdp", axis=0, tiled=True),
        lax.all_gather(bias_table.astype(jnp.bfloat16), "fsdp", axis=0, tiled=True),
        lax.all_gather(self_query.astype(jnp.bfloat16), "fsdp", axis=0, tiled=True),
        lax.all_gather(self_key.astype(jnp.bfloat16), "fsdp", axis=0, tiled=True),
        lax.all_gather(self_value.astype(jnp.bfloat16), "fsdp", axis=0, tiled=True),
        lax.all_gather(self_output.astype(jnp.bfloat16), "fsdp", axis=0, tiled=True),
        lax.all_gather(cross_query.astype(jnp.bfloat16), "fsdp", axis=0, tiled=True),
        lax.all_gather(cross_key.astype(jnp.bfloat16), "fsdp", axis=0, tiled=True),
        lax.all_gather(cross_value.astype(jnp.bfloat16), "fsdp", axis=0, tiled=True),
        lax.all_gather(cross_output.astype(jnp.bfloat16), "fsdp", axis=0, tiled=True),
        lax.all_gather(ffn_inner.astype(jnp.bfloat16), "fsdp", axis=0, tiled=True),
        lax.all_gather(ffn_outer.astype(jnp.bfloat16), "fsdp", axis=0, tiled=True),
    )
    gain_self = full[0].astype(jnp.float32)
    gain_cross = full[1].astype(jnp.float32)
    gain_ffn = full[2].astype(jnp.float32)
    table_full = full[3]
    full_self_query, full_self_key, full_self_value, full_self_output = (
        full[4],
        full[5],
        full[6],
        full[7],
    )
    full_cross_query, full_cross_key, full_cross_value, full_cross_output = (
        full[8],
        full[9],
        full[10],
        full[11],
    )
    full_inner, full_outer = (full[12], full[13])
    buckets = table_full.shape[0]
    row_count = tokens.shape[0]
    enc_count = encoded.shape[0]
    width = tokens.shape[1]
    ctx_count = lax.axis_size("ctx")
    my_index = lax.axis_index("ctx")
    lengths = tgt_lengths[0]
    enc_sizes = enc_lengths[0]
    pairing = deal[0]
    row_iota = jnp.arange(row_count, dtype=jnp.int32)
    enc_iota = jnp.arange(enc_count, dtype=jnp.int32)
    q_index = my_index * row_count + row_iota
    q_seg = seg_ids(q_index, lengths)
    choose = q_seg[:, None] == jnp.arange(pairing.shape[0], dtype=jnp.int32)[None, :]
    q_pair = jnp.sum(jnp.where(choose, pairing[None, :], 0), axis=1).astype(jnp.int32)

    def stats_init():
        return (
            jnp.full((HEADS, row_count), NEG, jnp.float32),
            jnp.zeros((HEADS, row_count), jnp.float32),
        )

    def running_init():
        return jnp.zeros((HEADS, row_count, HEAD_DIM), jnp.float32)

    def to_rows(running):
        return jnp.transpose(running, (1, 0, 2)).reshape(row_count, width)

    def self_bias(distance):
        return jnp.einsum(
            "qkb,bh->hqk",
            bias_onehot(distance, buckets),
            table_full,
            preferred_element_type=jnp.float32,
        )

    x_start = tokens.astype(jnp.float32)
    normed_self, inverse_self = rms_forward(x_start, gain_self)
    in_self = normed_self.astype(jnp.bfloat16)
    query_self = project(in_self, full_self_query).astype(jnp.bfloat16)
    key_self = project(in_self, full_self_key).astype(jnp.bfloat16)
    value_self = project(in_self, full_self_value).astype(jnp.bfloat16)
    query_heads = heads_of(query_self)

    def self_stat_block(state, piece, start):
        key_index = start + jnp.arange(piece[0].shape[0], dtype=jnp.int32)
        allowed, distance = self_allowed(q_index, key_index, lengths)

        def compute(current):
            return stats_step(
                current, query_heads, heads_of(piece[0]), allowed, self_bias(distance)
            )

        return lax.cond(jnp.any(allowed), compute, keep_state, state)

    peak_self, total_self = fold_blocks(
        stats_init(),
        (lax.all_gather(key_self, "ctx", axis=0, tiled=True),),
        jnp.int32(0),
        self_stat_block,
    )
    lse_self = peak_self + jnp.log(total_self)

    def self_value_block(running, piece, start):
        key_index = start + jnp.arange(piece[0].shape[0], dtype=jnp.int32)
        allowed, distance = self_allowed(q_index, key_index, lengths)

        def compute(current):
            return value_step(
                current,
                query_heads,
                heads_of(piece[0]),
                heads_of(piece[1]),
                allowed,
                self_bias(distance),
                lse_self,
            )

        return lax.cond(jnp.any(allowed), compute, keep_state, running)

    attn_self = to_rows(
        fold_blocks(
            running_init(),
            (
                lax.all_gather(key_self, "ctx", axis=0, tiled=True),
                lax.all_gather(value_self, "ctx", axis=0, tiled=True),
            ),
            jnp.int32(0),
            self_value_block,
        )
    )
    attn_self_low = attn_self.astype(jnp.bfloat16)
    x_mid = x_start + project(attn_self_low, full_self_output)
    normed_cross, inverse_cross = rms_forward(x_mid, gain_cross)
    in_cross = normed_cross.astype(jnp.bfloat16)
    query_cross = project(in_cross, full_cross_query).astype(jnp.bfloat16)
    key_cross = project(encoded, full_cross_key).astype(jnp.bfloat16)
    value_cross = project(encoded, full_cross_value).astype(jnp.bfloat16)
    query_cross_heads = heads_of(query_cross)

    def cross_stat_block(state, piece, start):
        enc_index = start + jnp.arange(piece[0].shape[0], dtype=jnp.int32)
        allowed = cross_allowed(q_pair, enc_index, enc_sizes)

        def compute(current):
            return stats_step(current, query_cross_heads, heads_of(piece[0]), allowed, None)

        return lax.cond(jnp.any(allowed), compute, keep_state, state)

    peak_cross, total_cross = fold_blocks(
        stats_init(),
        (lax.all_gather(key_cross, "ctx", axis=0, tiled=True),),
        jnp.int32(0),
        cross_stat_block,
    )
    lse_cross = peak_cross + jnp.log(total_cross)

    def cross_value_block(running, piece, start):
        enc_index = start + jnp.arange(piece[0].shape[0], dtype=jnp.int32)
        allowed = cross_allowed(q_pair, enc_index, enc_sizes)

        def compute(current):
            return value_step(
                current,
                query_cross_heads,
                heads_of(piece[0]),
                heads_of(piece[1]),
                allowed,
                None,
                lse_cross,
            )

        return lax.cond(jnp.any(allowed), compute, keep_state, running)

    attn_cross = to_rows(
        fold_blocks(
            running_init(),
            (
                lax.all_gather(key_cross, "ctx", axis=0, tiled=True),
                lax.all_gather(value_cross, "ctx", axis=0, tiled=True),
            ),
            jnp.int32(0),
            cross_value_block,
        )
    )
    attn_cross_low = attn_cross.astype(jnp.bfloat16)
    x_late = x_mid + project(attn_cross_low, full_cross_output)
    normed_ffn, inverse_ffn = rms_forward(x_late, gain_ffn)
    in_ffn = normed_ffn.astype(jnp.bfloat16)
    pre_act = project(in_ffn, full_inner)
    activated, slope = gelu_parts(pre_act)
    hidden = activated.astype(jnp.bfloat16)
    output = x_late + project(hidden, full_outer)
    d_outer = weight_grad(hidden, cotangent)
    d_hidden = back_project(cotangent, full_outer)
    d_pre = (d_hidden * slope).astype(jnp.bfloat16)
    d_inner = weight_grad(in_ffn, d_pre)
    d_normed_ffn = back_project(d_pre, full_inner)
    dx_ffn, d_gain_ffn = rms_backward(x_late, inverse_ffn, gain_ffn, d_normed_ffn)
    grad_late = cotangent.astype(jnp.float32) + dx_ffn
    grad_late_low = grad_late.astype(jnp.bfloat16)
    d_cross_output = weight_grad(attn_cross_low, grad_late_low)
    go_cross = back_project(grad_late_low, full_cross_output).astype(jnp.bfloat16)
    dout_cross = heads_of(go_cross)
    delta_cross = jnp.einsum("qhd,qhd->hq", dout_cross.astype(jnp.float32), heads_of(attn_cross))

    def cross_turn(step, carry):
        held, moving, d_query = carry
        anchor = jnp.mod(my_index - step, ctx_count)
        enc_index = anchor * enc_count + enc_iota
        allowed = cross_allowed(q_pair, enc_index, enc_sizes)

        def compute(unused):
            d_q, d_k, d_v, d_s = grad_block(
                query_cross_heads,
                heads_of(held[0]),
                heads_of(held[1]),
                dout_cross,
                lse_cross,
                delta_cross,
                allowed,
                None,
            )
            return (
                d_q.reshape(row_count, width),
                jnp.stack([d_k.reshape(enc_count, width), d_v.reshape(enc_count, width)]),
            )

        def cross_skip(unused):
            return (
                jnp.zeros((row_count, width), jnp.float32),
                jnp.zeros((2, enc_count, width), jnp.float32),
            )

        d_q_add, d_kv_add = lax.cond(jnp.any(allowed), compute, cross_skip, 0)
        held = shifted(held, "ctx", 1)
        moving = shifted(moving + d_kv_add, "ctx", 1)
        return (held, moving, d_query + d_q_add)

    returned = lax.fori_loop(
        0,
        ctx_count,
        cross_turn,
        (
            jnp.stack([key_cross, value_cross]),
            jnp.zeros((2, enc_count, width), jnp.float32),
            jnp.zeros((row_count, width), jnp.float32),
        ),
    )
    dq_cross = returned[2].astype(jnp.bfloat16)
    dk_cross = returned[1][0].astype(jnp.bfloat16)
    dv_cross = returned[1][1].astype(jnp.bfloat16)
    d_cross_query = weight_grad(in_cross, dq_cross)
    d_cross_key = weight_grad(encoded, dk_cross)
    d_cross_value = weight_grad(encoded, dv_cross)
    enc_grad = back_project(dk_cross, full_cross_key) + back_project(dv_cross, full_cross_value)
    dx_cross, d_gain_cross = rms_backward(
        x_mid, inverse_cross, gain_cross, back_project(dq_cross, full_cross_query)
    )
    grad_mid = grad_late + dx_cross
    grad_mid_low = grad_mid.astype(jnp.bfloat16)
    d_self_output = weight_grad(attn_self_low, grad_mid_low)
    go_self = back_project(grad_mid_low, full_self_output).astype(jnp.bfloat16)
    dout_self = heads_of(go_self)
    delta_self = jnp.einsum("qhd,qhd->hq", dout_self.astype(jnp.float32), heads_of(attn_self))

    def keys_turn(step, carry):
        held, moving, d_query, d_table = carry
        anchor = jnp.mod(my_index - step, ctx_count)
        key_index = anchor * row_count + row_iota
        allowed, distance = self_allowed(q_index, key_index, lengths)

        def compute(unused):
            onehot = bias_onehot(distance, buckets)
            bias = jnp.einsum("qkb,bh->hqk", onehot, table_full, preferred_element_type=jnp.float32)
            d_q, d_k, d_v, d_s = grad_block(
                query_heads,
                heads_of(held[0]),
                heads_of(held[1]),
                dout_self,
                lse_self,
                delta_self,
                allowed,
                bias,
            )
            d_t = jnp.einsum("hqk,qkb->bh", d_s, onehot, preferred_element_type=jnp.float32)
            return (
                d_q.reshape(row_count, width),
                jnp.stack([d_k.reshape(row_count, width), d_v.reshape(row_count, width)]),
                d_t,
            )

        def keys_skip(unused):
            return (
                jnp.zeros((row_count, width), jnp.float32),
                jnp.zeros((2, row_count, width), jnp.float32),
                jnp.zeros((buckets, HEADS), jnp.float32),
            )

        d_q_add, d_kv_add, d_t_add = lax.cond(jnp.any(allowed), compute, keys_skip, 0)
        held = from_behind(held, "ctx", 1)
        moving = shifted(moving + d_kv_add, "ctx", 1)
        return (held, moving, d_query + d_q_add, d_table + d_t_add)

    looped = lax.fori_loop(
        0,
        ctx_count,
        keys_turn,
        (
            jnp.stack([key_self, value_self]),
            jnp.zeros((2, row_count, width), jnp.float32),
            jnp.zeros((row_count, width), jnp.float32),
            jnp.zeros((buckets, HEADS), jnp.float32),
        ),
    )
    d_query_self = looped[2]
    d_kv_self = looped[1]
    d_table = looped[3]
    dq_self = d_query_self.astype(jnp.bfloat16)
    dk_self = d_kv_self[0].astype(jnp.bfloat16)
    dv_self = d_kv_self[1].astype(jnp.bfloat16)
    d_self_query = weight_grad(in_self, dq_self)
    d_self_key = weight_grad(in_self, dk_self)
    d_self_value = weight_grad(in_self, dv_self)
    d_normed_self = (
        back_project(dq_self, full_self_query)
        + back_project(dk_self, full_self_key)
        + back_project(dv_self, full_self_value)
    )
    dx_self, d_gain_self = rms_backward(x_start, inverse_self, gain_self, d_normed_self)
    grad_tokens = grad_mid + dx_self
    shards = (
        lax.psum_scatter(d_gain_self, "fsdp", scatter_dimension=0, tiled=True),
        lax.psum_scatter(d_gain_cross, "fsdp", scatter_dimension=0, tiled=True),
        lax.psum_scatter(d_gain_ffn, "fsdp", scatter_dimension=0, tiled=True),
        lax.psum_scatter(d_table, "fsdp", scatter_dimension=0, tiled=True),
        lax.psum_scatter(d_self_query, "fsdp", scatter_dimension=0, tiled=True),
        lax.psum_scatter(d_self_key, "fsdp", scatter_dimension=0, tiled=True),
        lax.psum_scatter(d_self_value, "fsdp", scatter_dimension=0, tiled=True),
        lax.psum_scatter(d_self_output, "fsdp", scatter_dimension=0, tiled=True),
        lax.psum_scatter(d_cross_query, "fsdp", scatter_dimension=0, tiled=True),
        lax.psum_scatter(d_cross_key, "fsdp", scatter_dimension=0, tiled=True),
        lax.psum_scatter(d_cross_value, "fsdp", scatter_dimension=0, tiled=True),
        lax.psum_scatter(d_cross_output, "fsdp", scatter_dimension=0, tiled=True),
        lax.psum_scatter(d_inner, "fsdp", scatter_dimension=0, tiled=True),
        lax.psum_scatter(d_outer, "fsdp", scatter_dimension=0, tiled=True),
    )
    totals = lax.psum(
        (
            shards[0],
            shards[1],
            shards[2],
            shards[3],
            shards[4],
            shards[5],
            shards[6],
            shards[7],
            shards[8],
            shards[9],
            shards[10],
            shards[11],
            shards[12],
            shards[13],
        ),
        "ctx",
    )
    return (
        output,
        grad_tokens,
        enc_grad,
        totals[0],
        totals[1],
        totals[2],
        totals[3],
        totals[4],
        totals[5],
        totals[6],
        totals[7],
        totals[8],
        totals[9],
        totals[10],
        totals[11],
        totals[12],
        totals[13],
    )


def solution(mesh):
    in_specs = (
        P(("fsdp", "ctx"), None),
        P(("fsdp", "ctx"), None),
        P(("fsdp", "ctx"), None),
        P("fsdp", None),
        P("fsdp", None),
        P("fsdp", None),
        P("fsdp"),
        P("fsdp"),
        P("fsdp"),
        P("fsdp", None),
        P("fsdp", None),
        P("fsdp", None),
        P("fsdp", None),
        P("fsdp", None),
        P("fsdp", None),
        P("fsdp", None),
        P("fsdp", None),
        P("fsdp", None),
        P("fsdp", None),
        P("fsdp", None),
    )
    out_specs = (
        P(("fsdp", "ctx"), None),
        P(("fsdp", "ctx"), None),
        P(("fsdp", "ctx"), None),
        P("fsdp"),
        P("fsdp"),
        P("fsdp"),
        P("fsdp", None),
        P("fsdp", None),
        P("fsdp", None),
        P("fsdp", None),
        P("fsdp", None),
        P("fsdp", None),
        P("fsdp", None),
        P("fsdp", None),
        P("fsdp", None),
        P("fsdp", None),
        P("fsdp", None),
    )
    return jax.shard_map(
        on_device, mesh=mesh, in_specs=in_specs, out_specs=out_specs, check_vma=False
    )
```

profile of v0, /device:TPU:0, one launch (start us, length us, event | category | flops | bytes accessed | tf_op | source)
XLA Modules:
  0.0 2191.9 jit_solution(9571934918248721555)
XLA Ops:
  38.2 22.4 %all-gather.24.cloned.1.call-done = bf16[768,768]{1,0:T(8,128)(2,1)} async-done(((bf16[384,768]{1,0:T(8,128)(2,1)}), bf16[768,768]{1,0:T(8,128)(2,1)}) %all-gather.24.cloned.1.call-update) | async-done | bytes 1179664 | tf_op jit(solution)/shard_map/all_gather | solution.py:189
  65.4 20.2 all-gather.30.cloned.1.call-done
  87.9 22.4 %all-gather.36.cloned.1.call-done = bf16[768,768]{1,0:T(8,128)(2,1)} async-done(((bf16[384,768]{1,0:T(8,128)(2,1)}), bf16[768,768]{1,0:T(8,128)(2,1)}) %all-gather.36.cloned.1.call-update) | async-done | bytes 1179664 | tf_op jit(solution)/shard_map/all_gather | solution.py:193
  143.1 40.1 %all-gather.20.cloned.1.call-done = bf16[2048,768]{1,0:T(8,128)(2,1)} async-done(((bf16[128,768]{1,0:T(8,128)(2,1)}), bf16[2048,768]{1,0:T(8,128)(2,1)}) %all-gather.20.cloned.1.call-update) | async-done | bytes 3145744 | tf_op jit(solution)/shard_map/all_gather | solution.py:299
  187.8 35.4 %while.104 = (s32[]{:T(128)}, f32[12,128]{1,0:T(8,128)S(1)}, f32[12,128]{1,0:T(8,128)S(1)}, s32[1,6]{1,0:T(1,128)}, s32[4]{0:T(128)}, /*index=5*/bf16[2048,768]{...) while((s32[]{:T(128)}, f32[12,128]{1,0:T(8,128)S(1)}, ...), condition=%wide.region_10.11_spmd.clone, body=%wide.region_2.10_spmd.clone.sunk | while | flops 161364224 | bytes 23165024 | solution.py:141
  235.0 37.9 %while.105 = (s32[]{:T(128)}, f32[12,128,64]{1,2,0:T(8,128)}, s32[1,6]{1,0:T(1,128)}, s32[4]{0:T(128)}, bf16[2048,768]{0,1:T(8,128)(2,1)}, /*index=5*/bf16[128,1...) while((s32[]{:T(128)}, f32[12,128,64]{1,2,0:T(8,128)}, ...), condition=%wide.region_17.18_spmd.clone, body=%wide.region_11.17_spmd.clone.sunk | while | flops 261336320 | bytes 19617844 | solution.py:141
  280.0 46.4 %all-gather.32.cloned.1.call-done = bf16[2048,768]{1,0:T(8,128)(2,1)} async-done(((bf16[128,768]{1,0:T(8,128)(2,1)}), bf16[2048,768]{1,0:T(8,128)(2,1)}) %all-gather.32.cloned.1.call-update) | async-done | bytes 3145744 | tf_op jit(solution)/shard_map/all_gather | solution.py:353
  331.0 42.3 %all-gather.38.cloned.1.call-done = bf16[2048,768]{1,0:T(8,128)(2,1)} async-done(((bf16[128,768]{1,0:T(8,128)(2,1)}), bf16[2048,768]{1,0:T(8,128)(2,1)}) %all-gather.38.cloned.1.call-update) | async-done | bytes 3145744 | tf_op jit(solution)/shard_map/all_gather | solution.py:354
  377.9 36.1 %while.102 = (s32[]{:T(128)}, f32[12,128]{1,0:T(8,128)S(1)}, f32[12,128]{1,0:T(8,128)S(1)}, s32[128]{0:T(128)}, s32[4]{0:T(128)}, /*index=5*/s32[1,6]{1,0:T(1,12...) while((s32[]{:T(128)}, f32[12,128]{1,0:T(8,128)S(1)}, ...), condition=%wide.region_30.31_spmd, body=%wide.region_23.30_spmd.sunk | while | flops 105525248 | bytes 9132817 | solution.py:141
  414.0 37.7 %while.103 = (s32[]{:T(128)}, f32[12,128,64]{1,2,0:T(8,128)S(1)}, s32[128]{0:T(128)}, s32[4]{0:T(128)}, s32[1,6]{1,0:T(1,128)S(1)}, /*index=5*/bf16[2048,768]{0,...) while((s32[]{:T(128)}, f32[12,128,64]{1,2,0:T(8,128)S(1)}, ...), condition=%wide.region_36.37_spmd, body=%wide.region_31.36_spmd.sunk | while | flops 204710912 | bytes 5847809 | solution.py:141
  464.3 60.9 %all-gather.44.cloned.1.call-done = bf16[3072,768]{1,0:T(8,128)(2,1)} async-done(((bf16[1536,768]{1,0:T(8,128)(2,1)}), bf16[3072,768]{1,0:T(8,128)(2,1)}) %all-gather.44.cloned.1.call-update) | async-done | bytes 4718608 | tf_op jit(solution)/shard_map/all_gather | solution.py:196
  534.5 410.1 %while.106 = (s32[]{:T(128)}, bf16[2,128,768]{1,2,0:T(8,128)(2,1)}, f32[2,128,768]{1,2,0:T(8,128)S(1)}, f32[128,768]{0,1:T(8,128)S(1)}, s32[128]{0:T(128)}, /*in...) while((s32[]{:T(128)}, bf16[2,128,768]{1,2,0:T(8,128)(2,1)}, ...), condition=%wide.region_44.45_spmd.clone, body=%wide.region_39.44_spmd.clone.sunk | while | flops 127633680 | bytes 17571048 | solution.py:414
  567.2 18.5 collective-permute-done
  592.8 18.5 collective-permute-done
  618.5 18.5 collective-permute-done
  644.1 18.5 collective-permute-done
  669.7 18.5 collective-permute-done
  695.4 18.5 collective-permute-done
  721.0 18.5 collective-permute-done
  746.6 18.5 collective-permute-done
  772.2 18.5 collective-permute-done
  797.9 18.5 collective-permute-done
  823.5 18.5 collective-permute-done
  959.7 433.0 %while.107 = (s32[]{:T(128)}, bf16[2,128,768]{1,2,0:T(8,128)(2,1)}, f32[2,128,768]{1,2,0:T(8,128)}, f32[128,768]{0,1:T(8,128)}, f32[32,12]{0,1:T(8,128)}, /*inde...) while((s32[]{:T(128)}, bf16[2,128,768]{1,2,0:T(8,128)(2,1)}, ...), condition=%wide.region_52.53_spmd.clone, body=%wide.region_46.52_spmd.clone.sunk | while | flops 154899728 | bytes 25949608 | solution.py:479
  1437.9 37.0 %reduce-scatter.18.cloned.1.call-done = f32[384,768]{1,0:T(8,128)} async-done(((f32[768,768]{1,0:T(8,128)}), f32[384,768]{1,0:T(8,128)}) %reduce-scatter.18.cloned.1.call-update) | async-done | bytes 1179664 | tf_op jit(solution)/shard_map/reduce_scatter | solution.py:513
  1474.9 37.5 %reduce-scatter.16.cloned.1.call-done = f32[384,768]{1,0:T(8,128)} async-done(((f32[768,768]{1,0:T(8,128)}), f32[384,768]{1,0:T(8,128)}) %reduce-scatter.16.cloned.1.call-update) | async-done | bytes 1179664 | tf_op jit(solution)/shard_map/reduce_scatter | solution.py:512
  1512.4 37.0 %reduce-scatter.26.cloned.1.call-done = f32[384,768]{0,1:T(8,128)} async-done(((f32[768,768]{0,1:T(8,128)}), f32[384,768]{0,1:T(8,128)}) %reduce-scatter.26.cloned.1.call-update) | async-done | bytes 1179664 | tf_op jit(solution)/shard_map/reduce_scatter | solution.py:517
  1549.4 37.1 %reduce-scatter.24.cloned.1.call-done = f32[384,768]{0,1:T(8,128)} async-done(((f32[768,768]{0,1:T(8,128)}), f32[384,768]{0,1:T(8,128)}) %reduce-scatter.24.cloned.1.call-update) | async-done | bytes 1179664 | tf_op jit(solution)/shard_map/reduce_scatter | solution.py:516
  1586.5 112.9 %reduce-scatter.32.cloned.1.call-done = f32[1536,768]{1,0:T(8,128)} async-done(((f32[3072,768]{1,0:T(8,128)}), f32[1536,768]{1,0:T(8,128)}) %reduce-scatter.32.cloned.1.call-update) | async-done | bytes 4718608 | tf_op jit(solution)/shard_map/reduce_scatter | solution.py:520
  1699.4 112.7 %reduce-scatter.30.cloned.1.call-done = f32[384,3072]{1,0:T(8,128)} async-done(((f32[768,3072]{1,0:T(8,128)}), f32[384,3072]{1,0:T(8,128)}) %reduce-scatter.30.cloned.1.call-update) | async-done | bytes 4718608 | tf_op jit(solution)/shard_map/reduce_scatter | solution.py:519
  1836.2 63.4 %all-reduce.3 = (f32[384]{0:T(512)}, f32[384]{0:T(512)}, f32[384]{0:T(512)}, f32[16,12]{1,0:T(8,128)}) all-reduce(f32[384]{0:T(512)S(1)} %dynamic-slice.1, f32[384]{0:T(512)S(1)} %dynamic-slice.3, f32[384]{0:T(512)S(1)} %copy-done.76, f32[16,12]{1,0:T(8,128)} %reduce-scatter.12.cloned.1.call-done), channel_id=1, replica_groups=mesh['ctx'=16,'fsdp'=2] {'ctx'}, use_global_device_ids=true, to_apply=%region_56.57 | all-reduce | flops 1344 | bytes 10752 | tf_op jit(solution)/shard_map/psum | solution.py:522
  1899.6 268.0 %all-reduce.8.cloned.1.call-done = (f32[384,768]{1,0:T(8,128)}, f32[384,768]{1,0:T(8,128)}, f32[384,768]{1,0:T(8,128)}, f32[384,768]{1,0:T(8,128)}, f32[384,768]...) async-done(((f32[384,768]{1,0:T(8,128)}, f32[384,768]{1,0:T(8,128)}, ...) | async-done | bytes 18874384 | tf_op jit(solution)/shard_map/psum | solution.py:522
  (1263 shorter events, 1090.5 us)
Async XLA Ops:
  7.2 28.5 %all-gather.18.cloned.1.call-start = ((), (), s32[]{:S(2)}) async-start(), calls=%async_computation.11 | async-start | bytes 1769472 | tf_op jit(solution)/shard_map/all_gather | solution.py:188
  9.5 51.1 %all-gather.24.cloned.1.call-start = ((), (), s32[]{:S(2)}) async-start(), calls=%async_computation.14 | async-start | bytes 1769472 | tf_op jit(solution)/shard_map/all_gather | solution.py:189
  10.5 75.1 %all-gather.30.cloned.1.call-start = ((), (), s32[]{:S(2)}) async-start(), calls=%async_computation.17 | async-start | bytes 1769472 | tf_op jit(solution)/shard_map/all_gather | solution.py:192
  11.9 98.4 %all-gather.36.cloned.1.call-start = ((), (), s32[]{:S(2)}) async-start(), calls=%async_computation.20 | async-start | bytes 1769472 | tf_op jit(solution)/shard_map/all_gather | solution.py:193
  12.9 127.4 %all-gather.22.cloned.1.call-start = ((), (), s32[]{:S(2)}) async-start(), calls=%async_computation.13 | async-start | bytes 1769472 | tf_op jit(solution)/shard_map/all_gather | solution.py:187
  14.2 168.9 %all-gather.20.cloned.1.call-start = ((), (), s32[]{:S(2)}) async-start(), calls=%async_computation.12 | async-start | bytes 3342336 | tf_op jit(solution)/shard_map/all_gather | solution.py:299
  38.1 191.4 %all-gather.26.cloned.1.call-start = ((), (), s32[]{:S(2)}) async-start(), calls=%async_computation.15 | async-start | bytes 3342336 | tf_op jit(solution)/shard_map/all_gather | solution.py:300
  63.0 211.0 %all-gather.28.cloned.1.call-start = ((), (), s32[]{:S(2)}) async-start(), calls=%async_computation.16 | async-start | bytes 1769472 | tf_op jit(solution)/shard_map/all_gather | solution.py:190
  63.9 214.3 %all-gather.34.cloned.1.call-start = ((), (), s32[]{:S(2)}) async-start(), calls=%async_computation.19 | async-start | bytes 1769472 | tf_op jit(solution)/shard_map/all_gather | solution.py:191
  65.3 261.0 %all-gather.32.cloned.1.call-start = ((), (), s32[]{:S(2)}) async-start(), calls=%async_computation.18 | async-start | bytes 3342336 | tf_op jit(solution)/shard_map/all_gather | solution.py:353
  87.8 285.4 %all-gather.38.cloned.1.call-start = ((), (), s32[]{:S(2)}) async-start(), calls=%async_computation.21 | async-start | bytes 3342336 | tf_op jit(solution)/shard_map/all_gather | solution.py:354
  112.6 339.2 %all-gather.40.cloned.1.call-start = ((), (), s32[]{:S(2)}) async-start(), calls=%async_computation.22 | async-start | bytes 1769472 | tf_op jit(solution)/shard_map/all_gather | solution.py:194
  113.6 347.5 %all-gather.42.cloned.1.call-start = ((), (), s32[]{:S(2)}) async-start(), calls=%async_computation.23 | async-start | bytes 7077888 | tf_op jit(solution)/shard_map/all_gather | solution.py:195
  117.7 407.4 %all-gather.44.cloned.1.call-start = ((), (), s32[]{:S(2)}) async-start(), calls=%async_computation.24 | async-start | bytes 7077888 | tf_op jit(solution)/shard_map/all_gather | solution.py:196
  122.2 1299.0 %reduce-scatter.22.cloned.1.call-start = ((), (), s32[]{:S(2)}) async-start(), calls=%async_computation.30 | async-start | bytes 3538944 | tf_op jit(solution)/shard_map/reduce_scatter | solution.py:515
  947.9 473.4 %reduce-scatter.20.cloned.1.call-start = ((), (), s32[]{:S(2)}) async-start(), calls=%async_computation.29 | async-start | bytes 3538944 | tf_op jit(solution)/shard_map/reduce_scatter | solution.py:514
  952.5 468.8 %reduce-scatter.28.cloned.1.call-start = ((), (), s32[]{:S(2)}) async-start(), calls=%async_computation.33 | async-start | bytes 3538944 | tf_op jit(solution)/shard_map/reduce_scatter | solution.py:518
  958.7 479.2 %reduce-scatter.14.cloned.1.call-start = ((), (), s32[]{:S(2)}) async-start(), calls=%async_computation.26 | async-start | bytes 3538944 | tf_op jit(solution)/shard_map/reduce_scatter | solution.py:511
  1140.0 22.6 %collective-permute-start.3 = (f32[2,128,768]{1,2,0:T(8,128)S(1)}, f32[2,128,768]{1,2,0:T(8,128)S(1)}, u32[]{:S(2)}, u32[]{:S(2)}) collective-permute-start(f32[2,128,768]{1,2,0:T(8,128)S(1)} %add.900), channel_id=1, source_target_pairs={{0,2},{2,4},{4,6},{6,8},{8,10},{10,12},{12,14},{14,16},{16,18},{18... | collective-permute-start | bytes 2359304 | tf_op jit(solution)/shard_map/while/body/eval_jaxpr/ppermute | solution.py:20
  1168.7 22.6 %collective-permute-start.3 = (f32[2,128,768]{1,2,0:T(8,128)S(1)}, f32[2,128,768]{1,2,0:T(8,128)S(1)}, u32[]{:S(2)}, u32[]{:S(2)}) collective-permute-start(f32[2,128,768]{1,2,0:T(8,128)S(1)} %add.900), channel_id=1, source_target_pairs={{0,2},{2,4},{4,6},{6,8},{8,10},{10,12},{12,14},{14,16},{16,18},{18... | collective-permute-start | bytes 2359304 | tf_op jit(solution)/shard_map/while/body/eval_jaxpr/ppermute | solution.py:20
  1226.0 22.6 %collective-permute-start.3 = (f32[2,128,768]{1,2,0:T(8,128)S(1)}, f32[2,128,768]{1,2,0:T(8,128)S(1)}, u32[]{:S(2)}, u32[]{:S(2)}) collective-permute-start(f32[2,128,768]{1,2,0:T(8,128)S(1)} %add.900), channel_id=1, source_target_pairs={{0,2},{2,4},{4,6},{6,8},{8,10},{10,12},{12,14},{14,16},{16,18},{18... | collective-permute-start | bytes 2359304 | tf_op jit(solution)/shard_map/while/body/eval_jaxpr/ppermute | solution.py:20
  1254.6 22.6 %collective-permute-start.3 = (f32[2,128,768]{1,2,0:T(8,128)S(1)}, f32[2,128,768]{1,2,0:T(8,128)S(1)}, u32[]{:S(2)}, u32[]{:S(2)}) collective-permute-start(f32[2,128,768]{1,2,0:T(8,128)S(1)} %add.900), channel_id=1, source_target_pairs={{0,2},{2,4},{4,6},{6,8},{8,10},{10,12},{12,14},{14,16},{16,18},{18... | collective-permute-start | bytes 2359304 | tf_op jit(solution)/shard_map/while/body/eval_jaxpr/ppermute | solution.py:20
  1311.9 22.6 %collective-permute-start.3 = (f32[2,128,768]{1,2,0:T(8,128)S(1)}, f32[2,128,768]{1,2,0:T(8,128)S(1)}, u32[]{:S(2)}, u32[]{:S(2)}) collective-permute-start(f32[2,128,768]{1,2,0:T(8,128)S(1)} %add.900), channel_id=1, source_target_pairs={{0,2},{2,4},{4,6},{6,8},{8,10},{10,12},{12,14},{14,16},{16,18},{18... | collective-permute-start | bytes 2359304 | tf_op jit(solution)/shard_map/while/body/eval_jaxpr/ppermute | solution.py:20
  1340.5 22.6 %collective-permute-start.3 = (f32[2,128,768]{1,2,0:T(8,128)S(1)}, f32[2,128,768]{1,2,0:T(8,128)S(1)}, u32[]{:S(2)}, u32[]{:S(2)}) collective-permute-start(f32[2,128,768]{1,2,0:T(8,128)S(1)} %add.900), channel_id=1, source_target_pairs={{0,2},{2,4},{4,6},{6,8},{8,10},{10,12},{12,14},{14,16},{16,18},{18... | collective-permute-start | bytes 2359304 | tf_op jit(solution)/shard_map/while/body/eval_jaxpr/ppermute | solution.py:20
  1395.7 79.2 %reduce-scatter.18.cloned.1.call-start = ((), (), s32[]{:S(2)}) async-start(), calls=%async_computation.28 | async-start | bytes 3538944 | tf_op jit(solution)/shard_map/reduce_scatter | solution.py:513
  1398.9 113.5 %reduce-scatter.16.cloned.1.call-start = ((), (), s32[]{:S(2)}) async-start(), calls=%async_computation.27 | async-start | bytes 3538944 | tf_op jit(solution)/shard_map/reduce_scatter | solution.py:512
  1400.9 148.5 %reduce-scatter.26.cloned.1.call-start = ((), (), s32[]{:S(2)}) async-start(), calls=%async_computation.32 | async-start | bytes 3538944 | tf_op jit(solution)/shard_map/reduce_scatter | solution.py:517
  1404.0 182.5 %reduce-scatter.24.cloned.1.call-start = ((), (), s32[]{:S(2)}) async-start(), calls=%async_computation.31 | async-start | bytes 3538944 | tf_op jit(solution)/shard_map/reduce_scatter | solution.py:516
  1405.9 293.5 %reduce-scatter.32.cloned.1.call-start = ((), (), s32[]{:S(2)}) async-start(), calls=%async_computation.35 | async-start | bytes 14155776 | tf_op jit(solution)/shard_map/reduce_scatter | solution.py:520
  1412.6 399.6 %reduce-scatter.30.cloned.1.call-start = ((), (), s32[]{:S(2)}) async-start(), calls=%async_computation.34 | async-start | bytes 14155776 | tf_op jit(solution)/shard_map/reduce_scatter | solution.py:519
  1419.8 416.4 %reduce-scatter.12.cloned.1.call-start = ((), (), s32[]{:S(2)}) async-start(), calls=%async_computation.25 | async-start | bytes 24576 | tf_op jit(solution)/shard_map/reduce_scatter | solution.py:510
  1421.2 746.5 %all-reduce.8.cloned.1.call-start = ((), (), s32[]{:S(2)}) async-start(), calls=%async_computation.36 | async-start | bytes 37748736 | tf_op jit(solution)/shard_map/psum | solution.py:522
  (240 other events, 3216.0 us)
Sparse Core Ops, SparseCore 0:
  10.2 25.4 all-gather.17
  37.8 22.7 all-gather.23
  62.7 22.7 all-gather.29
  87.5 22.7 all-gather.35
  112.3 22.8 all-gather.21
  137.9 45.1 all-gather.19
  185.4 44.0 all-gather.25
  231.6 21.5 all-gather.27
  255.3 22.7 all-gather.33
  280.9 45.4 all-gather.31
  329.2 43.9 all-gather.37
  375.2 21.5 all-gather.39
  398.4 62.6 all-gather.41
  462.5 62.6 all-gather.43
  948.0 30.5 reduce-scatter.21
  980.8 34.6 reduce-scatter.19
  1017.6 34.7 reduce-scatter.27
  1395.8 42.0 reduce-scatter.13
  1440.2 34.7 reduce-scatter.17
  1477.7 34.6 reduce-scatter.15
  1514.7 34.7 reduce-scatter.25
  1551.7 34.6 reduce-scatter.23
  1588.8 110.5 reduce-scatter.31
  1701.6 110.5 reduce-scatter.29
  1814.9 9.7 reduce-scatter.11
  1830.9 336.7 all-reduce.7
where the time goes:
time: 2210 us; the launch traced here: 2190 us
  waiting for transfers between devices  1490 us (67%)
  other arithmetic  197 us (9%)
  local copies, waits for them, and re-layouts  170 us (8%)
  matrix products  133 us (6%)
  blocking collectives  89.5 us (4%)
  loops' own time  54.3 us (2%)
  starting transfers between devices  47.6 us (2%)
    ppermute x48, waiting for transfers between devices, shifted(): lax.ppermute(value, axis, [(i, (i + by) % size) for i in range(size)])  541 us
    psum x1, waiting for transfers between devices, on_device(): lax.psum((shards[0], shards[1], shards[2], shards[3], shards[4], shards[5...  268 us
    reduce_scatter x1, waiting for transfers between devices, on_device(): lax.psum_scatter(d_outer, 'fsdp', scatter_dimension=0, tiled=True)  113 us
    reduce_scatter x1, waiting for transfers between devices, on_device(): lax.psum_scatter(d_inner, 'fsdp', scatter_dimension=0, tiled=True)  113 us
    psum x1, blocking collectives, on_device(): lax.psum((shards[0], shards[1], shards[2], shards[3], shards[4], shards[5...  63.4 us
    all_gather x1, waiting for transfers between devices, on_device(): lax.all_gather(ffn_outer.astype(jnp.bfloat16), 'fsdp', axis=0, tiled=True)  60.9 us
    while x192, local copies, waits for them, and re-layouts  52.5 us
    all_gather x1, waiting for transfers between devices, on_device(): lax.all_gather(key_cross, 'ctx', axis=0, tiled=True)  46.4 us
  transfers between devices with their start and end apart: 90, of which 51 were waited for; matrix products, arithmetic and copies ran while one was open for 16% of the time, Pallas kernels for 0%

commit v1 on v0

v1 whole, which is shorter than its diff:
```python
import functools
import math

import jax
import jax.numpy as jnp
import numpy as np
from jax import lax
from jax.experimental import pallas as pl
from jax.experimental.pallas import tpu as pltpu
from jax.sharding import Mesh
from jax.sharding import PartitionSpec as P

HEADS = 12
HEAD_DIM = 64
BUCKETS = 32
EPS = 1e-06
NEG = -1e30
GELU_C = 0.7978845608028654
GELU_A = 0.044715

LOCAL = HEADS // 2
PAIRS = LOCAL // 2
HALF = LOCAL * HEAD_DIM
ROWS = 256
VMEM_LIMIT = 56 << 20

F32 = jnp.float32
BF16 = jnp.bfloat16


def bucket_edges():
    edges = []
    for level in range(1, 16):
        distance = 16
        while int(math.log(distance / 16.0) / math.log(8.0) * 16.0) < level:
            distance += 1
        edges.append(distance)
    return edges


def buckets_of(distances):
    clipped = np.maximum(np.asarray(distances), 0)
    large = np.full(clipped.shape, 16)
    for edge in bucket_edges():
        large = large + (clipped >= edge)
    return np.where(clipped < 16, clipped, large)


LANES = np.arange(2 * ROWS)
QK_DISTANCE = np.where(LANES <= ROWS, ROWS - LANES, 3 * ROWS - LANES)
KQ_DISTANCE = LANES
QK_ONEHOT = np.eye(BUCKETS, dtype=np.float32)[buckets_of(QK_DISTANCE)]
KQ_ONEHOT = np.eye(BUCKETS, dtype=np.float32)[buckets_of(KQ_DISTANCE)]


def dot_nt(left, right):
    return lax.dot_general(left, right, (((1,), (1,)), ((), ())), preferred_element_type=F32)


def dot_tn(left, right):
    return lax.dot_general(left, right, (((0,), (0,)), ((), ())), preferred_element_type=F32)


def dot_nn(left, right):
    return lax.dot_general(left, right, (((1,), (0,)), ((), ())), preferred_element_type=F32)


def spans(ref):
    starts, ends, at = [], [], jnp.int32(0)
    for i in range(ref.shape[1]):
        starts.append(at)
        at = at + ref[0, i]
        ends.append(at)
    return starts, ends


def seg_of(index, ends):
    found = jnp.zeros(index.shape, jnp.int32)
    for end in ends[:-1]:
        found = found + (index >= end).astype(jnp.int32)
    return found


def iota(shape, axis):
    return lax.broadcasted_iota(jnp.int32, shape, axis)


def split_pair(pair):
    low = iota(pair.shape, 1) < HEAD_DIM
    zero = jnp.zeros_like(pair)
    return jnp.concatenate([jnp.where(low, pair, zero), jnp.where(low, zero, pair)], axis=0)


def join_pair(both):
    rows = both.shape[0] // 2
    low = iota((rows, both.shape[1]), 1) < HEAD_DIM
    return jnp.where(low, both[:rows], both[rows:])


def fill_tiles(bias_ref, tiles, first, second):
    for h in range(LOCAL):
        rolled = pltpu.roll(
            jnp.broadcast_to(bias_ref[h : h + 1, :], (ROWS, 2 * ROWS)), 0, 1, stride=1, stride_axis=0
        )
        tiles[first, h] = rolled[:, :ROWS]
        tiles[second, h] = rolled[:, ROWS:]
        tiles[0, h] = jnp.broadcast_to(bias_ref[h : h + 1, 2 * ROWS - 1 :], (ROWS, ROWS))


def softmax_and_values(s_scr, mx_scr, l_scr, acc_scr, values, visit, o_ref, lse_ref):
    lse = jnp.zeros((ROWS, 128), F32)
    lane = iota((ROWS, 128), 1)
    for p in range(PAIRS):
        peak = jnp.max(mx_scr[p], axis=1, keepdims=True)
        l_scr[...] = jnp.zeros_like(l_scr)
        acc_scr[...] = jnp.zeros_like(acc_scr)

        def block(j, p=p, peak=peak):
            at = pl.multiple_of(j * ROWS, ROWS)
            weights = jnp.exp(s_scr[p, :, pl.ds(at, ROWS)] - peak)
            l_scr[...] += weights
            acc_scr[...] += dot_nn(weights.astype(BF16), values(at, p))

        visit(block)
        total = jnp.sum(l_scr[...], axis=1, keepdims=True)
        o_ref[:, 128 * p : 128 * p + 128] = join_pair(acc_scr[...] / total)
        both = peak + jnp.log(total)
        lse = jnp.where(lane == 2 * p, both[:ROWS], lse)
        lse = jnp.where(lane == 2 * p + 1, both[ROWS:], lse)
    lse_ref[...] = lse


def self_forward_kernel(chip_ref, len_ref, bias_ref, qkv_ref, o_ref, lse_ref, tiles, qs, s_scr, mx_scr, l_scr, acc_scr):
    chip = chip_ref[0]
    starts, ends = spans(len_ref)
    base = pl.multiple_of(chip * ROWS, ROWS)
    first = jnp.int32(0)
    for end in ends[:-1]:
        first = jnp.where(base >= end, end, first)
    j_min = first // ROWS
    fill_tiles(bias_ref, tiles, 1, 2)
    for p in range(PAIRS):
        qs[p] = split_pair(qkv_ref[pl.ds(base, ROWS), 128 * p : 128 * p + 128])
    mx_scr[...] = jnp.full_like(mx_scr, NEG)
    q_row = base + iota((ROWS, 1), 0)
    q_seg = seg_of(q_row, ends)

    def scores(j, _):
        at = pl.multiple_of(j * ROWS, ROWS)
        k_row = at + iota((1, ROWS), 1)
        allowed = (q_seg == seg_of(k_row, ends)) & (k_row <= q_row)
        masked = jnp.where(allowed, 0.0, NEG)
        tile = jnp.maximum(j - chip + 2, 0)
        for p in range(PAIRS):
            keys = qkv_ref[pl.ds(at, ROWS), HALF + 128 * p : HALF + 128 * p + 128]
            raw = dot_nt(qs[p], keys)
            for i in range(2):
                rows = slice(i * ROWS, (i + 1) * ROWS)
                value = raw[rows] + (tiles[tile, 2 * p + i] + masked)
                s_scr[p, rows, pl.ds(at, ROWS)] = value
                mx_scr[p, rows] = jnp.maximum(mx_scr[p, rows], value)
        return 0

    lax.fori_loop(j_min, chip + 1, scores, 0)

    def visit(block):
        lax.fori_loop(j_min, chip + 1, lambda j, c: (block(j), c)[1], 0)

    softmax_and_values(
        s_scr, mx_scr, l_scr, acc_scr,
        lambda at, p: qkv_ref[pl.ds(at, ROWS), 2 * HALF + 128 * p : 2 * HALF + 128 * p + 128],
        visit, o_ref, lse_ref,
    )


def cross_flags(chip, len_ref, enc_ref, deal_ref):
    starts, ends = spans(len_ref)
    e_starts, e_ends = spans(enc_ref)
    base = chip * ROWS
    ranges = []
    for i in range(len(ends)):
        live = (starts[i] < base + ROWS) & (ends[i] > base)
        low, high = jnp.int32(0), jnp.int32(0)
        for e in range(len(e_ends)):
            hit = deal_ref[0, i] == e
            low = jnp.where(hit, e_starts[e], low)
            high = jnp.where(hit, e_ends[e], high)
        ranges.append((live, low, high))

    def wanted(at):
        found = jnp.bool_(False)
        for live, low, high in ranges:
            found = found | (live & (low < at + ROWS) & (high > at))
        return found

    q_seg = seg_of(base + iota((ROWS, 1), 0), ends)
    q_pair = jnp.zeros((ROWS, 1), jnp.int32)
    for i in range(len(ends)):
        q_pair = q_pair + jnp.where(q_seg == i, deal_ref[0, i], 0)
    return wanted, q_pair, e_ends


def cross_forward_kernel(chip_ref, len_ref, enc_ref, deal_ref, q_ref, kv_ref, o_ref, lse_ref, qs, s_scr, mx_scr, l_scr, acc_scr):
    chip = chip_ref[0]
    wanted, q_pair, e_ends = cross_flags(chip, len_ref, enc_ref, deal_ref)
    for p in range(PAIRS):
        qs[p] = split_pair(q_ref[:, 128 * p : 128 * p + 128])
    mx_scr[...] = jnp.full_like(mx_scr, NEG)
    blocks = kv_ref.shape[0] // ROWS

    def visit(block):
        def body(j, c):
            @pl.when(wanted(j * ROWS))
            def _():
                block(j)

            return c

        lax.fori_loop(0, blocks, body, 0)

    def scores(j):
        at = pl.multiple_of(j * ROWS, ROWS)
        k_row = at + iota((1, ROWS), 1)
        masked = jnp.where(q_pair == seg_of(k_row, e_ends), 0.0, NEG)
        for p in range(PAIRS):
            raw = dot_nt(qs[p], kv_ref[pl.ds(at, ROWS), 128 * p : 128 * p + 128])
            for i in range(2):
                rows = slice(i * ROWS, (i + 1) * ROWS)
                value = raw[rows] + masked
                s_scr[p, rows, pl.ds(at, ROWS)] = value
                mx_scr[p, rows] = jnp.maximum(mx_scr[p, rows], value)

    visit(scores)
    softmax_and_values(
        s_scr, mx_scr, l_scr, acc_scr,
        lambda at, p: kv_ref[pl.ds(at, ROWS), HALF + 128 * p : HALF + 128 * p + 128],
        visit, o_ref, lse_ref,
    )


def row_stats(go_ref, o_ref, lse_ref, gs, lse_scr, delta_scr):
    lane = iota((ROWS, 128), 1)
    low = lane < HEAD_DIM
    deltas = jnp.zeros((ROWS, 128), F32)
    for p in range(PAIRS):
        columns = slice(128 * p, 128 * p + 128)
        grads = go_ref[:, columns]
        gs[p] = split_pair(grads)
        product = grads.astype(F32) * o_ref[:, columns]
        for i in range(2):
            part = jnp.where(low if i == 0 else ~low, product, 0.0)
            delta = jnp.sum(part, axis=1, keepdims=True)
            rows = slice(i * ROWS, (i + 1) * ROWS)
            delta_scr[p, rows] = jnp.broadcast_to(delta, (ROWS, 128))
            lse_scr[p, rows] = jnp.broadcast_to(
                jnp.sum(jnp.where(lane == 2 * p + i, lse_ref[...], 0.0), axis=1, keepdims=True), (ROWS, 128)
            )
            deltas = jnp.where(lane == 8 + 2 * p + i, delta, deltas)
    return deltas


def self_query_grad_kernel(
    chip_ref, len_ref, bias_ref, qkv_ref, go_ref, o_ref, lse_ref, dq_ref, stat_ref, dist_ref,
    tiles, qs, gs, lse_scr, delta_scr, dq_scr, ds_scr,
):
    chip = chip_ref[0]
    starts, ends = spans(len_ref)
    base = pl.multiple_of(chip * ROWS, ROWS)
    first = jnp.int32(0)
    for end in ends[:-1]:
        first = jnp.where(base >= end, end, first)
    fill_tiles(bias_ref, tiles, 1, 2)
    deltas = row_stats(go_ref, o_ref, lse_ref, gs, lse_scr, delta_scr)
    stats = jnp.where(iota((ROWS, 128), 1) < 8, lse_ref[...], deltas)
    stat_ref[...] = jnp.transpose(stats)[:16]
    for p in range(PAIRS):
        qs[p] = split_pair(qkv_ref[pl.ds(base, ROWS), 128 * p : 128 * p + 128])
    dq_scr[...] = jnp.zeros_like(dq_scr)
    ds_scr[...] = jnp.zeros_like(ds_scr)
    q_row = base + iota((ROWS, 1), 0)
    q_seg = seg_of(q_row, ends)

    def block(j, _):
        at = pl.multiple_of(j * ROWS, ROWS)
        k_row = at + iota((1, ROWS), 1)
        allowed = (q_seg == seg_of(k_row, ends)) & (k_row <= q_row)
        masked = jnp.where(allowed, 0.0, NEG)
        tile = jnp.maximum(j - chip + 2, 0)
        for p in range(PAIRS):
            keys = qkv_ref[pl.ds(at, ROWS), HALF + 128 * p : HALF + 128 * p + 128]
            values = qkv_ref[pl.ds(at, ROWS), 2 * HALF + 128 * p : 2 * HALF + 128 * p + 128]
            raw = dot_nt(qs[p], keys)
            dprobs = dot_nt(gs[p], values)
            grads = []
            for i in range(2):
                rows = slice(i * ROWS, (i + 1) * ROWS)
                value = raw[rows] + (tiles[tile, 2 * p + i] + masked)
                probs = jnp.exp(value - lse_scr[p, rows, :1])
                ds = (probs * (dprobs[rows] - delta_scr[p, rows, :1])).astype(BF16)
                ds_scr[tile, 2 * p + i] += ds.astype(F32)
                grads.append(ds)
            dq_scr[p] += dot_nn(jnp.concatenate(grads, axis=0), keys)
        return 0

    lax.fori_loop(first // ROWS, chip + 1, block, 0)
    dist_ref[...] = jnp.zeros_like(dist_ref)
    lanes = iota((1, 2 * ROWS), 1)
    for p in range(PAIRS):
        dq_ref[:, 128 * p : 128 * p + 128] = join_pair(dq_scr[p]).astype(BF16)
    for h in range(LOCAL):
        folded = jnp.concatenate([ds_scr[1, h], ds_scr[2, h]], axis=1)
        rows = ROWS
        while rows > 1:
            rows //= 2
            folded = folded[:rows] + pltpu.roll(folded[rows:], 2 * ROWS - rows, 1)
        far = jnp.sum(jnp.sum(ds_scr[0, h], axis=0, keepdims=True), axis=1, keepdims=True)
        dist_ref[h : h + 1, :] = folded + jnp.where(lanes == 2 * ROWS - 1, far, 0.0)


def self_key_grad_kernel(chip_ref, len_ref, bias_ref, qkv_ref, go_ref, stat_ref, dkv_ref, tiles, ks, vs, dk_scr, dv_scr):
    chip = chip_ref[0]
    starts, ends = spans(len_ref)
    base = pl.multiple_of(chip * ROWS, ROWS)
    last = ends[-1]
    for end in reversed(ends[:-1]):
        last = jnp.where(base + ROWS - 1 < end, end, last)
    fill_tiles(bias_ref, tiles, 2, 1)
    for p in range(PAIRS):
        ks[p] = split_pair(qkv_ref[pl.ds(base, ROWS), HALF + 128 * p : HALF + 128 * p + 128])
        vs[p] = split_pair(qkv_ref[pl.ds(base, ROWS), 2 * HALF + 128 * p : 2 * HALF + 128 * p + 128])
    dk_scr[...] = jnp.zeros_like(dk_scr)
    dv_scr[...] = jnp.zeros_like(dv_scr)
    k_row = base + iota((ROWS, 1), 0)
    k_seg = seg_of(k_row, ends)

    def block(i, _):
        at = pl.multiple_of(i * ROWS, ROWS)
        q_row = at + iota((1, ROWS), 1)
        allowed = (k_seg == seg_of(q_row, ends)) & (k_row <= q_row)
        masked = jnp.where(allowed, 0.0, NEG)
        tile = jnp.maximum(2 - (i - chip), 0)
        for p in range(PAIRS):
            queries = qkv_ref[pl.ds(at, ROWS), 128 * p : 128 * p + 128]
            grads = go_ref[pl.ds(at, ROWS), 128 * p : 128 * p + 128]
            raw = dot_nt(ks[p], queries)
            dprobs = dot_nt(vs[p], grads)
            weights, dscores = [], []
            for e in range(2):
                rows = slice(e * ROWS, (e + 1) * ROWS)
                h = 2 * p + e
                value = raw[rows] + (tiles[tile, h] + masked)
                probs = jnp.exp(value - stat_ref[i, h : h + 1, :])
                weights.append(probs.astype(BF16))
                dscores.append((probs * (dprobs[rows] - stat_ref[i, 8 + h : 9 + h, :])).astype(BF16))
            dv_scr[p] += dot_nn(jnp.concatenate(weights, axis=0), grads)
            dk_scr[p] += dot_nn(jnp.concatenate(dscores, axis=0), queries)
        return 0

    lax.fori_loop(chip, (last - 1) // ROWS + 1, block, 0)
    for p in range(PAIRS):
        dkv_ref[:, 128 * p : 128 * p + 128] = join_pair(dk_scr[p]).astype(BF16)
        dkv_ref[:, HALF + 128 * p : HALF + 128 * p + 128] = join_pair(dv_scr[p]).astype(BF16)


def cross_grad_kernel(
    chip_ref, len_ref, enc_ref, deal_ref, q_ref, go_ref, o_ref, lse_ref, kv_ref, dq_ref, dkv_ref,
    qs, gs, lse_scr, delta_scr, dq_scr,
):
    chip = chip_ref[0]
    wanted, q_pair, e_ends = cross_flags(chip, len_ref, enc_ref, deal_ref)
    row_stats(go_ref, o_ref, lse_ref, gs, lse_scr, delta_scr)
    for p in range(PAIRS):
        qs[p] = split_pair(q_ref[:, 128 * p : 128 * p + 128])
    dq_scr[...] = jnp.zeros_like(dq_scr)

    def block(j, c):
        at = pl.multiple_of(j * ROWS, ROWS)
        hit = wanted(at)

        @pl.when(hit)
        def _():
            k_row = at + iota((1, ROWS), 1)
            masked = jnp.where(q_pair == seg_of(k_row, e_ends), 0.0, NEG)
            for p in range(PAIRS):
                columns = slice(128 * p, 128 * p + 128)
                v_columns = slice(HALF + 128 * p, HALF + 128 * p + 128)
                keys = kv_ref[pl.ds(at, ROWS), columns]
                raw = dot_nt(qs[p], keys)
                dprobs = dot_nt(gs[p], kv_ref[pl.ds(at, ROWS), v_columns])
                weights, dscores = [], []
                for i in range(2):
                    rows = slice(i * ROWS, (i + 1) * ROWS)
                    probs = jnp.exp(raw[rows] + masked - lse_scr[p, rows, :1])
                    weights.append(probs.astype(BF16))
                    dscores.append((probs * (dprobs[rows] - delta_scr[p, rows, :1])).astype(BF16))
                ds = jnp.concatenate(dscores, axis=0)
                dq_scr[p] += dot_nn(ds, keys)
                dkv_ref[pl.ds(at, ROWS), columns] = dot_tn(ds, qs[p]).astype(BF16)
                dkv_ref[pl.ds(at, ROWS), v_columns] = dot_tn(jnp.concatenate(weights, axis=0), gs[p]).astype(BF16)

        @pl.when(jnp.logical_not(hit))
        def _():
            dkv_ref[pl.ds(at, ROWS), :] = jnp.zeros((ROWS, 2 * HALF), BF16)

        return c

    lax.fori_loop(0, kv_ref.shape[0] // ROWS, block, 0)
    for p in range(PAIRS):
        dq_ref[:, 128 * p : 128 * p + 128] = join_pair(dq_scr[p]).astype(BF16)


SMEM = pl.BlockSpec(memory_space=pltpu.SMEM)
VMEM = pl.BlockSpec(memory_space=pltpu.VMEM)


def call(kernel, scalars, arrays, outs, scratch, flops):
    moved = sum(a.size * a.dtype.itemsize for a in arrays) + sum(math.prod(s) * jnp.dtype(d).itemsize for s, d in outs)
    return pl.pallas_call(
        kernel,
        out_shape=[jax.ShapeDtypeStruct(s, d) for s, d in outs],
        in_specs=[SMEM] * len(scalars) + [VMEM] * len(arrays),
        out_specs=[VMEM] * len(outs),
        scratch_shapes=[pltpu.VMEM(s, d) for s, d in scratch],
        compiler_params=pltpu.CompilerParams(vmem_limit_bytes=VMEM_LIMIT),
        cost_estimate=pl.CostEstimate(flops=flops, transcendentals=flops // 256, bytes_accessed=moved),
    )(*scalars, *arrays)


TILES = ((3, LOCAL, ROWS, ROWS), F32)
STACK = ((PAIRS, 2 * ROWS, 128), BF16)
COLUMN = ((PAIRS, 2 * ROWS, 128), F32)


def self_forward(chip, lengths, bias, qkv):
    n = qkv.shape[0]
    return call(
        self_forward_kernel, (chip, lengths), (bias, qkv),
        [((ROWS, HALF), F32), ((ROWS, 128), F32)],
        [TILES, STACK, ((PAIRS, 2 * ROWS, n), F32), ((PAIRS, 2 * ROWS, ROWS), F32), ((2 * ROWS, ROWS), F32), ((2 * ROWS, 128), F32)],
        8 * ROWS * n * HALF,
    )


def cross_forward(chip, lengths, enc, deal, query, kv):
    n = kv.shape[0]
    return call(
        cross_forward_kernel, (chip, lengths, enc, deal), (query, kv),
        [((ROWS, HALF), F32), ((ROWS, 128), F32)],
        [STACK, ((PAIRS, 2 * ROWS, n), F32), ((PAIRS, 2 * ROWS, ROWS), F32), ((2 * ROWS, ROWS), F32), ((2 * ROWS, 128), F32)],
        8 * ROWS * n * HALF,
    )


def self_query_grad(chip, lengths, bias, qkv, go, attn, lse):
    n = qkv.shape[0]
    return call(
        self_query_grad_kernel, (chip, lengths), (bias, qkv, go, attn, lse),
        [((ROWS, HALF), BF16), ((16, ROWS), F32), ((8, 2 * ROWS), F32)],
        [TILES, STACK, STACK, COLUMN, COLUMN, COLUMN, TILES],
        12 * ROWS * n * HALF,
    )


def self_key_grad(chip, lengths, bias, qkv, go, stats):
    n = qkv.shape[0]
    return call(
        self_key_grad_kernel, (chip, lengths), (bias, qkv, go, stats),
        [((ROWS, 2 * HALF), BF16)],
        [TILES, STACK, STACK, COLUMN, COLUMN],
        16 * ROWS * n * HALF,
    )[0]


def cross_grad(chip, lengths, enc, deal, query, go, attn, lse, kv):
    n = kv.shape[0]
    return call(
        cross_grad_kernel, (chip, lengths, enc, deal), (query, go, attn, lse, kv),
        [((ROWS, HALF), BF16), ((n, 2 * HALF), BF16)],
        [STACK, STACK, COLUMN, COLUMN, COLUMN],
        20 * ROWS * n * HALF,
    )


def swap_core(value):
    return lax.ppermute(value, "core", [(0, 1), (1, 0)])


def by_core(own, other, axis):
    core = lax.axis_index("core")
    return jnp.where(
        core == 0, jnp.concatenate([own, other], axis=axis), jnp.concatenate([other, own], axis=axis)
    )


def both_cores(own, axis):
    return by_core(own, swap_core(own), axis)


def gather_fsdp(own):
    count = lax.axis_size("fsdp")
    if count != 2:
        return lax.all_gather(own, "fsdp", axis=0, tiled=True)
    other = lax.ppermute(own, "fsdp", [(0, 1), (1, 0)])
    return jnp.where(
        lax.axis_index("fsdp") == 0,
        jnp.concatenate([own, other], axis=0),
        jnp.concatenate([other, own], axis=0),
    )


def scatter_fsdp(terms):
    count = lax.axis_size("fsdp")
    if count != 2:
        return lax.psum_scatter(terms, "fsdp", scatter_dimension=0, tiled=True)
    index = lax.axis_index("fsdp")
    rows = terms.shape[0] // 2
    other = lax.dynamic_slice_in_dim(terms, (1 - index) * rows, rows, 0).astype(BF16)
    own = lax.dynamic_slice_in_dim(terms, index * rows, rows, 0)
    return own + lax.ppermute(other, "fsdp", [(0, 1), (1, 0)]).astype(F32)


def spread(value, axes):
    count = lax.axis_size(axes)
    return lax.all_to_all(jnp.broadcast_to(value[None], (count,) + value.shape), axes, 0, 0, tiled=True)


CHIPS = ("z", "y")


def gather_rows(own):
    blocks = spread(own, CHIPS)
    other = swap_core(blocks)
    core = lax.axis_index("core")
    both = jnp.where(
        core == 0, jnp.stack([blocks, other], axis=1), jnp.stack([other, blocks], axis=1)
    )
    return both.reshape(-1, own.shape[1])


def sum_over(value, axis):
    count = lax.axis_size(axis)
    parts = value.reshape((count, value.shape[0] // count) + value.shape[1:])
    return jnp.sum(lax.all_to_all(parts, axis, 0, 0, tiled=True).astype(F32), axis=0)


def reduce_chips(value):
    rows = value.shape[0]
    part = sum_over(value.astype(BF16), "y").astype(BF16)
    part = sum_over(part, "z").astype(BF16)
    part = spread(part, "z").reshape((-1,) + value.shape[1:])
    return spread(part, "y").reshape((rows,) + value.shape[1:])


def inverse_rms(value):
    return lax.rsqrt(jnp.mean(value * value, axis=-1, keepdims=True) + EPS)


def rms_backward(value, inverse, gain, grad):
    scaled = grad * gain
    cubed = inverse * inverse * inverse
    dvalue = inverse * scaled - value * cubed * jnp.mean(scaled * value, axis=-1, keepdims=True)
    return (dvalue, jnp.sum(grad * value * inverse, axis=0))


def gelu_parts(value):
    tangent = jnp.tanh(GELU_C * (value + GELU_A * value * value * value))
    result = 0.5 * value * (1.0 + tangent)
    slope = 0.5 * (1.0 + tangent) + 0.5 * value * (1.0 - tangent * tangent) * GELU_C * (
        1.0 + 3.0 * GELU_A * value * value
    )
    return (result, slope)


def on_device(
    tokens, encoded, cotangent, tgt_lengths, enc_lengths, deal,
    ln_self, ln_cross, ln_ffn, bias_table,
    self_query, self_key, self_value, self_output,
    cross_query, cross_key, cross_value, cross_output,
    ffn_inner, ffn_outer,
):
    core = lax.axis_index("core")
    fsdp = lax.axis_index("fsdp")
    n_fsdp = lax.axis_size("fsdp")
    chip = lax.axis_index(CHIPS)
    chip_ref = chip.reshape(1).astype(jnp.int32)
    rows, width = tokens.shape
    hidden_half = ffn_inner.shape[1] // 2
    unit = hidden_half // n_fsdp

    def mine(value, axis):
        size = value.shape[axis] // 2
        return lax.dynamic_slice_in_dim(value, core * size, size, axis)

    small = jnp.concatenate(
        [ln_self, ln_cross, ln_ffn, bias_table.reshape(-1)], axis=0
    ).astype(BF16)[None]
    small = gather_fsdp(small)
    part = width // n_fsdp
    gain_self = small[:, :part].reshape(-1).astype(F32)
    gain_cross = small[:, part : 2 * part].reshape(-1).astype(F32)
    gain_ffn = small[:, 2 * part : 3 * part].reshape(-1).astype(F32)
    table = small[:, 3 * part :].reshape(BUCKETS, HEADS)
    table = lax.dynamic_slice_in_dim(table, core * LOCAL, LOCAL, 1).astype(F32)
    pad = jnp.zeros((2, 2 * ROWS), F32)
    highest = functools.partial(jnp.einsum, "bh,tb->ht", precision=lax.Precision.HIGHEST)
    bias_qk = jnp.concatenate([highest(table, QK_ONEHOT), pad], axis=0)
    bias_kq = jnp.concatenate([highest(table, KQ_ONEHOT), pad], axis=0)

    def gather_columns(*weights):
        return gather_fsdp(jnp.concatenate([mine(w, 1).astype(BF16) for w in weights], axis=1))

    w_qkv = gather_columns(self_query, self_key, self_value)
    w_rest = gather_columns(self_output, cross_query, cross_key, cross_value, cross_output)
    w_cq = w_rest[:, HALF : 2 * HALF]
    w_ckv = w_rest[:, 2 * HALF : 4 * HALF]
    w_so = both_cores(w_rest[:, :HALF], 1)
    w_co = both_cores(w_rest[:, 4 * HALF :], 1)
    inner_units = ffn_inner.reshape(ffn_inner.shape[0], n_fsdp, 2, unit)
    inner_units = lax.dynamic_index_in_dim(inner_units, core, 2, keepdims=False)
    w_inner = gather_fsdp(inner_units.reshape(ffn_inner.shape[0], hidden_half).astype(BF16))
    w_outer = gather_fsdp(mine(ffn_outer, 0).astype(BF16))

    x_group = gather_rows(tokens)
    e_group = gather_rows(encoded)
    cot = both_cores(cotangent, 0).astype(F32)
    cot_low = both_cores(cotangent, 0)

    x_wide = x_group.astype(F32)
    h_group = (x_wide * inverse_rms(x_wide) * gain_self).astype(BF16)
    qkv = dot_nn(h_group, w_qkv).astype(BF16)
    attn_self, lse_self = self_forward(chip_ref, tgt_lengths, bias_qk, qkv)
    attn_self_full = both_cores(attn_self.astype(BF16), 1)
    x_chip = lax.dynamic_slice_in_dim(x_group, chip * ROWS, ROWS, 0).astype(F32)
    h_chip = lax.dynamic_slice_in_dim(h_group, chip * ROWS, ROWS, 0)
    e_chip = lax.dynamic_slice_in_dim(e_group, chip * ROWS, ROWS, 0)
    x_mid = x_chip + dot_nn(attn_self_full, w_so)

    inv_cross = inverse_rms(x_mid)
    in_cross = (x_mid * inv_cross * gain_cross).astype(BF16)
    q_cross = dot_nn(in_cross, w_cq).astype(BF16)
    kv_cross = dot_nn(e_group, w_ckv).astype(BF16)
    attn_cross, lse_cross = cross_forward(chip_ref, tgt_lengths, enc_lengths, deal, q_cross, kv_cross)
    attn_cross_full = both_cores(attn_cross.astype(BF16), 1)
    x_late = x_mid + dot_nn(attn_cross_full, w_co)

    inv_ffn = inverse_rms(x_late)
    in_ffn = (x_late * inv_ffn * gain_ffn).astype(BF16)
    pre_act = dot_nn(in_ffn, w_inner)
    activated, slope = gelu_parts(pre_act)
    hidden = activated.astype(BF16)
    out_part = dot_nn(hidden, w_outer)

    def across(partial):
        other = lax.dynamic_slice_in_dim(partial, (1 - core) * rows, rows, 0)
        return mine(partial, 0) + swap_core(other)

    output = mine(x_late, 0) + across(out_part)

    d_outer = dot_tn(hidden, cot_low)
    d_pre = (dot_nt(cot_low, w_outer) * slope).astype(BF16)
    d_inner = dot_tn(in_ffn, d_pre)
    e_ffn = dot_nt(d_pre, w_inner)
    e_ffn = e_ffn + swap_core(e_ffn)
    dx_ffn, d_gain_ffn = rms_backward(x_late, inv_ffn, gain_ffn, e_ffn)
    grad_late = cot + dx_ffn
    late_low = grad_late.astype(BF16)

    d_co = dot_tn(attn_cross_full, mine(late_low, 1))
    go_cross = dot_nt(late_low, mine(w_co, 0)).astype(BF16)
    dq_cross, dkv_part = cross_grad(
        chip_ref, tgt_lengths, enc_lengths, deal, q_cross, go_cross, attn_cross, lse_cross, kv_cross
    )
    dkv_cross = sum_over(dkv_part, CHIPS).astype(BF16)
    d_cq = dot_tn(in_cross, dq_cross)
    e_cross = dot_nt(dq_cross, w_cq)
    e_cross = e_cross + swap_core(e_cross)
    dx_cross, d_gain_cross = rms_backward(x_mid, inv_cross, gain_cross, e_cross)
    grad_mid = grad_late + dx_cross
    mid_low = grad_mid.astype(BF16)
    d_ckv = dot_tn(e_chip, dkv_cross)
    enc_grad = across(dot_nt(dkv_cross, w_ckv))

    d_so = dot_tn(attn_self_full, mine(mid_low, 1))
    w_so_rows = mine(w_so, 0)
    go_self = dot_nt(mid_low, w_so_rows).astype(BF16)
    dq_self, stats, dist = self_query_grad(chip_ref, tgt_lengths, bias_qk, qkv, go_self, attn_self, lse_self)
    go_group = dot_nt(gather_rows(mine(mid_low, 0)), w_so_rows).astype(BF16)
    stats_group = spread(stats, CHIPS).reshape((-1,) + stats.shape)
    dkv_self = self_key_grad(chip_ref, tgt_lengths, bias_kq, qkv, go_group, stats_group)
    d_table = jnp.einsum("ht,tb->bh", dist[:LOCAL], QK_ONEHOT, precision=lax.Precision.HIGHEST)
    dqkv = jnp.concatenate([dq_self, dkv_self], axis=1)
    d_qkv = dot_tn(h_chip, dqkv)
    e_self = across(dot_nt(dqkv, w_qkv))
    x_own = tokens.astype(F32)
    dx_self, d_gain_self = rms_backward(x_own, inverse_rms(x_own), gain_self, e_self)
    grad_tokens = mine(grad_mid, 0) + dx_self

    def finish_columns(*grads):
        done = reduce_chips(scatter_fsdp(jnp.concatenate(grads, axis=1)))
        own, other = done.astype(F32), swap_core(done).astype(F32)
        return [
            by_core(own[:, i : i + HALF], other[:, i : i + HALF], 1) for i in range(0, done.shape[1], HALF)
        ]

    g_outer = reduce_chips(scatter_fsdp(d_outer))
    g_outer = both_cores(g_outer, 0).astype(F32)
    g_inner = reduce_chips(scatter_fsdp(d_inner)).reshape(-1, n_fsdp, 1, unit)
    g_inner = both_cores(g_inner, 2).reshape(ffn_inner.shape).astype(F32)
    g_co, g_cq, g_ck, g_cv = finish_columns(d_co, d_cq, d_ckv)
    g_so, g_sq, g_sk, g_sv = finish_columns(d_so, d_qkv)

    own_table = jnp.zeros((BUCKETS, 2, LOCAL), F32)
    own_table = lax.dynamic_update_slice(own_table, d_table[:, None], (0, core, 0))
    vector = jnp.concatenate(
        [d_gain_self, 0.5 * d_gain_cross, 0.5 * d_gain_ffn, own_table.reshape(-1)], axis=0
    )
    vector = lax.psum(vector, ("z", "y", "core", "fsdp"))

    def owned(value):
        size = value.shape[0] // n_fsdp
        return lax.dynamic_slice_in_dim(value, fsdp * size, size, 0)

    return (
        output, grad_tokens, enc_grad,
        owned(vector[:width]), owned(vector[width : 2 * width]), owned(vector[2 * width : 3 * width]),
        owned(vector[3 * width :].reshape(BUCKETS, HEADS)),
        g_sq, g_sk, g_sv, g_so, g_cq, g_ck, g_cv, g_co, g_inner, g_outer,
    )


def solution(mesh):
    n_ctx, n_fsdp = mesh.shape["ctx"], mesh.shape["fsdp"]
    n_z = 4
    grid = Mesh(mesh.devices.reshape(n_z, n_ctx // (2 * n_z), 2, n_fsdp), ("z", "y", "core", "fsdp"))
    by_rows = P(("fsdp", "z", "y", "core"), None)
    split = P("fsdp", None)
    vector = P("fsdp")
    in_specs = (by_rows,) * 3 + (split,) * 3 + (vector,) * 3 + (split,) * 11
    out_specs = (by_rows,) * 3 + (vector,) * 3 + (split,) * 11
    return jax.shard_map(on_device, mesh=grid, in_specs=in_specs, out_specs=out_specs, check_vma=False)
```

time: 2210 us -> 733 us (0.33)
  waiting for transfers between devices: 1490 us -> 260 us
  other arithmetic: 197 us -> 83.8 us
  local copies, waits for them, and re-layouts: 170 us -> 72.4 us
  matrix products: 133 us -> 58.8 us
  starting transfers between devices: 47.6 us -> 107 us
  Pallas kernels: 0 us -> 55.6 us
  loops' own time: 54.3 us -> 0 us
    ppermute x64 -> x26, waiting for transfers between devices: 541 us -> 49.7 us  [the longest x5 31.9 us: gather_fsdp(): other = lax.ppermute(own, 'fsdp', [(0, 1), (1, 0)])]
    reduce_scatter x11 -> x0, waiting for transfers between devices: 391 us -> none  [the longest x1 113 us: on_device(): lax.psum_scatter(d_outer, 'fsdp', scatter_dimension=0, tiled=True)]
    all_gather x14 -> x0, waiting for transfers between devices: 285 us -> none  [the longest x1 60.9 us: on_device(): lax.all_gather(ffn_outer.astype(jnp.bfloat16), 'fsdp', axis=0, tiled=True)]
    psum x1 -> x0, waiting for transfers between devices: 268 us -> none  [on_device(): lax.psum((shards[0], shards[1], shards[2], shards[3], shards[4], shards[5...]
    all_to_all x0 -> x20, waiting for transfers between devices: none -> 210 us  [the longest x11 107 us: spread(): lax.all_to_all(jnp.broadcast_to(value[None], (count,) + value.shape), axe...]
    all_to_all x0 -> x20, starting transfers between devices: none -> 96.8 us  [the longest x11 53.4 us: spread(): lax.all_to_all(jnp.broadcast_to(value[None], (count,) + value.shape), axe...]
    add x163 -> x3, other arithmetic: 89 us -> 5.51 us  [the longest x1 1.91 us: on_device(): grad_tokens = mine(grad_mid, 0) + dx_self]
    dot_general x129 -> x25, matrix products: 133 us -> 58.8 us  [the longest x7 24.6 us: dot_nn(): lax.dot_general(left, right, (((1,), (0,)), ((), ())), preferred_element_...]
  transfers between devices with their start and end apart: 90 -> 46, of which waited for: 51 -> 19; matrix products, arithmetic and copies ran while one was open for 16% -> 26% of each run, Pallas kernels for 0% -> 8%
where the time goes in v1:
time: 733 us; the launch traced here: 719 us
  waiting for transfers between devices  260 us (35%)
  starting transfers between devices  107 us (15%)
  other arithmetic  83.8 us (11%)
  blocking collectives  79 us (11%)
  local copies, waits for them, and re-layouts  72.4 us (10%)
  matrix products  58.8 us (8%)
  Pallas kernels  55.6 us (8%)
    all_to_all x11, waiting for transfers between devices, spread(): lax.all_to_all(jnp.broadcast_to(value[None], (count,) + value.shape), axe...  107 us
    all_to_all x9, waiting for transfers between devices, sum_over(): lax.all_to_all(parts, axis, 0, 0, tiled=True).astype(F32)  103 us
    pallas_call x5, Pallas kernels, call(): pl.pallas_call(kernel, out_shape=[jax.ShapeDtypeStruct(s, d) for s, d in...  55.6 us
    all_to_all x11, starting transfers between devices, spread(): lax.all_to_all(jnp.broadcast_to(value[None], (count,) + value.shape), axe...  53.4 us
    all_to_all x9, starting transfers between devices, sum_over(): lax.all_to_all(parts, axis, 0, 0, tiled=True).astype(F32)  43.4 us
    psum x1, blocking collectives, on_device(): vector = lax.psum(vector, ('z', 'y', 'core', 'fsdp'))  40 us
    all_to_all x1, blocking collectives, spread(): lax.all_to_all(jnp.broadcast_to(value[None], (count,) + value.shape), axe...  39 us
    ppermute x5, waiting for transfers between devices, gather_fsdp(): other = lax.ppermute(own, 'fsdp', [(0, 1), (1, 0)])  31.9 us
  transfers between devices with their start and end apart: 46, of which 19 were waited for; matrix products, arithmetic and copies ran while one was open for 26% of the time, Pallas kernels for 8%

profile of v1, /device:TPU:0, one launch (start us, length us, event | category | flops | bytes accessed | tf_op | source)
XLA Modules:
  0.0 718.8 jit_solution(9958616743185526697)
XLA Ops:
  3.0 7.4 %all-to-all-start = ((bf16[8,128,768]{2,1,0:T(8,128)(2,1)}), bf16[8,128,768]{2,1,0:T(8,128)(2,1)}, u32[]{:S(2)}, u32[]{:S(2)}) async-start(bf16[8,128,768]{2,1,0:T(8,128)(2,1)} %broadcast_in_dim.36), calls=%async_computation | async-start | bytes 3145728 | tf_op jit(solution)/shard_map/all_to_all | solution.py:524
  10.6 36.9 %all-to-all-done = bf16[8,128,768]{2,1,0:T(8,128)(2,1)} async-done(((bf16[8,128,768]{2,1,0:T(8,128)(2,1)}), bf16[8,128,768]{2,1,0:T(8,128)(2,1)}, u32[]{:S(2)}, u32[]{:S(2)}) %all-to-all-start) | async-done | bytes 1572896 | tf_op jit(solution)/shard_map/all_to_all | solution.py:524
  78.3 20.8 %collective-permute-done.4 = bf16[384,1920]{1,0:T(8,128)(2,1)} collective-permute-done((bf16[384,1920]{1,0:T(8,128)(2,1)}, bf16[384,1920]{1,0:T(8,128)(2,1)}, u32[]{:S(2)}, u32[]{:S(2)}) %collective-permute-start.4) | collective-permute-done | bytes 1474592 | tf_op jit(solution)/shard_map/ppermute | solution.py:503
  109.2 8.9 %collective-permute-done.2 = bf16[384,1152]{1,0:T(8,128)(2,1)} collective-permute-done((bf16[384,1152]{1,0:T(8,128)(2,1)}, bf16[384,1152]{1,0:T(8,128)(2,1)}, u32[]{:S(2)}, u32[]{:S(2)}) %collective-permute-start.2) | collective-permute-done | bytes 884768 | tf_op jit(solution)/shard_map/ppermute | solution.py:503
  118.1 8.0 %convolution_convert_fusion.qkv_ref = bf16[2048,1152]{1,0:T(8,128)(2,1)} fusion(bf16[2048,768]{1,0:T(8,128)(2,1)S(1)} %multiply_convert_fusion, bf16[384,1152]{1,0:T(8,128)(2,1)} %collective-permute-done.2, bf16[384,384]{1,0:T(8,128)(2,1)S(1)} %copy-done.31, bf16[384,384]{1,0:T(8,128)(2,1)S(1)} %copy-done.34, bf16[384,384]{1,0:T(8,128)(2,1)S(1)} %copy-done.28, ...), kind=kOutput, calls=%fused_computation | convolution fusion | flops 3641278464 | bytes 9633793 | tf_op jit(solution)/shard_map/dot_general | solution.py:65
  126.1 5.9 shard_map.350
  144.8 13.5 %shard_map.351 = (f32[256,384]{1,0:T(8,128)}, f32[256,128]{1,0:T(8,128)}) custom-call(s32[1]{0:T(128)} %bitcast.3.chip_ref, s32[1,6]{1,0:T(1,128)} %len_ref.9, s32[1,6]{1,0:T(1,128)} %enc_ref.3, s32[1,6]{1,0:T(1,128)} %deal_ref.3, bf16[256,384]{1,0:T(8,128)(2,1)} %convolution_convert_fusion.5.q_ref, bf16[2048,768]{1,0:T(8,128)(2,1)} %convolution_convert_fusion.1.kv_ref), custom_call_target="tpu_custom_call" | custom-call | flops 1610612736 | bytes 3866624 | tf_op jit(solution)/shard_map/pallas_call | solution.py:418
  194.2 17.1 %shard_map.352 = (bf16[256,384]{1,0:T(8,128)(2,1)}, bf16[2048,768]{1,0:T(8,128)(2,1)}) custom-call(s32[1]{0:T(128)} %bitcast.3.chip_ref, s32[1,6]{1,0:T(1,128)} %len_ref.9, s32[1,6]{1,0:T(1,128)} %enc_ref.3, s32[1,6]{1,0:T(1,128)} %deal_ref.3, bf16[256,384]{1,0:T(8,128)(2,1)} %convolution_convert_fusion.5.q_ref, ...), custom_call_target="tpu_custom_call" | custom-call | flops 4026531840 | bytes 7405568 | tf_op jit(solution)/shard_map/pallas_call | solution.py:418
  219.7 17.8 %collective-permute-done.22 = bf16[384,1536]{1,0:T(8,128)(2,1)} collective-permute-done((bf16[384,1536]{1,0:T(8,128)(2,1)}, bf16[384,1536]{1,0:T(8,128)(2,1)}, u32[]{:S(2)}, u32[]{:S(2)}) %collective-permute-start.22) | collective-permute-done | bytes 1179680 | tf_op jit(solution)/shard_map/ppermute | solution.py:519
  243.7 12.0 %all-to-all-start.13 = ((bf16[2,192,1536]{2,1,0:T(8,128)(2,1)}), bf16[2,192,1536]{2,1,0:T(8,128)(2,1)S(1)}, u32[]{:S(2)}, u32[]{:S(2)}) async-start(bf16[2,192,1536]{2,1,0:T(8,128)(2,1)} %bitcast.23), calls=%async_computation.13 | async-start | bytes 2359296 | tf_op jit(solution)/shard_map/all_to_all | solution.py:543
  259.7 6.7 shard_map.353
  272.3 9.1 %all-to-all-start.3 = ((f32[8,16,256]{2,1,0:T(8,128)}), f32[8,16,256]{2,1,0:T(8,128)}, u32[]{:S(2)}, u32[]{:S(2)}) async-start(f32[8,16,256]{2,1,0:T(8,128)} %broadcast_in_dim.39), calls=%async_computation.3 | async-start | bytes 262144 | tf_op jit(solution)/shard_map/all_to_all | solution.py:524
  282.5 6.3 all-to-all-done.3.stat_ref
  293.4 13.1 %all-to-all-done.18 = bf16[4,96,768]{2,1,0:T(8,128)(2,1)S(1)} async-done(((bf16[4,96,768]{2,1,0:T(8,128)(2,1)}), bf16[4,96,768]{2,1,0:T(8,128)(2,1)S(1)}, u32[]{:S(2)}, u32[]{:S(2)}) %all-to-all-start.18) | async-done | bytes 589856 | tf_op jit(solution)/shard_map/all_to_all | solution.py:543
  310.2 14.9 %all-to-all-done.14 = bf16[4,48,1536]{2,1,0:T(8,128)(2,1)S(1)} async-done(((bf16[4,48,1536]{2,1,0:T(8,128)(2,1)}), bf16[4,48,1536]{2,1,0:T(8,128)(2,1)S(1)}, u32[]{:S(2)}, u32[]{:S(2)}) %all-to-all-start.14) | async-done | bytes 589856 | tf_op jit(solution)/shard_map/all_to_all | solution.py:543
  329.4 15.3 %all-to-all-done.19 = bf16[4,96,768]{2,1,0:T(8,128)(2,1)S(1)} async-done(((bf16[4,96,768]{2,1,0:T(8,128)(2,1)}), bf16[4,96,768]{2,1,0:T(8,128)(2,1)S(1)}, u32[]{:S(2)}, u32[]{:S(2)}) %all-to-all-start.19) | async-done | bytes 589856 | tf_op jit(solution)/shard_map/all_to_all | solution.py:524
  345.6 39.0 %all_to_all.105 = bf16[8,128,768]{2,1,0:T(8,128)(2,1)S(1)} all-to-all(bf16[8,128,768]{2,1,0:T(8,128)(2,1)S(1)} %broadcast_in_dim.38), channel_id=1, replica_groups=mesh['z'=4,'y'=2,'core'=2,'fsdp'=2] {'z','y'}, dimensions={0} | all-to-all | bytes 3145728 | tf_op jit(solution)/shard_map/all_to_all | solution.py:524
  402.6 12.4 %shard_map.354 = bf16[256,768]{1,0:T(8,128)(2,1)} custom-call(s32[1]{0:T(128)} %bitcast.3.chip_ref, s32[1,6]{1,0:T(1,128)} %len_ref.9, f32[8,512]{1,0:T(8,128)} %concatenate.193.bias_ref, bf16[2048,1152]{1,0:T(8,128)(2,1)} %convolution_convert_fusion.qkv_ref, bf16[2048,384]{1,0:T(8,128)(2,1)} %convolution_convert_fusion.2.go_ref, ...), custom_call_target="tpu_custom_call" | custom-call | flops 3221225472 | bytes 6832128 | tf_op jit(solution)/shard_map/pallas_call | solution.py:418
  416.8 41.9 %all-to-all-done.4 = bf16[8,256,768]{2,1,0:T(8,128)(2,1)} async-done(((bf16[8,256,768]{2,1,0:T(8,128)(2,1)}), bf16[8,256,768]{2,1,0:T(8,128)(2,1)}, u32[]{:S(2)}, u32[]{:S(2)}) %all-to-all-start.4) | async-done | bytes 3145760 | tf_op jit(solution)/shard_map/all_to_all | solution.py:543
  475.1 5.3 all-to-all-done.15
  490.4 11.2 %all-to-all-done.20 = bf16[2,384,768]{2,1,0:T(8,128)(2,1)} async-done(((bf16[2,384,768]{2,1,0:T(8,128)(2,1)}), bf16[2,384,768]{2,1,0:T(8,128)(2,1)}, u32[]{:S(2)}, u32[]{:S(2)}) %all-to-all-start.20) | async-done | bytes 1179680 | tf_op jit(solution)/shard_map/all_to_all | solution.py:524
  511.0 11.0 %all-to-all-done.16 = bf16[2,192,1536]{2,1,0:T(8,128)(2,1)} async-done(((bf16[2,192,1536]{2,1,0:T(8,128)(2,1)}), bf16[2,192,1536]{2,1,0:T(8,128)(2,1)}, u32[]{:S(2)}, u32[]{:S(2)}) %all-to-all-start.16) | async-done | bytes 1179680 | tf_op jit(solution)/shard_map/all_to_all | solution.py:524
  529.3 8.9 %all-to-all-done.5 = bf16[2,192,1536]{2,1,0:T(8,128)(2,1)S(1)} async-done(((bf16[2,192,1536]{2,1,0:T(8,128)(2,1)}), bf16[2,192,1536]{2,1,0:T(8,128)(2,1)S(1)}, u32[]{:S(2)}, u32[]{:S(2)}) %all-to-all-start.5) | async-done | bytes 1179680 | tf_op jit(solution)/shard_map/all_to_all | solution.py:543
  543.0 10.6 %all-to-all-done.9 = bf16[2,192,1536]{2,1,0:T(8,128)(2,1)S(1)} async-done(((bf16[2,192,1536]{2,1,0:T(8,128)(2,1)}), bf16[2,192,1536]{2,1,0:T(8,128)(2,1)S(1)}, u32[]{:S(2)}, u32[]{:S(2)}) %all-to-all-start.9) | async-done | bytes 1179680 | tf_op jit(solution)/shard_map/all_to_all | solution.py:543
  578.0 5.2 fusion.7
  584.4 8.8 %all-to-all-done.10 = bf16[4,48,1536]{2,1,0:T(8,128)(2,1)S(1)} async-done(((bf16[4,48,1536]{2,1,0:T(8,128)(2,1)}), bf16[4,48,1536]{2,1,0:T(8,128)(2,1)S(1)}, u32[]{:S(2)}, u32[]{:S(2)}) %all-to-all-start.10) | async-done | bytes 589856 | tf_op jit(solution)/shard_map/all_to_all | solution.py:543
  601.9 6.1 copy.63
  608.0 6.2 copy.64
  620.2 5.0 all-to-all-start.11
  628.1 40.0 %psum.7 = f32[2688]{0:T(1024)S(1)} all-reduce(f32[2688]{0:T(1024)S(1)} %pad_maximum_fusion.5), channel_id=1, replica_groups=mesh['z'=4,'y'=2,'core'=2,'fsdp'=2] {'z','y','core','fsdp'}, use_global_device_ids=true, to_apply=%region_11.12 | all-reduce | flops 2688 | bytes 21504 | tf_op jit(solution)/shard_map/psum | solution.py:717
  679.4 10.2 %all-to-all-done.8 = bf16[2,192,1536]{2,1,0:T(8,128)(2,1)S(1)} async-done(((bf16[2,192,1536]{2,1,0:T(8,128)(2,1)}), bf16[2,192,1536]{2,1,0:T(8,128)(2,1)S(1)}, u32[]{:S(2)}, u32[]{:S(2)}) %all-to-all-start.8) | async-done | bytes 1179680 | tf_op jit(solution)/shard_map/all_to_all | solution.py:524
  696.1 11.4 %all-to-all-done.12 = bf16[2,192,1536]{2,1,0:T(8,128)(2,1)S(1)} async-done(((bf16[2,192,1536]{2,1,0:T(8,128)(2,1)}), bf16[2,192,1536]{2,1,0:T(8,128)(2,1)S(1)}, u32[]{:S(2)}, u32[]{:S(2)}) %all-to-all-start.12) | async-done | bytes 1179680 | tf_op jit(solution)/shard_map/all_to_all | solution.py:524
  (345 shorter events, 269.9 us)
Async XLA Ops:
  3.0 44.5 %all-to-all-start = ((bf16[8,128,768]{2,1,0:T(8,128)(2,1)}), bf16[8,128,768]{2,1,0:T(8,128)(2,1)}, u32[]{:S(2)}, u32[]{:S(2)}) async-start(bf16[8,128,768]{2,1,0:T(8,128)(2,1)} %broadcast_in_dim.36), calls=%async_computation | async-start | bytes 3145728 | tf_op jit(solution)/shard_map/all_to_all | solution.py:524
  48.8 55.4 %all-to-all-start.1 = ((bf16[8,128,768]{2,1,0:T(8,128)(2,1)}), bf16[8,128,768]{2,1,0:T(8,128)(2,1)}, u32[]{:S(2)}, u32[]{:S(2)}) async-start(bf16[8,128,768]{2,1,0:T(8,128)(2,1)} %broadcast_in_dim.37), calls=%async_computation.1 | async-start | bytes 3145728 | tf_op jit(solution)/shard_map/all_to_all | solution.py:524
  53.1 22.9 %collective-permute-start.1 = (bf16[1,1344]{1,0:T(2,128)(2,1)S(1)}, bf16[1,1344]{1,0:T(2,128)(2,1)S(1)}, u32[]{:S(2)}, u32[]{:S(2)}) collective-permute-start(bf16[1,1344]{1,0:T(2,128)(2,1)S(1)} %constant_dynamic-update-slice_fusion), channel_id=1, source_target_pairs={{0,1},{1,0},{2,3},{3,2},{4,5},{5,4},{6,7},{7,6},{8,9},{9,8},{10,11... | collective-permute-start | bytes 8072 | tf_op jit(solution)/shard_map/ppermute | solution.py:503
  54.6 116.9 %collective-permute-start.12 = (bf16[128,768]{1,0:T(8,128)(2,1)}, bf16[128,768]{1,0:T(8,128)(2,1)}, u32[]{:S(2)}, u32[]{:S(2)}) collective-permute-start(bf16[128,768]{1,0:T(8,128)(2,1)} %param.25), channel_id=1, source_target_pairs={{0,2},{2,0},{1,3},{3,1},{4,6},{6,4},{5,7},{7,5},{8,10},{10,8},{9,1... | collective-permute-start | bytes 589832 | tf_op jit(solution)/shard_map/ppermute | solution.py:485
  63.7 35.4 %collective-permute-start.4 = (bf16[384,1920]{1,0:T(8,128)(2,1)}, bf16[384,1920]{1,0:T(8,128)(2,1)}, u32[]{:S(2)}, u32[]{:S(2)}) collective-permute-start(bf16[384,1920]{1,0:T(8,128)(2,1)} %fusion.41), channel_id=1, source_target_pairs={{0,1},{1,0},{2,3},{3,2},{4,5},{5,4},{6,7},{7,6},{8,9},{9,8},{10,11... | collective-permute-start | bytes 4423688 | tf_op jit(solution)/shard_map/ppermute | solution.py:503
  65.7 38.5 %collective-permute-start = (bf16[8,128,768]{2,1,0:T(8,128)(2,1)}, bf16[8,128,768]{2,1,0:T(8,128)(2,1)}, u32[]{:S(2)}, u32[]{:S(2)}) collective-permute-start(bf16[8,128,768]{2,1,0:T(8,128)(2,1)} %all-to-all-done), channel_id=1, source_target_pairs={{0,2},{2,0},{1,3},{3,1},{4,6},{6,4},{5,7},{7,5},{8,10},{10,8},{9,1... | collective-permute-start | bytes 4718600 | tf_op jit(solution)/shard_map/ppermute | solution.py:485
  67.0 51.0 %collective-permute-start.2 = (bf16[384,1152]{1,0:T(8,128)(2,1)}, bf16[384,1152]{1,0:T(8,128)(2,1)}, u32[]{:S(2)}, u32[]{:S(2)}) collective-permute-start(bf16[384,1152]{1,0:T(8,128)(2,1)} %pad_maximum_fusion.1), channel_id=1, source_target_pairs={{0,1},{1,0},{2,3},{3,2},{4,5},{5,4},{6,7},{7,6},{8,9},{9,8},{10,11... | collective-permute-start | bytes 2654216 | tf_op jit(solution)/shard_map/ppermute | solution.py:503
  76.0 95.5 %collective-permute-start.10 = (bf16[768,768]{1,0:T(8,128)(2,1)}, bf16[768,768]{1,0:T(8,128)(2,1)}, u32[]{:S(2)}, u32[]{:S(2)}) collective-permute-start(bf16[768,768]{1,0:T(8,128)(2,1)} %dynamic-slice_convert_fusion.3), channel_id=1, source_target_pairs={{0,1},{1,0},{2,3},{3,2},{4,5},{5,4},{6,7},{7,6},{8,9},{9,8},{10,11... | collective-permute-start | bytes 3538952 | tf_op jit(solution)/shard_map/ppermute | solution.py:503
  99.1 69.1 %collective-permute-start.9 = (bf16[384,1536]{0,1:T(8,128)(2,1)}, bf16[384,1536]{0,1:T(8,128)(2,1)}, u32[]{:S(2)}, u32[]{:S(2)}) collective-permute-start(bf16[384,1536]{0,1:T(8,128)(2,1)} %bitcast.9), channel_id=1, source_target_pairs={{0,1},{1,0},{2,3},{3,2},{4,5},{5,4},{6,7},{7,6},{8,9},{9,8},{10,11... | collective-permute-start | bytes 3538952 | tf_op jit(solution)/shard_map/ppermute | solution.py:503
  104.2 28.8 %collective-permute-start.6 = (bf16[8,128,768]{2,1,0:T(8,128)(2,1)}, bf16[8,128,768]{2,1,0:T(8,128)(2,1)}, u32[]{:S(2)}, u32[]{:S(2)}) collective-permute-start(bf16[8,128,768]{2,1,0:T(8,128)(2,1)} %all-to-all-done.1), channel_id=1, source_target_pairs={{0,2},{2,0},{1,3},{3,1},{4,6},{6,4},{5,7},{7,5},{8,10},{10,8},{9,1... | collective-permute-start | bytes 4718600 | tf_op jit(solution)/shard_map/ppermute | solution.py:485
  118.0 23.0 %collective-permute-start.5 = (bf16[768,384]{1,0:T(8,128)(2,1)S(1)}, bf16[768,384]{1,0:T(8,128)(2,1)}, u32[]{:S(2)}, u32[]{:S(2)}) collective-permute-start(bf16[768,384]{1,0:T(8,128)(2,1)S(1)} %copy-done.23), channel_id=1, source_target_pairs={{0,2},{2,0},{1,3},{3,1},{4,6},{6,4},{5,7},{7,5},{8,10},{10,8},{9,1... | collective-permute-start | bytes 1769480 | tf_op jit(solution)/shard_map/ppermute | solution.py:485
  141.0 21.3 %collective-permute-start.8 = (bf16[768,384]{1,0:T(8,128)(2,1)S(1)}, bf16[768,384]{1,0:T(8,128)(2,1)}, u32[]{:S(2)}, u32[]{:S(2)}) collective-permute-start(bf16[768,384]{1,0:T(8,128)(2,1)S(1)} %get-tuple-element.99), channel_id=1, source_target_pairs={{0,2},{2,0},{1,3},{3,1},{4,6},{6,4},{5,7},{7,5},{8,10},{10,8},{9,1... | collective-permute-start | bytes 1769480 | tf_op jit(solution)/shard_map/ppermute | solution.py:485
  183.5 30.0 %collective-permute-start.24 = (bf16[768,768]{1,0:T(8,128)(2,1)}, bf16[768,768]{1,0:T(8,128)(2,1)}, u32[]{:S(2)}, u32[]{:S(2)}) collective-permute-start(bf16[768,768]{1,0:T(8,128)(2,1)} %dynamic-slice_convert_fusion), channel_id=1, source_target_pairs={{0,1},{1,0},{2,3},{3,2},{4,5},{5,4},{6,7},{7,6},{8,9},{9,8},{10,11... | collective-permute-start | bytes 3538952 | tf_op jit(solution)/shard_map/ppermute | solution.py:519
  188.3 49.2 %collective-permute-start.22 = (bf16[384,1536]{1,0:T(8,128)(2,1)}, bf16[384,1536]{1,0:T(8,128)(2,1)}, u32[]{:S(2)}, u32[]{:S(2)}) collective-permute-start(bf16[384,1536]{1,0:T(8,128)(2,1)} %dynamic-slice_convert_fusion.1), channel_id=1, source_target_pairs={{0,1},{1,0},{2,3},{3,2},{4,5},{5,4},{6,7},{7,6},{8,9},{9,8},{10,11... | collective-permute-start | bytes 3538952 | tf_op jit(solution)/shard_map/ppermute | solution.py:519
  213.5 27.3 %collective-permute-start.14 = (f32[256,768]{1,0:T(8,128)}, f32[256,768]{1,0:T(8,128)S(1)}, u32[]{:S(2)}, u32[]{:S(2)}) collective-permute-start(f32[256,768]{1,0:T(8,128)} %fusion.17), channel_id=1, source_target_pairs={{0,2},{2,0},{1,3},{3,1},{4,6},{6,4},{5,7},{7,5},{8,10},{10,8},{9,1... | collective-permute-start | bytes 2359304 | tf_op jit(solution)/shard_map/ppermute | solution.py:485
  216.1 27.6 %all-to-all-start.17 = ((bf16[2,384,768]{2,1,0:T(8,128)(2,1)}), bf16[2,384,768]{2,1,0:T(8,128)(2,1)S(1)}, u32[]{:S(2)}, u32[]{:S(2)}) async-start(bf16[2,384,768]{2,1,0:T(8,128)(2,1)} %bitcast.27), calls=%async_computation.17 | async-start | bytes 2359296 | tf_op jit(solution)/shard_map/all_to_all | solution.py:543
  243.7 27.2 %all-to-all-start.13 = ((bf16[2,192,1536]{2,1,0:T(8,128)(2,1)}), bf16[2,192,1536]{2,1,0:T(8,128)(2,1)S(1)}, u32[]{:S(2)}, u32[]{:S(2)}) async-start(bf16[2,192,1536]{2,1,0:T(8,128)(2,1)} %bitcast.23), calls=%async_computation.13 | async-start | bytes 2359296 | tf_op jit(solution)/shard_map/all_to_all | solution.py:543
  306.6 18.4 %all-to-all-start.14 = ((bf16[4,48,1536]{2,1,0:T(8,128)(2,1)}), bf16[4,48,1536]{2,1,0:T(8,128)(2,1)S(1)}, u32[]{:S(2)}, u32[]{:S(2)}) async-start(bf16[4,48,1536]{2,1,0:T(8,128)(2,1)} %bitcast.24), calls=%async_computation.14 | async-start | bytes 1179648 | tf_op jit(solution)/shard_map/all_to_all | solution.py:543
  325.9 18.8 %all-to-all-start.19 = ((bf16[4,96,768]{2,1,0:T(8,128)(2,1)}), bf16[4,96,768]{2,1,0:T(8,128)(2,1)S(1)}, u32[]{:S(2)}, u32[]{:S(2)}) async-start(bf16[4,96,768]{2,1,0:T(8,128)(2,1)} %broadcast_in_dim.51), calls=%async_computation.19 | async-start | bytes 1179648 | tf_op jit(solution)/shard_map/all_to_all | solution.py:524
  384.6 74.1 %all-to-all-start.4 = ((bf16[8,256,768]{2,1,0:T(8,128)(2,1)}), bf16[8,256,768]{2,1,0:T(8,128)(2,1)}, u32[]{:S(2)}, u32[]{:S(2)}) async-start(bf16[8,256,768]{2,1,0:T(8,128)(2,1)} %bitcast.59), calls=%async_computation.4 | async-start | bytes 6291456 | tf_op jit(solution)/shard_map/all_to_all | solution.py:543
  460.5 19.9 %all-to-all-start.15 = ((bf16[4,48,1536]{2,1,0:T(8,128)(2,1)}), bf16[4,48,1536]{2,1,0:T(8,128)(2,1)}, u32[]{:S(2)}, u32[]{:S(2)}) async-start(bf16[4,48,1536]{2,1,0:T(8,128)(2,1)} %broadcast_in_dim.48), calls=%async_computation.15 | async-start | bytes 1179648 | tf_op jit(solution)/shard_map/all_to_all | solution.py:524
  467.0 41.2 %collective-permute-start.18 = (bf16[384,1536]{1,0:T(8,128)(2,1)}, bf16[384,1536]{1,0:T(8,128)(2,1)}, u32[]{:S(2)}, u32[]{:S(2)}) collective-permute-start(bf16[384,1536]{1,0:T(8,128)(2,1)} %fusion.2), channel_id=1, source_target_pairs={{0,1},{1,0},{2,3},{3,2},{4,5},{5,4},{6,7},{7,6},{8,9},{9,8},{10,11... | collective-permute-start | bytes 3538952 | tf_op jit(solution)/shard_map/ppermute | solution.py:519
  482.6 19.1 %all-to-all-start.20 = ((bf16[2,384,768]{2,1,0:T(8,128)(2,1)}), bf16[2,384,768]{2,1,0:T(8,128)(2,1)}, u32[]{:S(2)}, u32[]{:S(2)}) async-start(bf16[2,384,768]{2,1,0:T(8,128)(2,1)} %broadcast_in_dim.53), calls=%async_computation.20 | async-start | bytes 2359296 | tf_op jit(solution)/shard_map/all_to_all | solution.py:524
  489.9 35.7 %collective-permute-start.20 = (bf16[384,1536]{0,1:T(8,128)(2,1)}, bf16[384,1536]{0,1:T(8,128)(2,1)}, u32[]{:S(2)}, u32[]{:S(2)}) collective-permute-start(bf16[384,1536]{0,1:T(8,128)(2,1)} %dynamic-slice_convert_fusion.2), channel_id=1, source_target_pairs={{0,1},{1,0},{2,3},{3,2},{4,5},{5,4},{6,7},{7,6},{8,9},{9,8},{10,11... | collective-permute-start | bytes 3538952 | tf_op jit(solution)/shard_map/ppermute | solution.py:519
  503.8 18.1 %all-to-all-start.16 = ((bf16[2,192,1536]{2,1,0:T(8,128)(2,1)}), bf16[2,192,1536]{2,1,0:T(8,128)(2,1)}, u32[]{:S(2)}, u32[]{:S(2)}) async-start(bf16[2,192,1536]{2,1,0:T(8,128)(2,1)} %broadcast_in_dim.50), calls=%async_computation.16 | async-start | bytes 2359296 | tf_op jit(solution)/shard_map/all_to_all | solution.py:524
  553.5 18.6 %all-to-all-start.6 = ((bf16[4,48,1536]{2,1,0:T(8,128)(2,1)}), bf16[4,48,1536]{2,1,0:T(8,128)(2,1)}, u32[]{:S(2)}, u32[]{:S(2)}) async-start(bf16[4,48,1536]{2,1,0:T(8,128)(2,1)} %bitcast.16), calls=%async_computation.6 | async-start | bytes 1179648 | tf_op jit(solution)/shard_map/all_to_all | solution.py:543
  567.9 29.7 %collective-permute-start.23 = (bf16[384,2,1,768]{3,0,2,1:T(8,128)(2,1)S(1)}, bf16[384,2,1,768]{3,0,2,1:T(8,128)(2,1)}, u32[]{:S(2)}, u32[]{:S(2)}) collective-permute-start(bf16[384,2,1,768]{3,0,2,1:T(8,128)(2,1)S(1)} %copy.61), channel_id=1, source_target_pairs={{0,2},{2,0},{1,3},{3,1},{4,6},{6,4},{5,7},{7,5},{8,10},{10,8},{9,1... | collective-permute-start | bytes 3538952 | tf_op jit(solution)/shard_map/ppermute | solution.py:485
  572.1 21.1 %all-to-all-start.10 = ((bf16[4,48,1536]{2,1,0:T(8,128)(2,1)}), bf16[4,48,1536]{2,1,0:T(8,128)(2,1)S(1)}, u32[]{:S(2)}, u32[]{:S(2)}) async-start(bf16[4,48,1536]{2,1,0:T(8,128)(2,1)} %bitcast.64), calls=%async_computation.10 | async-start | bytes 1179648 | tf_op jit(solution)/shard_map/all_to_all | solution.py:543
  594.1 25.3 %all-to-all-start.7 = ((bf16[4,48,1536]{2,1,0:T(8,128)(2,1)}), bf16[4,48,1536]{2,1,0:T(8,128)(2,1)S(1)}, u32[]{:S(2)}, u32[]{:S(2)}) async-start(bf16[4,48,1536]{2,1,0:T(8,128)(2,1)} %broadcast_in_dim.42), calls=%async_computation.7 | async-start | bytes 1179648 | tf_op jit(solution)/shard_map/all_to_all | solution.py:524
  620.2 50.0 %all-to-all-start.11 = ((bf16[4,48,1536]{2,1,0:T(8,128)(2,1)}), bf16[4,48,1536]{2,1,0:T(8,128)(2,1)S(1)}, u32[]{:S(2)}, u32[]{:S(2)}) async-start(bf16[4,48,1536]{2,1,0:T(8,128)(2,1)} %broadcast_in_dim.45), calls=%async_computation.11 | async-start | bytes 1179648 | tf_op jit(solution)/shard_map/all_to_all | solution.py:524
  626.0 51.6 %collective-permute-start.17 = (f32[128,768]{1,0:T(8,128)}, f32[128,768]{1,0:T(8,128)}, u32[]{:S(2)}, u32[]{:S(2)}) collective-permute-start(f32[128,768]{1,0:T(8,128)} %constant_dynamic-slice_fusion.1), channel_id=1, source_target_pairs={{0,2},{2,0},{1,3},{3,1},{4,6},{6,4},{5,7},{7,5},{8,10},{10,8},{9,1... | collective-permute-start | bytes 1179656 | tf_op jit(solution)/shard_map/ppermute | solution.py:485
  671.3 18.2 %all-to-all-start.8 = ((bf16[2,192,1536]{2,1,0:T(8,128)(2,1)}), bf16[2,192,1536]{2,1,0:T(8,128)(2,1)S(1)}, u32[]{:S(2)}, u32[]{:S(2)}) async-start(bf16[2,192,1536]{2,1,0:T(8,128)(2,1)} %broadcast_in_dim.44), calls=%async_computation.8 | async-start | bytes 2359296 | tf_op jit(solution)/shard_map/all_to_all | solution.py:524
  (79 other events, 749.8 us)

commit v2 on v1

v2 whole, which is shorter than its diff:
```python
import functools
import math

import jax
import jax.numpy as jnp
import numpy as np
from jax import lax
from jax.experimental import pallas as pl
from jax.experimental.pallas import tpu as pltpu
from jax.sharding import Mesh
from jax.sharding import PartitionSpec as P

HEADS = 12
HEAD_DIM = 64
BUCKETS = 32
EPS = 1e-06
NEG = -1e30
GELU_C = 0.7978845608028654
GELU_A = 0.044715

LOCAL = HEADS // 2
PAIRS = LOCAL // 2
HALF = LOCAL * HEAD_DIM
ROWS = 256
VMEM_LIMIT = 56 << 20

F32 = jnp.float32
BF16 = jnp.bfloat16


def bucket_edges():
    edges = []
    for level in range(1, 16):
        distance = 16
        while int(math.log(distance / 16.0) / math.log(8.0) * 16.0) < level:
            distance += 1
        edges.append(distance)
    return edges


def buckets_of(distances):
    clipped = np.maximum(np.asarray(distances), 0)
    large = np.full(clipped.shape, 16)
    for edge in bucket_edges():
        large = large + (clipped >= edge)
    return np.where(clipped < 16, clipped, large)


LANES = np.arange(2 * ROWS)
QK_DISTANCE = np.where(LANES <= ROWS, ROWS - LANES, 3 * ROWS - LANES)
KQ_DISTANCE = LANES
QK_ONEHOT = np.eye(BUCKETS, dtype=np.float32)[buckets_of(QK_DISTANCE)]
KQ_ONEHOT = np.eye(BUCKETS, dtype=np.float32)[buckets_of(KQ_DISTANCE)]


def dot_nt(left, right):
    return lax.dot_general(left, right, (((1,), (1,)), ((), ())), preferred_element_type=F32)


def dot_tn(left, right):
    return lax.dot_general(left, right, (((0,), (0,)), ((), ())), preferred_element_type=F32)


def dot_nn(left, right):
    return lax.dot_general(left, right, (((1,), (0,)), ((), ())), preferred_element_type=F32)


def spans(ref):
    starts, ends, at = [], [], jnp.int32(0)
    for i in range(ref.shape[1]):
        starts.append(at)
        at = at + ref[0, i]
        ends.append(at)
    return starts, ends


def seg_of(index, ends):
    found = jnp.zeros(index.shape, jnp.int32)
    for end in ends[:-1]:
        found = found + (index >= end).astype(jnp.int32)
    return found


def iota(shape, axis):
    return lax.broadcasted_iota(jnp.int32, shape, axis)


def split_pair(pair):
    low = iota(pair.shape, 1) < HEAD_DIM
    zero = jnp.zeros_like(pair)
    return jnp.concatenate([jnp.where(low, pair, zero), jnp.where(low, zero, pair)], axis=0)


def join_pair(both):
    rows = both.shape[0] // 2
    low = iota((rows, both.shape[1]), 1) < HEAD_DIM
    return jnp.where(low, both[:rows], both[rows:])


def fill_tiles(bias_ref, tiles, first, second):
    for h in range(LOCAL):
        rolled = pltpu.roll(
            jnp.broadcast_to(bias_ref[h : h + 1, :], (ROWS, 2 * ROWS)), 0, 1, stride=1, stride_axis=0
        )
        tiles[first, h] = rolled[:, :ROWS]
        tiles[second, h] = rolled[:, ROWS:]
        tiles[0, h] = jnp.broadcast_to(bias_ref[h : h + 1, 2 * ROWS - 1 :], (ROWS, ROWS))


def lanes_of(p):
    return pl.ds(pl.multiple_of(p * 128, 128), 128)


def each_pair(body):
    lax.fori_loop(0, PAIRS, lambda p, c: (body(p), c)[1], 0)


def rms_inverse(value):
    return lax.rsqrt(jnp.mean(value * value, axis=-1, keepdims=True) + EPS)


def attend(p, queries, keys, values, visit, extra, s_scr, mx_scr, l_scr, acc_scr, qs, o_ref, low_ref, lse_ref):
    qs[...] = split_pair(queries)
    mx_scr[...] = jnp.full_like(mx_scr, NEG)

    def scores(j):
        at = pl.multiple_of(j * ROWS, ROWS)
        raw = dot_nt(qs[...], keys(at))
        for i in range(2):
            rows = slice(i * ROWS, (i + 1) * ROWS)
            value = raw[rows] + extra(j, at, 2 * p + i)
            s_scr[rows, pl.ds(at, ROWS)] = value
            mx_scr[rows] = jnp.maximum(mx_scr[rows], value)

    visit(scores)
    peak = jnp.max(mx_scr[...], axis=1, keepdims=True)
    l_scr[...] = jnp.zeros_like(l_scr)
    acc_scr[...] = jnp.zeros_like(acc_scr)

    def weigh(j):
        at = pl.multiple_of(j * ROWS, ROWS)
        weights = jnp.exp(s_scr[:, pl.ds(at, ROWS)] - peak)
        l_scr[...] += weights
        acc_scr[...] += dot_nn(weights.astype(BF16), values(at))

    visit(weigh)
    total = jnp.sum(l_scr[...], axis=1, keepdims=True)
    result = join_pair(acc_scr[...] / total)
    o_ref[:, lanes_of(p)] = result
    low_ref[:, lanes_of(p)] = result.astype(BF16)
    both = peak + jnp.log(total)
    lane = iota((ROWS, 128), 1)
    lse = jnp.where(lane == 2 * p, both[:ROWS], lse_ref[...])
    lse_ref[...] = jnp.where(lane == 2 * p + 1, both[ROWS:], lse)


ATTEND = lambda n: [
    ((2 * ROWS, n), F32), ((2 * ROWS, ROWS), F32), ((2 * ROWS, ROWS), F32), ((2 * ROWS, 128), F32), ((2 * ROWS, 128), BF16),
]


def set_rows(target, parts, side):
    if len(parts) == 1:
        target[...] = parts[0][...]
        return
    rows = parts[0].shape[0]
    target[pl.ds(pl.multiple_of(side * rows, rows), rows), :] = parts[0][...]
    target[pl.ds(pl.multiple_of((1 - side) * rows, rows), rows), :] = parts[1][...]


def first_of(base, ends):
    first = jnp.int32(0)
    for end in ends[:-1]:
        first = jnp.where(base >= end, end, first)
    return first


def self_stage_kernel(n_parts, at_ref, len_ref, xe_ref, gain_ref, bias_ref, *refs):
    parts, refs = refs[:n_parts], refs[n_parts:]
    qkv_ref, w_ref, o_ref, low_ref, lse_ref, tiles, mask, s_scr, mx_scr, l_scr, acc_scr, qs = refs
    chip, side = at_ref[0], at_ref[2]
    set_rows(w_ref, parts, side)
    fill_tiles(bias_ref, tiles, 1, 2)
    width = w_ref.shape[0]
    step = 512

    def body(i, c):
        at = pl.multiple_of(i * step, step)
        wide = xe_ref[pl.ds(at, step), :width].astype(F32)
        value = (wide * rms_inverse(wide) * gain_ref[...]).astype(BF16)
        result = dot_nn(value, w_ref[...])
        for j in range(qkv_ref.shape[0]):
            qkv_ref[j, pl.ds(at, step), :] = result[:, 128 * j : 128 * j + 128].astype(BF16)
        return c

    lax.fori_loop(0, xe_ref.shape[0] // step, body, 0)

    starts, ends = spans(len_ref)
    base = pl.multiple_of(chip * ROWS, ROWS)
    j_min = first_of(base, ends) // ROWS
    q_row = base + iota((ROWS, 1), 0)
    q_seg = seg_of(q_row, ends)
    lse_ref[...] = jnp.zeros_like(lse_ref)

    def fill_mask(j, c):
        at = pl.multiple_of(j * ROWS, ROWS)
        k_row = at + iota((1, ROWS), 1)
        mask[:, pl.ds(at, ROWS)] = jnp.where((q_seg == seg_of(k_row, ends)) & (k_row <= q_row), 0.0, NEG)
        return c

    lax.fori_loop(j_min, chip + 1, fill_mask, 0)

    def visit(block):
        lax.fori_loop(j_min, chip + 1, lambda j, c: (block(j), c)[1], 0)

    def extra(j, at, h):
        return tiles[jnp.maximum(j - chip + 2, 0), h] + mask[:, pl.ds(at, ROWS)]

    each_pair(
        lambda p: attend(
            p, qkv_ref[p, pl.ds(base, ROWS), :],
            lambda at: qkv_ref[PAIRS + p, pl.ds(at, ROWS), :],
            lambda at: qkv_ref[2 * PAIRS + p, pl.ds(at, ROWS), :],
            visit, extra, s_scr, mx_scr, l_scr, acc_scr, qs, o_ref, low_ref, lse_ref,
        )
    )


def add_heads(low_ref, other_ref, w_ref, core):
    own = pl.ds(pl.multiple_of(core * HALF, HALF), HALF)
    other = pl.ds(pl.multiple_of((1 - core) * HALF, HALF), HALF)
    return dot_nn(low_ref[...], w_ref[own, :]) + dot_nn(other_ref[...], w_ref[other, :])


def cross_stage_kernel(n_parts, at_ref, len_ref, enc_ref, deal_ref, xe_ref, gain_ref, low_ref, other_ref, *refs):
    outs, mates, parts, refs = refs[:n_parts], refs[n_parts : 2 * n_parts], refs[2 * n_parts : 3 * n_parts], refs[3 * n_parts :]
    mid_ref, in_ref, q_ref, kv_ref, o_ref, low2_ref, lse_ref, so_ref, co_ref, wc_ref, refs = *refs[:10], refs[10:]
    mask, s_scr, mx_scr, l_scr, acc_scr, qs = refs
    chip, core, side = at_ref[0], at_ref[1], at_ref[2]
    set_rows(wc_ref, parts, side)
    for pieces, column in ((outs, core), (mates, 1 - core)):
        lanes = pl.ds(pl.multiple_of(column * HALF, 128), HALF)
        for i, piece in enumerate(pieces):
            rows = piece.shape[0]
            at = pl.multiple_of((side if i == 0 else 1 - side) * rows, rows) if n_parts > 1 else 0
            so_ref[pl.ds(at, rows), lanes] = piece[:, :HALF]
            co_ref[pl.ds(at, rows), lanes] = piece[:, HALF:]
    width = so_ref.shape[0]
    base = pl.multiple_of(chip * ROWS, ROWS)
    mid = xe_ref[pl.ds(base, ROWS), :width].astype(F32) + add_heads(low_ref, other_ref, so_ref, core)
    mid_ref[...] = mid
    normed = (mid * rms_inverse(mid) * gain_ref[...]).astype(BF16)
    in_ref[...] = normed
    q_ref[...] = dot_nn(normed, wc_ref[:, :HALF]).astype(BF16)
    step = 512

    def body(i, c):
        at = pl.multiple_of(i * step, step)
        result = dot_nn(xe_ref[pl.ds(at, step), width:], wc_ref[:, HALF:])
        for j in range(kv_ref.shape[0]):
            kv_ref[j, pl.ds(at, step), :] = result[:, 128 * j : 128 * j + 128].astype(BF16)
        return c

    lax.fori_loop(0, xe_ref.shape[0] // step, body, 0)
    wanted, q_pair, e_ends = cross_flags(chip, len_ref, enc_ref, deal_ref)
    lse_ref[...] = jnp.zeros_like(lse_ref)

    def visit(block):
        def body(j, c):
            @pl.when(wanted(j * ROWS))
            def _():
                block(j)

            return c

        lax.fori_loop(0, kv_ref.shape[1] // ROWS, body, 0)

    def fill_mask(j):
        at = pl.multiple_of(j * ROWS, ROWS)
        mask[:, pl.ds(at, ROWS)] = jnp.where(q_pair == seg_of(at + iota((1, ROWS), 1), e_ends), 0.0, NEG)

    visit(fill_mask)
    each_pair(
        lambda p: attend(
            p, q_ref[:, lanes_of(p)],
            lambda at: kv_ref[p, pl.ds(at, ROWS), :],
            lambda at: kv_ref[PAIRS + p, pl.ds(at, ROWS), :],
            visit, lambda j, at, h: mask[:, pl.ds(at, ROWS)],
            s_scr, mx_scr, l_scr, acc_scr, qs, o_ref, low2_ref, lse_ref,
        )
    )


def gelu_parts(value):
    tangent = jnp.tanh(GELU_C * (value + GELU_A * value * value * value))
    result = 0.5 * value * (1.0 + tangent)
    slope = 0.5 * (1.0 + tangent) + 0.5 * value * (1.0 - tangent * tangent) * GELU_C * (
        1.0 + 3.0 * GELU_A * value * value
    )
    return (result, slope)


def own_rows(core, rows):
    return pl.ds(pl.multiple_of(core * rows, rows), rows)


def ffn_stage_kernel(n_parts, at_ref, mid_ref, gain_ref, low_ref, other_ref, co_ref, cot_ref, mate_ref, *refs):
    inner, outer, refs = refs[:n_parts], refs[n_parts : 2 * n_parts], refs[2 * n_parts :]
    late_ref, in_ref, hid_ref, dpre_ref, cot_out, keep_ref, send_ref, e_ref, wi_ref, wo_ref, part_scr = refs
    core, side = at_ref[1], at_ref[2]
    rows = cot_ref.shape[0]
    set_rows(wi_ref, inner, side)
    set_rows(wo_ref, outer, side)
    cot_out[own_rows(core, rows), :] = cot_ref[...]
    cot_out[own_rows(1 - core, rows), :] = mate_ref[...]
    late = mid_ref[...] + add_heads(low_ref, other_ref, co_ref, core)
    late_ref[...] = late
    normed = (late * rms_inverse(late) * gain_ref[...]).astype(BF16)
    in_ref[...] = normed
    columns = 512

    def body(i, c):
        at = pl.multiple_of(i * columns, columns)
        activated, slope = gelu_parts(dot_nn(normed, wi_ref[:, pl.ds(at, columns)]))
        hid_ref[:, pl.ds(at, columns)] = activated.astype(BF16)
        grads = dot_nt(cot_out[...], wo_ref[pl.ds(at, columns), :])
        dpre_ref[:, pl.ds(at, columns)] = (grads * slope).astype(BF16)
        return c

    lax.fori_loop(0, wi_ref.shape[1] // columns, body, 0)
    e_ref[...] = dot_nt(dpre_ref[...], wi_ref[...])
    part_scr[...] = dot_nn(hid_ref[...], wo_ref[...])
    keep_ref[...] = part_scr[own_rows(core, rows), :] + late_ref[own_rows(core, rows), :]
    send_ref[...] = part_scr[own_rows(1 - core, rows), :]


def ffn_grads_kernel(n_sides, at_ref, hid_ref, cot_ref, in_ref, dpre_ref, *outs):
    side = at_ref[2]
    rows = in_ref.shape[1] // n_sides
    width = cot_ref.shape[1]
    if n_sides != 2:
        outs[0][...] = dot_tn(hid_ref[...], cot_ref[...])
        outs[1][...] = dot_tn(in_ref[...], dpre_ref[...])
        return
    keep_ref, send_ref = outs
    for owner in range(2):
        for mine, target in ((True, keep_ref), (False, send_ref)):

            @pl.when((side == owner) == mine)
            def _():
                for part in range(2):
                    units = slice((2 * owner + part) * rows, (2 * owner + part + 1) * rows)
                    block = dot_tn(hid_ref[:, units], cot_ref[...])
                    target[:, part * width : (part + 1) * width] = block.astype(target.dtype)
                block = dot_tn(in_ref[:, owner * rows : (owner + 1) * rows], dpre_ref[...])
                target[:, 2 * width :] = block.astype(target.dtype)


def norm_grad(value, gain, grad):
    inverse = rms_inverse(value)
    scaled = grad * gain
    cubed = inverse * inverse * inverse
    dvalue = inverse * scaled - value * cubed * jnp.mean(scaled * value, axis=-1, keepdims=True)
    return dvalue, jnp.sum(grad * value * inverse, axis=0, keepdims=True)


def cross_flags(chip, len_ref, enc_ref, deal_ref):
    starts, ends = spans(len_ref)
    e_starts, e_ends = spans(enc_ref)
    base = chip * ROWS
    ranges = []
    for i in range(len(ends)):
        live = (starts[i] < base + ROWS) & (ends[i] > base)
        low, high = jnp.int32(0), jnp.int32(0)
        for e in range(len(e_ends)):
            hit = deal_ref[0, i] == e
            low = jnp.where(hit, e_starts[e], low)
            high = jnp.where(hit, e_ends[e], high)
        ranges.append((live, low, high))

    def wanted(at):
        found = jnp.bool_(False)
        for live, low, high in ranges:
            found = found | (live & (low < at + ROWS) & (high > at))
        return found

    q_seg = seg_of(base + iota((ROWS, 1), 0), ends)
    q_pair = jnp.zeros((ROWS, 1), jnp.int32)
    for i in range(len(ends)):
        q_pair = q_pair + jnp.where(q_seg == i, deal_ref[0, i], 0)
    return wanted, q_pair, e_ends


def row_stats(go_ref, o_ref, lse_ref, gs, lse_scr, delta_scr, stat_scr):
    lane = iota((ROWS, 128), 1)
    low = lane < HEAD_DIM
    stat_scr[...] = lse_ref[...]

    def pair(p):
        grads = go_ref[:, lanes_of(p)]
        gs[p] = split_pair(grads)
        product = grads.astype(F32) * o_ref[:, lanes_of(p)]
        for i in range(2):
            part = jnp.where(low if i == 0 else ~low, product, 0.0)
            delta = jnp.sum(part, axis=1, keepdims=True)
            rows = slice(i * ROWS, (i + 1) * ROWS)
            delta_scr[p, rows] = jnp.broadcast_to(delta, (ROWS, 128))
            lse_scr[p, rows] = jnp.broadcast_to(
                jnp.sum(jnp.where(lane == 2 * p + i, lse_ref[...], 0.0), axis=1, keepdims=True), (ROWS, 128)
            )
            stat_scr[...] = jnp.where(lane == 8 + 2 * p + i, delta, stat_scr[...])

    each_pair(pair)


def self_query_grad_kernel(
    at_ref, len_ref, bias_ref, qkv_ref, go_ref, o_ref, lse_ref, dq_ref, dist_ref,
    tiles, qs, gs, lse_scr, delta_scr, dq_scr, ds_scr, stat_scr,
):
    chip = at_ref[0]
    starts, ends = spans(len_ref)
    base = pl.multiple_of(chip * ROWS, ROWS)
    first = first_of(base, ends)
    fill_tiles(bias_ref, tiles, 1, 2)
    row_stats(go_ref, o_ref, lse_ref, gs, lse_scr, delta_scr, stat_scr)

    def start(p):
        qs[p] = split_pair(qkv_ref[p, pl.ds(base, ROWS), :])

    each_pair(start)
    dq_scr[...] = jnp.zeros_like(dq_scr)
    ds_scr[...] = jnp.zeros_like(ds_scr)
    q_row = base + iota((ROWS, 1), 0)
    q_seg = seg_of(q_row, ends)

    def block(j, _):
        at = pl.multiple_of(j * ROWS, ROWS)
        k_row = at + iota((1, ROWS), 1)
        allowed = (q_seg == seg_of(k_row, ends)) & (k_row <= q_row)
        masked = jnp.where(allowed, 0.0, NEG)
        tile = jnp.maximum(j - chip + 2, 0)

        def pair(p):
            keys = qkv_ref[PAIRS + p, pl.ds(at, ROWS), :]
            raw = dot_nt(qs[p], keys)
            dprobs = dot_nt(gs[p], qkv_ref[2 * PAIRS + p, pl.ds(at, ROWS), :])
            grads = []
            for i in range(2):
                rows = slice(i * ROWS, (i + 1) * ROWS)
                value = raw[rows] + (tiles[tile, 2 * p + i] + masked)
                probs = jnp.exp(value - lse_scr[p, rows, :1])
                ds = (probs * (dprobs[rows] - delta_scr[p, rows, :1])).astype(BF16)
                ds_scr[tile, 2 * p + i] += ds.astype(F32)
                grads.append(ds)
            dq_scr[p] += dot_nn(jnp.concatenate(grads, axis=0), keys)

        each_pair(pair)
        return 0

    lax.fori_loop(first // ROWS, chip + 1, block, 0)
    dist_ref[...] = jnp.zeros_like(dist_ref)
    lanes = iota((1, 2 * ROWS), 1)
    for p in range(PAIRS):
        dq_ref[:, 128 * p : 128 * p + 128] = join_pair(dq_scr[p]).astype(BF16)

    def fold(h, c):
        folded = jnp.concatenate([ds_scr[1, h], ds_scr[2, h]], axis=1)
        rows = ROWS
        while rows > 1:
            rows //= 2
            folded = folded[:rows] + pltpu.roll(folded[rows:], 2 * ROWS - rows, 1)
        far = jnp.sum(jnp.sum(ds_scr[0, h], axis=0, keepdims=True), axis=1, keepdims=True)
        dist_ref[pl.ds(h, 1), :] = folded + jnp.where(lanes == 2 * ROWS - 1, far, 0.0)
        return c

    lax.fori_loop(0, LOCAL, fold, 0)


def self_key_stage_kernel(
    at_ref, len_ref, bias_ref, qkv_ref, message_ref, so_ref, dq_ref, w_ref, x_ref, gain_ref, ckv_ref, small_ref,
    grads_ref, keep_ref, send_ref,
    go_ref, stat_ref, tiles, ks, vs, dk_scr, dv_scr, dqkv_scr, h_scr, e_scr,
):
    chip, core = at_ref[0], at_ref[1]
    starts, ends = spans(len_ref)
    base = pl.multiple_of(chip * ROWS, ROWS)
    last = ends[-1]
    for end in reversed(ends[:-1]):
        last = jnp.where(base + ROWS - 1 < end, end, last)
    stop = (last - 1) // ROWS + 1
    fill_tiles(bias_ref, tiles, 2, 1)
    heads = own_rows(core, HALF)
    half = ROWS // 2

    def receive(i, c):
        both = [message_ref[2 * i + e, :half, :] for e in range(2)]
        result = dot_nt(jnp.concatenate(both, axis=0), so_ref[heads, :])
        for p in range(PAIRS):
            go_ref[p, pl.ds(pl.multiple_of(i * ROWS, ROWS), ROWS), :] = result[:, 128 * p : 128 * p + 128].astype(BF16)
        parts = message_ref[2 * i + core, half:, :].astype(F32)
        stat_ref[i] = parts[:, :ROWS] + parts[:, ROWS : 2 * ROWS] + parts[:, 2 * ROWS :]
        return c

    lax.fori_loop(chip, stop, receive, 0)

    def start(p):
        ks[p] = split_pair(qkv_ref[PAIRS + p, pl.ds(base, ROWS), :])
        vs[p] = split_pair(qkv_ref[2 * PAIRS + p, pl.ds(base, ROWS), :])

    each_pair(start)
    dk_scr[...] = jnp.zeros_like(dk_scr)
    dv_scr[...] = jnp.zeros_like(dv_scr)
    k_row = base + iota((ROWS, 1), 0)
    k_seg = seg_of(k_row, ends)

    def block(i, _):
        at = pl.multiple_of(i * ROWS, ROWS)
        q_row = at + iota((1, ROWS), 1)
        allowed = (k_seg == seg_of(q_row, ends)) & (k_row <= q_row)
        masked = jnp.where(allowed, 0.0, NEG)
        tile = jnp.maximum(2 - (i - chip), 0)

        def pair(p):
            queries = qkv_ref[p, pl.ds(at, ROWS), :]
            grads = go_ref[p, pl.ds(at, ROWS), :]
            raw = dot_nt(ks[p], queries)
            dprobs = dot_nt(vs[p], grads)
            weights, dscores = [], []
            for e in range(2):
                rows = slice(e * ROWS, (e + 1) * ROWS)
                h = 2 * p + e
                value = raw[rows] + (tiles[tile, h] + masked)
                probs = jnp.exp(value - stat_ref[i, pl.ds(h, 1), :])
                weights.append(probs.astype(BF16))
                dscores.append((probs * (dprobs[rows] - stat_ref[i, pl.ds(8 + h, 1), :])).astype(BF16))
            dv_scr[p] += dot_nn(jnp.concatenate(weights, axis=0), grads)
            dk_scr[p] += dot_nn(jnp.concatenate(dscores, axis=0), queries)

        each_pair(pair)
        return 0

    lax.fori_loop(chip, stop, block, 0)
    dqkv_scr[:, :HALF] = dq_ref[...]
    for p in range(PAIRS):
        dqkv_scr[:, HALF + 128 * p : HALF + 128 * p + 128] = join_pair(dk_scr[p]).astype(BF16)
        dqkv_scr[:, 2 * HALF + 128 * p : 2 * HALF + 128 * p + 128] = join_pair(dv_scr[p]).astype(BF16)
    e_scr[...] = dot_nt(dqkv_scr[...], w_ref[...])
    keep_ref[...] = e_scr[own_rows(core, half), :]
    send_ref[...] = e_scr[own_rows(1 - core, half), :]
    wide = x_ref[...].astype(F32)
    scaled = wide * rms_inverse(wide)
    h_scr[...] = (scaled * gain_ref[...]).astype(BF16)
    dgain = jnp.sum(e_scr[...] * scaled, axis=0, keepdims=True)
    dgain = jnp.transpose(jnp.where(iota((128, dgain.shape[1]), 0) == 0, dgain, 0.0))
    columns = grads_ref.shape[1]
    grads_ref[:, columns - 128 :] = (small_ref[...] + dgain).astype(BF16)
    grads_ref[:, 3 * HALF : columns - 128] = ckv_ref[...]
    step = 256
    for i in range(0, h_scr.shape[1], step):
        grads_ref[i : i + step, : 3 * HALF] = dot_tn(h_scr[:, i : i + step], dqkv_scr[...]).astype(BF16)


def cross_grad_stage_kernel(
    at_ref, len_ref, enc_ref, deal_ref,
    e_ref, other_ref, late_ref, gain_ref, cot_ref, co_ref, q_ref, o_ref, lse_ref, kv_ref, wc_ref,
    grad_ref, low_ref, dgain_ref, dq_ref, dkv_ref, part_ref,
    go_ref, qs, gs, lse_scr, delta_scr, dq_scr, stat_scr,
):
    chip, core = at_ref[0], at_ref[1]
    dvalue, dgain = norm_grad(late_ref[...], gain_ref[...], e_ref[...] + other_ref[...])
    dgain_ref[...] = dgain
    grad = cot_ref[...].astype(F32) + dvalue
    grad_ref[...] = grad
    low_ref[...] = grad.astype(BF16)
    go_ref[...] = dot_nt(low_ref[...], co_ref[own_rows(core, HALF), :]).astype(BF16)
    wanted, q_pair, e_ends = cross_flags(chip, len_ref, enc_ref, deal_ref)
    row_stats(go_ref, o_ref, lse_ref, gs, lse_scr, delta_scr, stat_scr)

    def start(p):
        qs[p] = split_pair(q_ref[:, lanes_of(p)])

    each_pair(start)
    dq_scr[...] = jnp.zeros_like(dq_scr)

    def block(j, c):
        at = pl.multiple_of(j * ROWS, ROWS)
        hit = wanted(at)

        @pl.when(hit)
        def _():
            k_row = at + iota((1, ROWS), 1)
            masked = jnp.where(q_pair == seg_of(k_row, e_ends), 0.0, NEG)

            def pair(p):
                keys = kv_ref[p, pl.ds(at, ROWS), :]
                raw = dot_nt(qs[p], keys)
                dprobs = dot_nt(gs[p], kv_ref[PAIRS + p, pl.ds(at, ROWS), :])
                weights, dscores = [], []
                for i in range(2):
                    rows = slice(i * ROWS, (i + 1) * ROWS)
                    probs = jnp.exp(raw[rows] + masked - lse_scr[p, rows, :1])
                    weights.append(probs.astype(BF16))
                    dscores.append((probs * (dprobs[rows] - delta_scr[p, rows, :1])).astype(BF16))
                ds = jnp.concatenate(dscores, axis=0)
                dq_scr[p] += dot_nn(ds, keys)
                dkv_ref[pl.ds(at, ROWS), lanes_of(p)] = dot_tn(ds, qs[p]).astype(BF16)
                dkv_ref[pl.ds(at, ROWS), lanes_of(PAIRS + p)] = dot_tn(jnp.concatenate(weights, axis=0), gs[p]).astype(BF16)

            each_pair(pair)

        @pl.when(jnp.logical_not(hit))
        def _():
            dkv_ref[pl.ds(at, ROWS), :] = jnp.zeros((ROWS, 2 * HALF), BF16)

        return c

    lax.fori_loop(0, kv_ref.shape[1] // ROWS, block, 0)
    for p in range(PAIRS):
        dq_ref[:, 128 * p : 128 * p + 128] = join_pair(dq_scr[p]).astype(BF16)
    part_ref[...] = dot_nt(dq_ref[...], wc_ref[:, :HALF])


def self_grad_start_kernel(
    at_ref, e_ref, other_ref, mid_ref, gain_ref, late_grad_ref, so_ref, o_ref, lse_ref,
    grad_ref, low_ref, dgain_ref, go_ref, message_ref,
    stat_scr,
):
    core = at_ref[1]
    dvalue, dgain = norm_grad(mid_ref[...], gain_ref[...], e_ref[...] + other_ref[...])
    dgain_ref[...] = dgain
    grad = late_grad_ref[...] + dvalue
    grad_ref[...] = grad
    low_ref[...] = grad.astype(BF16)
    go_ref[...] = dot_nt(low_ref[...], so_ref[own_rows(core, HALF), :]).astype(BF16)
    half = ROWS // 2
    message_ref[:half, :] = low_ref[own_rows(core, half), :]
    lane = iota((ROWS, 128), 1)
    stat_scr[...] = lse_ref[...]

    def pair(p):
        product = go_ref[:, lanes_of(p)].astype(F32) * o_ref[:, lanes_of(p)]
        for i in range(2):
            part = jnp.where((lane < HEAD_DIM) if i == 0 else (lane >= HEAD_DIM), product, 0.0)
            stat_scr[...] = jnp.where(lane == 8 + 2 * p + i, jnp.sum(part, axis=1, keepdims=True), stat_scr[...])

    each_pair(pair)
    rest = jnp.transpose(stat_scr[...])[:16]
    for part in range(3):
        high = rest.astype(BF16)
        message_ref[half:, part * ROWS : (part + 1) * ROWS] = high
        rest = rest - high.astype(F32)


def projection_grads_kernel(at_ref, low2_ref, other2_ref, b2_ref, in_ref, dq_ref, low1_ref, other1_ref, b1_ref, out_ref):
    core = at_ref[1]
    lanes = pl.ds(pl.multiple_of(core * HALF, 128), HALF)
    for at, own, other, grad in ((0, low2_ref, other2_ref, b2_ref), (2 * HALF, low1_ref, other1_ref, b1_ref)):
        grads = grad[:, lanes]
        for side, part in ((core, own), (1 - core, other)):
            out_ref[own_rows(side, HALF), at : at + HALF] = dot_tn(part[...], grads).astype(BF16)
    out_ref[:, HALF : 2 * HALF] = dot_tn(in_ref[...], dq_ref[...]).astype(BF16)


def encoder_grads_kernel(at_ref, dkv_ref, e_ref, wc_ref, grads_ref, keep_ref, send_ref, low_scr, e_scr):
    core = at_ref[1]
    half = ROWS // 2
    low_scr[...] = dkv_ref[...].astype(BF16)
    e_scr[...] = dot_nt(low_scr[...], wc_ref[:, HALF:])
    keep_ref[...] = e_scr[own_rows(core, half), :]
    send_ref[...] = e_scr[own_rows(1 - core, half), :]
    grads_ref[...] = dot_tn(e_ref[...], low_scr[...]).astype(BF16)


def token_grads_kernel(at_ref, e_ref, other_ref, x_ref, gain_ref, grad_ref, out_ref):
    dvalue, _ = norm_grad(x_ref[...].astype(F32), gain_ref[...], e_ref[...] + other_ref[...])
    out_ref[...] = grad_ref[own_rows(at_ref[1], out_ref.shape[0]), :] + dvalue


def finish_columns_kernel(at_ref, own_ref, other_ref, *outs):
    core = at_ref[1]
    for i, out in enumerate(outs):
        columns = slice(i * HALF, (i + 1) * HALF)
        out[:, pl.ds(pl.multiple_of(core * HALF, 128), HALF)] = own_ref[:, columns].astype(F32)
        out[:, pl.ds(pl.multiple_of((1 - core) * HALF, 128), HALF)] = other_ref[:, columns].astype(F32)


def finish_ffn_kernel(order, parts_ref, outer_ref, inner_ref):
    rows = parts_ref.shape[1]
    side = inner_ref.shape[0]
    width = outer_ref.shape[1]
    unit = inner_ref.shape[1] // 4
    for i, (core, place) in enumerate(order):
        at = place * rows
        for half in range(2):
            top = (2 * core + half) * side + at
            outer_ref[top : top + rows, :] = parts_ref[i, :, half * width : (half + 1) * width].astype(F32)
            lanes = slice((2 * half + core) * unit, (2 * half + core + 1) * unit)
            inner_ref[at : at + rows, lanes] = parts_ref[i, :, 2 * width + half * unit : 2 * width + (half + 1) * unit].astype(F32)


def finish_gathered_kernel(order, parts_ref, *outs):
    rows = parts_ref.shape[1]
    for i, (core, place) in enumerate(order):
        for j, out in enumerate(outs):
            out[place * rows : (place + 1) * rows, core * HALF : (core + 1) * HALF] = parts_ref[
                i, :, j * HALF : (j + 1) * HALF
            ].astype(F32)


def pack_kernel(groups, core_ref, *refs):
    count = sum(groups)
    ins, outs = list(refs[:count]), refs[count:]
    for size, out in zip(groups, outs):
        at = 0
        for _ in range(size):
            part = ins.pop(0)
            out[:, at : at + part.shape[1]] = part[...].astype(BF16)
            at += part.shape[1]


SMEM = pl.BlockSpec(memory_space=pltpu.SMEM)
VMEM = pl.BlockSpec(memory_space=pltpu.VMEM)


def call(kernel, scalars, arrays, outs, scratch, flops):
    moved = sum(a.size * a.dtype.itemsize for a in arrays) + sum(math.prod(s) * jnp.dtype(d).itemsize for s, d in outs)
    return pl.pallas_call(
        kernel,
        out_shape=[jax.ShapeDtypeStruct(s, d) for s, d in outs],
        in_specs=[SMEM] * len(scalars) + [VMEM] * len(arrays),
        out_specs=[VMEM] * len(outs),
        scratch_shapes=[pltpu.VMEM(s, d) for s, d in scratch],
        compiler_params=pltpu.CompilerParams(vmem_limit_bytes=VMEM_LIMIT),
        cost_estimate=pl.CostEstimate(flops=flops, transcendentals=0, bytes_accessed=moved),
    )(*scalars, *arrays)


TILES = ((3, LOCAL, ROWS, ROWS), F32)
STACK = ((PAIRS, 2 * ROWS, 128), BF16)
COLUMN = ((PAIRS, 2 * ROWS, 128), F32)
LANE = ((ROWS, 128), F32)


def pack(core, groups):
    flat = [item for group in groups for item in group]
    return pl.pallas_call(
        functools.partial(pack_kernel, [len(g) for g in groups]),
        grid_spec=pltpu.PrefetchScalarGridSpec(
            num_scalar_prefetch=1,
            grid=(1,),
            in_specs=[
                pl.BlockSpec(shape, functools.partial(lambda index, i, c: index(c[0]), index)) for _, shape, index in flat
            ],
            out_specs=[
                pl.BlockSpec((g[0][1][0], sum(s[1] for _, s, _ in g)), lambda i, c: (0, 0)) for g in groups
            ],
        ),
        out_shape=[jax.ShapeDtypeStruct((g[0][1][0], sum(s[1] for _, s, _ in g)), BF16) for g in groups],
        compiler_params=pltpu.CompilerParams(vmem_limit_bytes=VMEM_LIMIT),
    )(core, *(w for w, _, _ in flat))


def swap_core(value):
    return lax.ppermute(value, "core", [(0, 1), (1, 0)])


def gather_fsdp(own):
    count = lax.axis_size("fsdp")
    if count != 2:
        return [lax.all_gather(own, "fsdp", axis=0, tiled=True)]
    return [own, lax.ppermute(own, "fsdp", [(0, 1), (1, 0)])]


CHIPS = ("z", "y")
GROUP = ("z", "y", "core")


def gather_rows(own):
    return lax.all_gather(own, GROUP, axis=0, tiled=True)


def bits_of(axis):
    return range((lax.axis_size(axis) - 1).bit_length())


def swap_bit(value, axis, bit):
    return lax.ppermute(value, axis, [(i, i ^ (1 << bit)) for i in range(lax.axis_size(axis))])


def halve(value, axis, bit):
    side = (lax.axis_index(axis) >> bit) & 1
    keep = lax.dynamic_index_in_dim(value, side, 0, keepdims=False).astype(F32)
    send = lax.dynamic_index_in_dim(value, 1 - side, 0, keepdims=False).astype(BF16)
    return keep + swap_bit(send, axis, bit).astype(F32)


def steps_of(*axes):
    return [(axis, bit) for axis in axes for bit in bits_of(axis)]


def scatter(value, steps):
    for axis, bit in steps:
        value = halve(value.reshape((2, value.shape[0] // 2) + value.shape[1:]), axis, bit)
    return value


def scatter_fsdp(terms):
    return scatter(terms, [("fsdp", bit) for bit in reversed(bits_of("fsdp"))])


def scatter_chips(value):
    nz, ny = lax.axis_size("z"), lax.axis_size("y")
    value = value.reshape((nz, ny, value.shape[0] // (nz * ny)) + value.shape[1:])
    value = jnp.swapaxes(value, 0, 1)
    value = value.reshape((nz * ny,) + value.shape[2:])
    steps = [(axis, bit) for axis in ("y", "z") for bit in reversed(bits_of(axis))]
    return scatter(value, steps)[0]


def after(value, *earlier):
    return lax.optimization_barrier((value, *earlier))[0]


def on_device(
    tokens, encoded, cotangent, tgt_lengths, enc_lengths, deal,
    ln_self, ln_cross, ln_ffn, bias_table,
    self_query, self_key, self_value, self_output,
    cross_query, cross_key, cross_value, cross_output,
    ffn_inner, ffn_outer,
):
    core = lax.axis_index("core")
    fsdp = lax.axis_index("fsdp")
    n_fsdp = lax.axis_size("fsdp")
    chip = lax.axis_index(CHIPS)
    at = jnp.stack([chip, core, fsdp]).astype(jnp.int32)
    core_ref = core.reshape(1).astype(jnp.int32)
    rows, width = tokens.shape
    n = 2 * rows * lax.axis_size(CHIPS)
    side = width // n_fsdp
    hidden_half = ffn_inner.shape[1] // 2
    unit = hidden_half // n_fsdp
    wide, flat = ((ROWS, width), F32), ((ROWS, width), BF16)

    def column(weight):
        return (weight, (side, HALF), lambda c: (0, c))

    (qkv_own,) = pack(core_ref, [[column(w) for w in (self_query, self_key, self_value)]])
    w_qkv = gather_fsdp(qkv_own)
    if unit % 128 == 0:
        inner_items = [(ffn_inner, (side, unit), functools.partial(lambda o, c: (0, 2 * o + c), o)) for o in range(n_fsdp)]
    else:
        inner_units = ffn_inner.reshape(side, n_fsdp, 2, unit)
        inner_units = lax.dynamic_index_in_dim(inner_units, core, 2, keepdims=False).reshape(side, hidden_half)
        inner_items = [(inner_units, (side, hidden_half), lambda c: (0, 0))]
    out_own, cross_own, inner_own, outer_own = pack(
        core_ref,
        [
            [column(w) for w in (self_output, cross_output)],
            [column(w) for w in (cross_query, cross_key, cross_value)],
            inner_items,
            [(ffn_outer, (unit, width), lambda c: (c, 0))],
        ],
    )
    w_out = gather_fsdp(out_own)
    w_cross = gather_fsdp(cross_own)
    inner_own, outer_own = after((inner_own, outer_own), w_cross[-1])
    w_inner, w_outer = gather_fsdp(inner_own), gather_fsdp(outer_own)
    w_out_mate = [swap_core(w) for w in w_out]
    cot_mate = swap_core(cotangent)

    small = jnp.concatenate([ln_self, ln_cross, ln_ffn, bias_table.reshape(-1)], axis=0).astype(BF16)[None]
    small = gather_fsdp(small)
    if len(small) == 2:
        small = jnp.where(fsdp == 0, jnp.concatenate(small, axis=0), jnp.concatenate(small[::-1], axis=0))
    else:
        small = small[0]
    gain_self, gain_cross, gain_ffn = (
        small[:, i * side : (i + 1) * side].reshape(1, width).astype(F32) for i in range(3)
    )
    table = small[:, 3 * side :].reshape(BUCKETS, HEADS)
    table = lax.dynamic_slice_in_dim(table, core * LOCAL, LOCAL, 1).astype(F32)
    onehots = np.concatenate([QK_ONEHOT, KQ_ONEHOT], axis=0)
    biases = jnp.einsum("bh,tb->ht", table, onehots, precision=lax.Precision.HIGHEST)
    biases = jnp.pad(biases, ((0, 2), (0, 0)))
    bias_qk, bias_kq = biases[:, : 2 * ROWS], biases[:, 2 * ROWS :]

    xe = gather_rows(jnp.concatenate([tokens, encoded], axis=1))
    qkv, w_qkv, attn_self, low_self, lse_self = call(
        functools.partial(self_stage_kernel, len(w_qkv)), (at, tgt_lengths), (xe, gain_self, bias_qk, *w_qkv),
        [((3 * PAIRS, n, 128), BF16), ((width, 3 * HALF), BF16), ((ROWS, HALF), F32), ((ROWS, HALF), BF16), LANE],
        [TILES, ((ROWS, n), F32), *ATTEND(n)],
        2 * n * width * 3 * HALF + 4 * ROWS * n * HALF,
    )
    low_self_other = swap_core(low_self)

    x_mid, in_cross, q_cross, kv_cross, attn_cross, low_cross, lse_cross, w_so, w_co, w_cross = call(
        functools.partial(cross_stage_kernel, len(w_out)), (at, tgt_lengths, enc_lengths, deal),
        (xe, gain_cross, low_self, low_self_other, *w_out, *w_out_mate, *w_cross),
        [
            wide, flat, ((ROWS, HALF), BF16), ((2 * PAIRS, n, 128), BF16), ((ROWS, HALF), F32), ((ROWS, HALF), BF16), LANE,
            ((width, width), BF16), ((width, width), BF16), ((width, 3 * HALF), BF16),
        ],
        [((ROWS, n), F32), *ATTEND(n)],
        2 * n * width * 2 * HALF + 4 * ROWS * n * HALF,
    )
    low_cross_other = swap_core(low_cross)

    half_rows = ((rows, width), F32)
    x_late, in_ffn, hidden, d_pre, cot, out_keep, out_send, e_ffn = call(
        functools.partial(ffn_stage_kernel, len(w_inner)), (at,),
        (x_mid, gain_ffn, low_cross, low_cross_other, w_co, cotangent, cot_mate, *w_inner, *w_outer),
        [wide, flat, ((ROWS, hidden_half), BF16), ((ROWS, hidden_half), BF16), flat, half_rows, half_rows, wide],
        [((width, hidden_half), BF16), ((hidden_half, width), BF16), wide],
        8 * ROWS * width * hidden_half,
    )
    e_ffn_other = swap_core(e_ffn)
    ffn_out = (
        [((side, 4 * width), F32), ((side, 4 * width), BF16)]
        if n_fsdp == 2
        else [((hidden_half, width), F32), ((width, hidden_half), F32)]
    )
    first = call(
        functools.partial(ffn_grads_kernel, n_fsdp), (at,), (hidden, cot, in_ffn, d_pre), ffn_out, [],
        4 * ROWS * width * hidden_half,
    )
    if n_fsdp == 2:
        first_other = lax.ppermute(first[1], "fsdp", [(0, 1), (1, 0)])
        e_ffn = after(e_ffn, first[1])
    output = out_keep + swap_core(out_send)

    grad_late, late_low, d_gain_ffn, dq_cross, dkv_part, e_cross = call(
        cross_grad_stage_kernel, (at, tgt_lengths, enc_lengths, deal),
        (e_ffn, e_ffn_other, x_late, gain_ffn, cot, w_co, q_cross, attn_cross, lse_cross, kv_cross, w_cross),
        [wide, flat, ((1, width), F32), ((ROWS, HALF), BF16), ((n, 2 * HALF), BF16), wide],
        [((ROWS, HALF), BF16), STACK, STACK, COLUMN, COLUMN, COLUMN, LANE],
        10 * ROWS * n * HALF,
    )
    e_cross_other = swap_core(e_cross)

    grad_mid, mid_low, d_gain_cross, go_self, message = call(
        self_grad_start_kernel, (at,), (e_cross, e_cross_other, x_mid, gain_cross, grad_late, w_so, attn_self, lse_self),
        [wide, flat, ((1, width), F32), ((ROWS, HALF), BF16), ((rows + 16, width), BF16)], [LANE],
        2 * ROWS * width * HALF,
    )
    message = lax.all_gather(message, GROUP, axis=0)
    (second,) = call(
        projection_grads_kernel, (at,),
        (low_cross, low_cross_other, late_low, in_cross, dq_cross, low_self, low_self_other, mid_low),
        [((width, 3 * HALF), BF16)], [], 6 * ROWS * width * HALF,
    )
    dq_self, dist = call(
        self_query_grad_kernel, (at, tgt_lengths), (bias_qk, qkv, after(go_self, second), attn_self, lse_self),
        [((ROWS, HALF), BF16), ((8, 2 * ROWS), F32)],
        [TILES, STACK, STACK, COLUMN, COLUMN, COLUMN, TILES, LANE],
        6 * ROWS * n * HALF,
    )
    x_chip = lax.dynamic_slice(xe, (chip * ROWS, 0), (ROWS, width))
    e_chip = lax.dynamic_slice(xe, (chip * ROWS, width), (ROWS, width))
    d_table = jnp.einsum("ht,tb->bh", dist[:LOCAL], QK_ONEHOT, precision=lax.Precision.HIGHEST)
    d_table = jnp.zeros((BUCKETS, 2, LOCAL), F32).at[:, core].set(d_table).reshape(n_fsdp, -1, HEADS)
    d_table = jnp.pad(d_table, ((0, 0), (0, side - d_table.shape[1]), (0, 0))).reshape(width, HEADS)
    none = jnp.zeros((width, 1), F32)
    small = [none, 0.5 * d_gain_cross.reshape(width, 1), 0.5 * d_gain_ffn.reshape(width, 1), d_table]
    small = jnp.pad(jnp.concatenate(small, axis=1), ((0, 0), (0, 128 - 3 - HEADS)))

    dkv_cross = scatter_chips(dkv_part)
    d_ckv, enc_keep, enc_send = call(
        encoder_grads_kernel, (at,), (dkv_cross, e_chip, w_cross),
        [((width, 2 * HALF), BF16), half_rows, half_rows], [((ROWS, 2 * HALF), BF16), wide],
        8 * ROWS * width * HALF,
    )
    enc_grad = enc_keep + swap_core(enc_send)

    steps = steps_of("y", "z")
    if n_fsdp == 2:
        first = first[0] + first_other.astype(F32)
    else:
        outer = first[0].reshape(n_fsdp, 2, side, width)
        first = jnp.concatenate([outer[:, 0], outer[:, 1], first[1].reshape(n_fsdp, side, hidden_half)], axis=2)
        first = scatter_fsdp(first)[0]
    second = scatter_fsdp(after(second, first).reshape(n_fsdp, side, -1))[0]
    first = scatter(first, steps[:1])
    second = scatter(second, steps[:1])

    d_qkv, e_keep, e_send = call(
        self_key_stage_kernel, (at, tgt_lengths),
        (bias_kq, qkv, after(message, dq_self), w_so, dq_self, w_qkv, x_chip, gain_self, d_ckv, small),
        [((width, 5 * HALF + 128), BF16), half_rows, half_rows],
        [
            ((PAIRS, n, 128), BF16), ((n // ROWS, 16, ROWS), F32), TILES, STACK, STACK, COLUMN, COLUMN,
            ((ROWS, 3 * HALF), BF16), flat, wide,
        ],
        8 * ROWS * n * HALF,
    )
    (grad_tokens,) = call(
        token_grads_kernel, (at,), (e_keep, swap_core(e_send), tokens, gain_self, grad_mid),
        [half_rows], [], 10 * rows * width,
    )

    def reduced(joined):
        count = n_fsdp * lax.axis_size(CHIPS)
        joined = joined.reshape(count, -1, joined.shape[1])
        terms = lax.all_to_all(joined, ("fsdp",) + CHIPS, 0, 0, tiled=True)
        total = jnp.sum(terms.astype(F32), axis=0).astype(BF16)
        copies = jnp.broadcast_to(total[None], (lax.axis_size(CHIPS),) + total.shape)
        own = lax.all_to_all(copies, CHIPS, 0, 0, tiled=True).reshape(-1, joined.shape[2])
        return own, swap_core(own)

    third = reduced(d_qkv)
    first = scatter(first, steps[1:]).astype(BF16)
    second = scatter(second, steps[1:]).astype(BF16)
    first = lax.all_gather(first, GROUP, axis=0)
    second = lax.all_gather(second, GROUP, axis=0)

    nz, ny = lax.axis_size("z"), lax.axis_size("y")
    order = []
    for z in range(nz):
        for y in range(ny):
            place = 0
            for axis, bit in steps:
                place = 2 * place + (((z if axis == "z" else y) >> bit) & 1)
            order += [(0, place), (1, place)]
    matrix = ((side, width), F32)
    g_co, g_cq, g_so = call(
        functools.partial(finish_gathered_kernel, order), (), (second,), [matrix] * 3, [], 6 * side * width
    )
    g_sq, g_sk, g_sv, g_ck, g_cv = call(finish_columns_kernel, (at,), third, [matrix] * 5, [], 10 * side * width)
    if n_fsdp == 2:
        g_outer, g_inner = call(
            functools.partial(finish_ffn_kernel, order), (), (first,),
            [(ffn_outer.shape, F32), (ffn_inner.shape, F32)], [], 8 * side * width,
        )
    else:
        places = np.argsort([2 * place + c for c, place in order])
        first = first[places].reshape(nz * ny, 2, -1, first.shape[2])
        pair = jnp.swapaxes(first, 0, 1).reshape(2, side, -1).astype(F32)
        g_outer = pair[:, :, : 2 * width].reshape(2, side, 2, width)
        g_outer = jnp.swapaxes(g_outer, 1, 2).reshape(ffn_outer.shape)
        g_inner = jnp.transpose(pair[:, :, 2 * width :].reshape(2, side, n_fsdp, unit), (1, 2, 0, 3))
        g_inner = g_inner.reshape(ffn_inner.shape)
    vectors = third[0][:, -128:].astype(F32) + third[1][:, -128:].astype(F32)

    return (
        output, grad_tokens, enc_grad,
        vectors[:, 0], vectors[:, 1], vectors[:, 2], vectors[: bias_table.shape[0], 3 : 3 + HEADS],
        g_sq, g_sk, g_sv, g_so, g_cq, g_ck, g_cv, g_co, g_inner, g_outer,
    )


def solution(mesh):
    n_ctx, n_fsdp = mesh.shape["ctx"], mesh.shape["fsdp"]
    n_z = 4
    grid = Mesh(mesh.devices.reshape(n_z, n_ctx // (2 * n_z), 2, n_fsdp), ("z", "y", "core", "fsdp"))
    by_rows = P(("fsdp", "z", "y", "core"), None)
    split = P("fsdp", None)
    vector = P("fsdp")
    in_specs = (by_rows,) * 3 + (split,) * 3 + (vector,) * 3 + (split,) * 11
    out_specs = (by_rows,) * 3 + (vector,) * 3 + (split,) * 11
    return jax.shard_map(on_device, mesh=grid, in_specs=in_specs, out_specs=out_specs, check_vma=False)
```

time: 733 us -> 501 us (0.68); the launches traced: 719 us -> 501 us
  Pallas kernels: 55.6 us -> 126 us
  other arithmetic: 83.8 us -> 20 us
  waiting for transfers between devices: 260 us -> 200 us
  matrix products: 58.8 us -> 1.29 us
  starting transfers between devices: 107 us -> 52.4 us
  local copies, waits for them, and re-layouts: 72.4 us -> 18.9 us
  between operations: 2.27 us -> 14.3 us
  blocking collectives: 79 us -> 68.1 us
    all_to_all x20 -> x1, waiting for transfers between devices: 210 us -> 0.01 us  [reduced(): terms = lax.all_to_all(joined, ('fsdp',) + CHIPS, 0, 0, tiled=True)]
    ppermute x9 -> x17, waiting for transfers between devices: 49.7 us -> 187 us  [the longest x10 120 us: swap_bit(): lax.ppermute(value, axis, [(i, i ^ 1 << bit) for i in range(lax.axis_size...]
    all_to_all x20 -> x1, starting transfers between devices: 96.8 us -> 3.74 us  [reduced(): terms = lax.all_to_all(joined, ('fsdp',) + CHIPS, 0, 0, tiled=True)]
    pallas_call x5 -> x14, Pallas kernels: 55.6 us -> 118 us  [call(): pl.pallas_call(kernel, out_shape=[jax.ShapeDtypeStruct(s, d) for s, d in...]
    dot_general x24 -> x1, matrix products: 58.2 us -> 0.42 us  [on_device(): jnp.einsum('bh,tb->ht', table, onehots, precision=lax.Precision.HIGHEST)]
    psum x1 -> x0, blocking collectives: 40 us -> none  [on_device(): vector = lax.psum(vector, ('z', 'y', 'core', 'fsdp'))]
    ppermute x9 -> x17, starting transfers between devices: 7.75 us -> 46 us  [the longest x10 37.4 us: swap_bit(): lax.ppermute(value, axis, [(i, i ^ 1 << bit) for i in range(lax.axis_size...]
    convert_element_type x15 -> x2, other arithmetic: 31.4 us -> 1.43 us  [the longest x1 0.77 us: on_device(): first = scatter(first, steps[1:]).astype(BF16)]
  transfers between devices with their start and end apart: 46 -> 33, of which waited for: 19 -> 13; matrix products, arithmetic and copies ran while one was open for 26% -> 6% of each run, Pallas kernels for 8% -> 22%
where the time goes in v2:
time: 501 us
  waiting for transfers between devices  200 us (40%)
  Pallas kernels  126 us (25%)
  blocking collectives  68.1 us (14%)
  starting transfers between devices  52.4 us (10%)
  other arithmetic  20 us (4%)
  local copies, waits for them, and re-layouts  18.9 us (4%)
  between operations  14.3 us (3%)
    ppermute x10, waiting for transfers between devices, swap_bit(): lax.ppermute(value, axis, [(i, i ^ 1 << bit) for i in range(lax.axis_size...  120 us
    pallas_call x14, Pallas kernels, call(): pl.pallas_call(kernel, out_shape=[jax.ShapeDtypeStruct(s, d) for s, d in...  118 us
    all_to_all x1, blocking collectives, reduced(): lax.all_to_all(copies, CHIPS, 0, 0, tiled=True).reshape(-1, joined.shape[2])  68.1 us
    ppermute x6, waiting for transfers between devices, gather_fsdp(): return [own, lax.ppermute(own, 'fsdp', [(0, 1), (1, 0)])]  53.8 us
    ppermute x10, starting transfers between devices, swap_bit(): lax.ppermute(value, axis, [(i, i ^ 1 << bit) for i in range(lax.axis_size...  37.4 us
    ppermute x1, waiting for transfers between devices, on_device(): first_other = lax.ppermute(first[1], 'fsdp', [(0, 1), (1, 0)])  13.7 us
  transfers between devices with their start and end apart: 33, of which 13 were waited for; matrix products, arithmetic and copies ran while one was open for 6% of the time, Pallas kernels for 22%

profile of v2, /device:TPU:0, one launch (start us, length us, event | category | flops | bytes accessed | tf_op | source)
XLA Modules:
  0.0 500.5 jit_solution(13782156602640701953)
XLA Ops:
  9.2 5.3 %shard_map.343 = (bf16[384,768]{1,0:T(8,128)(2,1)}, bf16[384,1152]{1,0:T(8,128)(2,1)}, bf16[384,1536]{1,0:T(8,128)(2,1)}, bf16[768,768]{1,0:T(8,128)(2,1)}) custom-call(s32[1]{0:T(128)} %bitcast.1.core_ref, f32[384,768]{1,0:T(8,128)} %refs_0_.3, f32[384,768]{1,0:T(8,128)} %refs_1_.3, f32[384,768]{1,0:T(8,128)} %refs_2_.3, f32[384,768]{1,0:T(8,128)} %refs_3_.1, ...), custom_call_target="tpu_custom_call" | custom-call | tf_op jit(solution)/shard_map/pallas_call | solution.py:746
  19.7 2.5 shard_map.341.refs_0_
  23.1 27.8 %collective-permute-done = bf16[1,1344]{1,0:T(2,128)(2,1)S(1)} collective-permute-done((bf16[1,1344]{1,0:T(2,128)(2,1)S(1)}, bf16[1,1344]{1,0:T(2,128)(2,1)S(1)}, u32[]{:S(2)}, u32[]{:S(2)}) %collective-permute-start) | collective-permute-done | bytes 2720 | tf_op jit(solution)/shard_map/ppermute | solution.py:771
  54.7 15.2 %collective-permute-done.1.refs_1_ = bf16[384,1152]{1,0:T(8,128)(2,1)} collective-permute-done((bf16[384,1152]{1,0:T(8,128)(2,1)}, bf16[384,1152]{1,0:T(8,128)(2,1)}, u32[]{:S(2)}, u32[]{:S(2)}) %collective-permute-start.1) | collective-permute-done | bytes 884768 | tf_op jit(solution)/shard_map/ppermute | solution.py:771
  69.9 5.5 %all-gather.8.cloned.1.call-done.xe_ref = bf16[2048,1536]{1,0:T(8,128)(2,1)} async-done(((bf16[128,1536]{1,0:T(8,128)(2,1)}), bf16[2048,1536]{1,0:T(8,128)(2,1)}) %all-gather.8.cloned.1.call-update) | async-done | bytes 6291472 | tf_op jit(solution)/shard_map/all_gather | solution.py:779
  75.5 14.5 %shard_map.342 = (bf16[9,2048,128]{2,1,0:T(8,128)(2,1)}, bf16[768,1152]{1,0:T(8,128)(2,1)}, f32[256,384]{1,0:T(8,128)}, bf16[256,384]{1,0:T(8,128)(2,1)}, f32[256,128]{1,0:T(8,128)}) custom-call(s32[3]{0:T(128)} %pad_add_fusion.at_ref, s32[1,6]{1,0:T(1,128)} %len_ref.9, bf16[2048,1536]{1,0:T(8,128)(2,1)} %all-gather.8.cloned.1.call-done.xe_ref, ...), custom_call_target="tpu_custom_call" | custom-call | flops 4429185024 | bytes 15289344 | tf_op jit(solution)/shard_map/pallas_call | solution.py:727
  92.3 16.3 %shard_map.344 = (f32[256,768]{1,0:T(8,128)}, bf16[256,768]{1,0:T(8,128)(2,1)}, bf16[256,384]{1,0:T(8,128)(2,1)}, bf16[6,2048,128]{2,1,0:T(8,128)(2,1)}, f32[256...) custom-call(s32[3]{0:T(128)} %pad_add_fusion.at_ref, ...), custom_call_target="tpu_custom_call" | custom-call | flops 3221225472 | bytes 20188160 | tf_op jit(solution)/shard_map/pallas_call | solution.py:727
  109.5 10.8 %collective-permute-done.10.refs_3_ = bf16[768,768]{1,0:T(8,128)(2,1)} collective-permute-done((bf16[768,768]{1,0:T(8,128)(2,1)S(1)}, bf16[768,768]{1,0:T(8,128)(2,1)}, u32[]{:S(2)}, u32[]{:S(2)}) %collective-permute-start.10) | collective-permute-done | bytes 1179680 | tf_op jit(solution)/shard_map/ppermute | solution.py:771
  121.0 8.7 %shard_map.345 = (f32[256,768]{1,0:T(8,128)}, bf16[256,768]{1,0:T(8,128)(2,1)}, bf16[256,1536]{1,0:T(8,128)(2,1)}, bf16[256,1536]{1,0:T(8,128)(2,1)}, bf16[256,7...) custom-call(s32[3]{0:T(128)} %pad_add_fusion.at_ref, ...), custom_call_target="tpu_custom_call" | custom-call | flops 2415919104 | bytes 12192768 | tf_op jit(solution)/shard_map/pallas_call | solution.py:727
  129.7 6.4 %shard_map.346 = (f32[384,3072]{1,0:T(8,128)}, bf16[384,3072]{1,0:T(8,128)(2,1)}) custom-call(s32[3]{0:T(128)} %pad_add_fusion.at_ref, bf16[256,1536]{1,0:T(8,128)(2,1)} %get-tuple-element.107.hid_ref, bf16[256,768]{1,0:T(8,128)(2,1)} %get-tuple-element.108.cot_ref, bf16[256,768]{1,0:T(8,128)(2,1)} %get-tuple-element.109.in_ref, ...), custom_call_target="tpu_custom_call" | custom-call | flops 1207959552 | bytes 9437184 | tf_op jit(solution)/shard_map/pallas_call | solution.py:727
  138.7 10.2 %shard_map.347 = (f32[256,768]{1,0:T(8,128)}, bf16[256,768]{1,0:T(8,128)(2,1)}, f32[1,768]{1,0:T(1,128)}, bf16[256,384]{1,0:T(8,128)(2,1)}, bf16[2048,768]{1,0:T(8,128)(2,1)}, /*index=5*/f32[256,768]{1,0:T(8,128)}) custom-call(s32[3]{0:T(128)} %pad_add_fusion.at_ref, s32[1,6]{1,0:T(1,128)} %len_ref.9, s32[1,6]{1,0:T(1,128)} %enc_ref.3, s32[1,6]{1,0:T(1,128)} %deal_ref.3, ...), custom_call_target="tpu_custom_call" | custom-call | flops 2013265920 | bytes 14882816 | tf_op jit(solution)/shard_map/pallas_call | solution.py:727
  152.3 4.7 shard_map.348
  163.0 3.7 shard_map.349
  166.7 9.7 %shard_map.350 = (bf16[256,384]{1,0:T(8,128)(2,1)}, f32[8,512]{1,0:T(8,128)}) custom-call(s32[3]{0:T(128)} %pad_add_fusion.at_ref, s32[1,6]{1,0:T(1,128)} %len_ref.9, f32[8,512]{1,0:T(8,128)} %get-tuple-element.163.bias_ref, bf16[9,2048,128]{2,1,0:T(8,128)(2,1)} %get-tuple-element.105.qkv_ref, bf16[256,384]{1,0:T(8,128)(2,1)} %get-tuple-element.130.go_ref, ...), custom_call_target="tpu_custom_call" | custom-call | flops 1207959552 | bytes 5668864 | tf_op jit(solution)/shard_map/pallas_call | solution.py:727
  176.3 13.7 %collective-permute-done.20 = bf16[384,3072]{1,0:T(8,128)(2,1)} collective-permute-done((bf16[384,3072]{1,0:T(8,128)(2,1)}, bf16[384,3072]{1,0:T(8,128)(2,1)}, u32[]{:S(2)}, u32[]{:S(2)}) %collective-permute-start.20) | collective-permute-done | bytes 2359328 | tf_op jit(solution)/shard_map/ppermute | solution.py:927
  190.0 4.9 convert_add_fusion
  202.0 15.6 %collective-permute-done.21 = bf16[1,384,1152]{2,1,0:T(8,128)(2,1)} collective-permute-done((bf16[1,384,1152]{2,1,0:T(8,128)(2,1)}, bf16[1,384,1152]{2,1,0:T(8,128)(2,1)}, u32[]{:S(2)}, u32[]{:S(2)}) %collective-permute-start.21) | collective-permute-done | bytes 884768 | tf_op jit(solution)/shard_map/ppermute | solution.py:787
  220.9 12.8 %collective-permute-start.15 = (bf16[2,256,768]{2,1,0:T(8,128)(2,1)S(1)}, bf16[2,256,768]{2,1,0:T(8,128)(2,1)S(1)}, u32[]{:S(2)}, u32[]{:S(2)}) collective-permute-start(bf16[2,256,768]{2,1,0:T(8,128)(2,1)S(1)} %fusion.3), channel_id=1, source_target_pairs={{0,16},{8,24},{16,0},{24,8},{1,17},{9,25},{17,1},{25,9},{2,18},{10... | collective-permute-start | bytes 2359304 | tf_op jit(solution)/shard_map/ppermute | solution.py:787
  235.7 8.5 %collective-permute-start.23 = (bf16[96,1152]{1,0:T(8,128)(2,1)S(1)}, bf16[96,1152]{1,0:T(8,128)(2,1)S(1)}, u32[]{:S(2)}, u32[]{:S(2)}) collective-permute-start(bf16[96,1152]{1,0:T(8,128)(2,1)S(1)} %fusion.8), channel_id=1, source_target_pairs={{0,8},{8,0},{16,24},{24,16},{1,9},{9,1},{17,25},{25,17},{2,10},{10... | collective-permute-start | bytes 663560 | tf_op jit(solution)/shard_map/ppermute | solution.py:787
  244.2 24.9 %collective-permute-done.15 = bf16[2,256,768]{2,1,0:T(8,128)(2,1)S(1)} collective-permute-done((bf16[2,256,768]{2,1,0:T(8,128)(2,1)S(1)}, bf16[2,256,768]{2,1,0:T(8,128)(2,1)S(1)}, u32[]{:S(2)}, u32[]{:S(2)}) %collective-permute-start.15) | collective-permute-done | bytes 786464 | tf_op jit(solution)/shard_map/ppermute | solution.py:787
  269.4 2.8 collective-permute-start.24
  272.3 2.5 collective-permute-start.16
  286.0 3.8 shard_map.351
  289.8 23.1 %shard_map.352 = (bf16[768,2048]{1,0:T(8,128)(2,1)}, f32[128,768]{1,0:T(8,128)}, f32[128,768]{1,0:T(8,128)}) custom-call(s32[3]{0:T(128)} %pad_add_fusion.at_ref, s32[1,6]{1,0:T(1,128)} %len_ref.9, f32[8,512]{1,0:T(8,128)} %get-tuple-element.162.bias_ref, bf16[9,2048,128]{2,1,0:T(8,128)(2,1)} %get-tuple-element.105.qkv_ref, bf16[16,144,768]{2,1,0:T(8,128)(2,1)} %bitcast.115, ...), custom_call_target="tpu_custom_call" | custom-call | flops 1610612736 | bytes 17320960 | tf_op jit(solution)/shard_map/pallas_call | solution.py:727
  312.9 3.7 all-to-all-start
  318.3 2.8 collective-permute-start.27
  321.1 76.8 %collective-permute-done.27 = bf16[48,3072]{1,0:T(8,128)(2,1)S(1)} collective-permute-done((bf16[48,3072]{1,0:T(8,128)(2,1)S(1)}, bf16[48,3072]{1,0:T(8,128)(2,1)S(1)}, u32[]{:S(2)}, u32[]{:S(2)}) %collective-permute-start.27) | collective-permute-done | bytes 294944 | tf_op jit(solution)/shard_map/ppermute | solution.py:787
  399.6 68.1 %all_to_all.10 = bf16[8,48,2048]{2,1,0:T(8,128)(2,1)S(1)} all-to-all(bf16[8,48,2048]{2,1,0:T(8,128)(2,1)S(1)} %broadcast_in_dim.16), channel_id=1, replica_groups=mesh['z'=4,'y'=2,'core'=2,'fsdp'=2] {'z','y'}, dimensions={0} | all-to-all | bytes 3145728 | tf_op jit(solution)/shard_map/all_to_all | solution.py:1006
  468.7 4.1 collective-permute-done.11
  474.4 3.3 shard_map.355
  480.8 6.7 %shard_map.356 = (f32[1536,768]{1,0:T(8,128)}, f32[384,3072]{1,0:T(8,128)}) custom-call(bf16[16,48,3072]{2,1,0:T(8,128)(2,1)} %bitcast.110), custom_call_target="tpu_custom_call" | custom-call | flops 2359296 | bytes 14155776 | tf_op jit(solution)/shard_map/pallas_call | solution.py:727
  489.3 4.7 shard_map.354
  (180 shorter events, 62.2 us)
Async XLA Ops:
  7.2 68.3 %all-gather.8.cloned.1.call-start = ((), (), s32[]{:S(2)}) async-start(), calls=%async_computation.2 | async-start | bytes 6684672 | tf_op jit(solution)/shard_map/all_gather | solution.py:779
  9.1 280.7 %all-gather.10.cloned.1.call-start = ((), (), s32[]{:S(2)}) async-start(), calls=%async_computation.3 | async-start | bytes 3760128 | tf_op jit(solution)/shard_map/all_gather | solution.py:945
  14.4 76.4 %collective-permute-start.4 = (bf16[384,768]{1,0:T(8,128)(2,1)}, bf16[384,768]{1,0:T(8,128)(2,1)}, u32[]{:S(2)}, u32[]{:S(2)}) collective-permute-start(bf16[384,768]{1,0:T(8,128)(2,1)} %get-tuple-element.94.refs_0_), channel_id=1, source_target_pairs={{0,2},{2,0},{1,3},{3,1},{4,6},{6,4},{5,7},{7,5},{8,10},{10,8},{9,1... | collective-permute-start | bytes 1769480 | tf_op jit(solution)/shard_map/ppermute | solution.py:764
  14.9 39.8 %collective-permute-start.3 = (bf16[384,768]{1,0:T(8,128)(2,1)}, bf16[384,768]{1,0:T(8,128)(2,1)}, u32[]{:S(2)}, u32[]{:S(2)}) collective-permute-start(bf16[384,768]{1,0:T(8,128)(2,1)} %get-tuple-element.94.refs_0_), channel_id=1, source_target_pairs={{0,1},{1,0},{2,3},{3,2},{4,5},{5,4},{6,7},{7,6},{8,9},{9,8},{10,11... | collective-permute-start | bytes 1769480 | tf_op jit(solution)/shard_map/ppermute | solution.py:771
  17.4 34.6 %collective-permute-start.6 = (bf16[384,1152]{1,0:T(8,128)(2,1)}, bf16[384,1152]{1,0:T(8,128)(2,1)}, u32[]{:S(2)}, u32[]{:S(2)}) collective-permute-start(bf16[384,1152]{1,0:T(8,128)(2,1)} %get-tuple-element.95.refs_4_), channel_id=1, source_target_pairs={{0,1},{1,0},{2,3},{3,2},{4,5},{5,4},{6,7},{7,6},{8,9},{9,8},{10,11... | collective-permute-start | bytes 2654216 | tf_op jit(solution)/shard_map/ppermute | solution.py:771
  17.7 33.1 %collective-permute-start = (bf16[1,1344]{1,0:T(2,128)(2,1)S(1)}, bf16[1,1344]{1,0:T(2,128)(2,1)S(1)}, u32[]{:S(2)}, u32[]{:S(2)}) collective-permute-start(bf16[1,1344]{1,0:T(2,128)(2,1)S(1)} %constant_dynamic-update-slice_fusion), channel_id=1, source_target_pairs={{0,1},{1,0},{2,3},{3,2},{4,5},{5,4},{6,7},{7,6},{8,9},{9,8},{10,11... | collective-permute-start | bytes 8072 | tf_op jit(solution)/shard_map/ppermute | solution.py:771
  22.2 47.7 %collective-permute-start.1 = (bf16[384,1152]{1,0:T(8,128)(2,1)}, bf16[384,1152]{1,0:T(8,128)(2,1)}, u32[]{:S(2)}, u32[]{:S(2)}) collective-permute-start(bf16[384,1152]{1,0:T(8,128)(2,1)} %shard_map.341.refs_0_), channel_id=1, source_target_pairs={{0,1},{1,0},{2,3},{3,2},{4,5},{5,4},{6,7},{7,6},{8,9},{9,8},{10,11... | collective-permute-start | bytes 2654216 | tf_op jit(solution)/shard_map/ppermute | solution.py:771
  52.0 57.5 %collective-permute-start.9 = (bf16[384,1536]{1,0:T(8,128)(2,1)S(1)}, bf16[384,1536]{1,0:T(8,128)(2,1)}, u32[]{:S(2)}, u32[]{:S(2)}) collective-permute-start(bf16[384,1536]{1,0:T(8,128)(2,1)S(1)} %copy-done.23), channel_id=1, source_target_pairs={{0,1},{1,0},{2,3},{3,2},{4,5},{5,4},{6,7},{7,6},{8,9},{9,8},{10,11... | collective-permute-start | bytes 3538952 | tf_op jit(solution)/shard_map/ppermute | solution.py:771
  54.0 66.3 %collective-permute-start.10 = (bf16[768,768]{1,0:T(8,128)(2,1)S(1)}, bf16[768,768]{1,0:T(8,128)(2,1)}, u32[]{:S(2)}, u32[]{:S(2)}) collective-permute-start(bf16[768,768]{1,0:T(8,128)(2,1)S(1)} %copy-done.24), channel_id=1, source_target_pairs={{0,1},{1,0},{2,3},{3,2},{4,5},{5,4},{6,7},{7,6},{8,9},{9,8},{10,11... | collective-permute-start | bytes 3538952 | tf_op jit(solution)/shard_map/ppermute | solution.py:771
  54.7 36.3 %collective-permute-start.5 = (bf16[384,768]{1,0:T(8,128)(2,1)}, bf16[384,768]{1,0:T(8,128)(2,1)}, u32[]{:S(2)}, u32[]{:S(2)}) collective-permute-start(bf16[384,768]{1,0:T(8,128)(2,1)} %collective-permute-done.3.refs_1_), channel_id=1, source_target_pairs={{0,2},{2,0},{1,3},{3,1},{4,6},{6,4},{5,7},{7,5},{8,10},{10,8},{9,1... | collective-permute-start | bytes 1769480 | tf_op jit(solution)/shard_map/ppermute | solution.py:764
  90.8 18.7 %collective-permute-start.8 = (bf16[128,768]{1,0:T(8,128)(2,1)S(1)}, bf16[128,768]{1,0:T(8,128)(2,1)S(1)}, u32[]{:S(2)}, u32[]{:S(2)}) collective-permute-start(bf16[128,768]{1,0:T(8,128)(2,1)S(1)} %copy-done.27), channel_id=1, source_target_pairs={{0,2},{2,0},{1,3},{3,1},{4,6},{6,4},{5,7},{7,5},{8,10},{10,8},{9,1... | collective-permute-start | bytes 589832 | tf_op jit(solution)/shard_map/ppermute | solution.py:764
  108.6 11.7 %collective-permute-start.7 = (bf16[256,384]{1,0:T(8,128)(2,1)}, bf16[256,384]{1,0:T(8,128)(2,1)S(1)}, u32[]{:S(2)}, u32[]{:S(2)}) collective-permute-start(bf16[256,384]{1,0:T(8,128)(2,1)} %get-tuple-element.97.low_ref.low2_ref), channel_id=1, source_target_pairs={{0,2},{2,0},{1,3},{3,1},{4,6},{6,4},{5,7},{7,5},{8,10},{10,8},{9,1... | collective-permute-start | bytes 589832 | tf_op jit(solution)/shard_map/ppermute | solution.py:764
  129.7 8.1 %collective-permute-start.12 = (f32[256,768]{1,0:T(8,128)}, f32[256,768]{1,0:T(8,128)S(1)}, u32[]{:S(2)}, u32[]{:S(2)}) collective-permute-start(f32[256,768]{1,0:T(8,128)} %get-tuple-element.112.e_ref), channel_id=1, source_target_pairs={{0,2},{2,0},{1,3},{3,1},{4,6},{6,4},{5,7},{7,5},{8,10},{10,8},{9,1... | collective-permute-start | bytes 2359304 | tf_op jit(solution)/shard_map/ppermute | solution.py:764
  136.0 54.0 %collective-permute-start.20 = (bf16[384,3072]{1,0:T(8,128)(2,1)}, bf16[384,3072]{1,0:T(8,128)(2,1)}, u32[]{:S(2)}, u32[]{:S(2)}) collective-permute-start(bf16[384,3072]{1,0:T(8,128)(2,1)} %get-tuple-element.111), channel_id=1, source_target_pairs={{0,1},{1,0},{2,3},{3,2},{4,5},{5,4},{6,7},{7,6},{8,9},{9,8},{10,11... | collective-permute-start | bytes 7077896 | tf_op jit(solution)/shard_map/ppermute | solution.py:927
  148.9 2.5 collective-permute-start.13
  157.1 317.3 %all-gather.12.cloned.1.call-start = ((), (), s32[]{:S(2)}) async-start(), calls=%async_computation.4 | async-start | bytes 1880064 | tf_op jit(solution)/shard_map/all_gather | solution.py:1013
  161.2 39.1 %collective-permute-start.14 = (bf16[4,256,768]{2,1,0:T(8,128)(2,1)}, bf16[4,256,768]{2,1,0:T(8,128)(2,1)S(1)}, u32[]{:S(2)}, u32[]{:S(2)}) collective-permute-start(bf16[4,256,768]{2,1,0:T(8,128)(2,1)} %dynamic-slice_bitcast_fusion), channel_id=1, source_target_pairs={{0,4},{4,0},{1,5},{5,1},{2,6},{6,2},{3,7},{7,3},{8,12},{12,8},{9,1... | collective-permute-start | bytes 4718600 | tf_op jit(solution)/shard_map/ppermute | solution.py:787
  195.9 21.6 %collective-permute-start.21 = (bf16[1,384,1152]{2,1,0:T(8,128)(2,1)}, bf16[1,384,1152]{2,1,0:T(8,128)(2,1)}, u32[]{:S(2)}, u32[]{:S(2)}) collective-permute-start(bf16[1,384,1152]{2,1,0:T(8,128)(2,1)} %dynamic-slice_bitcast_fusion.1), channel_id=1, source_target_pairs={{0,1},{1,0},{2,3},{3,2},{4,5},{5,4},{6,7},{7,6},{8,9},{9,8},{10,11... | collective-permute-start | bytes 2654216 | tf_op jit(solution)/shard_map/ppermute | solution.py:787
  219.0 16.7 %collective-permute-start.22 = (bf16[192,1152]{1,0:T(8,128)(2,1)S(1)}, bf16[192,1152]{1,0:T(8,128)(2,1)S(1)}, u32[]{:S(2)}, u32[]{:S(2)}) collective-permute-start(bf16[192,1152]{1,0:T(8,128)(2,1)S(1)} %fusion.6), channel_id=1, source_target_pairs={{0,4},{4,0},{1,5},{5,1},{2,6},{6,2},{3,7},{7,3},{8,12},{12,8},{9,1... | collective-permute-start | bytes 1327112 | tf_op jit(solution)/shard_map/ppermute | solution.py:787
  220.9 48.3 %collective-permute-start.15 = (bf16[2,256,768]{2,1,0:T(8,128)(2,1)S(1)}, bf16[2,256,768]{2,1,0:T(8,128)(2,1)S(1)}, u32[]{:S(2)}, u32[]{:S(2)}) collective-permute-start(bf16[2,256,768]{2,1,0:T(8,128)(2,1)S(1)} %fusion.3), channel_id=1, source_target_pairs={{0,16},{8,24},{16,0},{24,8},{1,17},{9,25},{17,1},{25,9},{2,18},{10... | collective-permute-start | bytes 2359304 | tf_op jit(solution)/shard_map/ppermute | solution.py:787
  235.5 41.4 %collective-permute-start.25 = (bf16[192,3072]{1,0:T(8,128)(2,1)S(1)}, bf16[192,3072]{1,0:T(8,128)(2,1)}, u32[]{:S(2)}, u32[]{:S(2)}) collective-permute-start(bf16[192,3072]{1,0:T(8,128)(2,1)S(1)} %fusion), channel_id=1, source_target_pairs={{0,4},{4,0},{1,5},{5,1},{2,6},{6,2},{3,7},{7,3},{8,12},{12,8},{9,1... | collective-permute-start | bytes 3538952 | tf_op jit(solution)/shard_map/ppermute | solution.py:787
  235.7 33.6 %collective-permute-start.23 = (bf16[96,1152]{1,0:T(8,128)(2,1)S(1)}, bf16[96,1152]{1,0:T(8,128)(2,1)S(1)}, u32[]{:S(2)}, u32[]{:S(2)}) collective-permute-start(bf16[96,1152]{1,0:T(8,128)(2,1)S(1)} %fusion.8), channel_id=1, source_target_pairs={{0,8},{8,0},{16,24},{24,16},{1,9},{9,1},{17,25},{25,17},{2,10},{10... | collective-permute-start | bytes 663560 | tf_op jit(solution)/shard_map/ppermute | solution.py:787
  269.4 6.8 %collective-permute-start.24 = (bf16[48,1152]{1,0:T(8,128)(2,1)S(1)}, bf16[48,1152]{1,0:T(8,128)(2,1)S(1)}, u32[]{:S(2)}, u32[]{:S(2)}) collective-permute-start(bf16[48,1152]{1,0:T(8,128)(2,1)S(1)} %fusion.10), channel_id=1, source_target_pairs={{0,16},{8,24},{16,0},{24,8},{1,17},{9,25},{17,1},{25,9},{2,18},{10... | collective-permute-start | bytes 331784 | tf_op jit(solution)/shard_map/ppermute | solution.py:787
  272.3 12.7 %collective-permute-start.16 = (bf16[1,256,768]{2,1,0:T(8,128)(2,1)S(1)}, bf16[1,256,768]{2,1,0:T(8,128)(2,1)S(1)}, u32[]{:S(2)}, u32[]{:S(2)}) collective-permute-start(bf16[1,256,768]{2,1,0:T(8,128)(2,1)S(1)} %dynamic-slice_convert_fusion.4), channel_id=1, source_target_pairs={{0,8},{8,0},{16,24},{24,16},{1,9},{9,1},{17,25},{25,17},{2,10},{10... | collective-permute-start | bytes 1179656 | tf_op jit(solution)/shard_map/ppermute | solution.py:787
  281.5 35.2 %collective-permute-start.26 = (bf16[96,3072]{1,0:T(8,128)(2,1)}, bf16[96,3072]{1,0:T(8,128)(2,1)}, u32[]{:S(2)}, u32[]{:S(2)}) collective-permute-start(bf16[96,3072]{1,0:T(8,128)(2,1)} %fusion.4), channel_id=1, source_target_pairs={{0,8},{8,0},{16,24},{24,16},{1,9},{9,1},{17,25},{25,17},{2,10},{10... | collective-permute-start | bytes 1769480 | tf_op jit(solution)/shard_map/ppermute | solution.py:787
  312.9 85.8 %all-to-all-start = ((bf16[16,48,2048]{2,1,0:T(8,128)(2,1)}), bf16[16,48,2048]{2,1,0:T(8,128)(2,1)S(1)}, u32[]{:S(2)}, u32[]{:S(2)}) async-start(bf16[16,48,2048]{2,1,0:T(8,128)(2,1)} %bitcast.116), calls=%async_computation | async-start | bytes 6291456 | tf_op jit(solution)/shard_map/all_to_all | solution.py:1003
  316.6 164.2 %all-gather.14.cloned.1.call-start = ((), (), s32[]{:S(2)}) async-start(), calls=%async_computation.5 | async-start | bytes 5013504 | tf_op jit(solution)/shard_map/all_gather | solution.py:1012
  318.3 79.6 %collective-permute-start.27 = (bf16[48,3072]{1,0:T(8,128)(2,1)S(1)}, bf16[48,3072]{1,0:T(8,128)(2,1)S(1)}, u32[]{:S(2)}, u32[]{:S(2)}) collective-permute-start(bf16[48,3072]{1,0:T(8,128)(2,1)S(1)} %fusion.7), channel_id=1, source_target_pairs={{0,16},{8,24},{16,0},{24,8},{1,17},{9,25},{17,1},{25,9},{2,18},{10... | collective-permute-start | bytes 884744 | tf_op jit(solution)/shard_map/ppermute | solution.py:787
  467.7 19.9 %collective-permute-start.19 = (bf16[384,2048]{1,0:T(8,128)(2,1)S(1)}, bf16[384,2048]{1,0:T(8,128)(2,1)S(1)}, u32[]{:S(2)}, u32[]{:S(2)}) collective-permute-start(bf16[384,2048]{1,0:T(8,128)(2,1)S(1)} %bitcast.105), channel_id=1, source_target_pairs={{0,2},{2,0},{1,3},{3,1},{4,6},{6,4},{5,7},{7,5},{8,10},{10,8},{9,1... | collective-permute-start | bytes 4718600 | tf_op jit(solution)/shard_map/ppermute | solution.py:764
  467.7 5.1 %collective-permute-start.11 = (f32[128,768]{1,0:T(8,128)S(1)}, f32[128,768]{1,0:T(8,128)S(1)}, u32[]{:S(2)}, u32[]{:S(2)}) collective-permute-start(f32[128,768]{1,0:T(8,128)S(1)} %copy-done.25), channel_id=1, source_target_pairs={{0,2},{2,0},{1,3},{3,1},{4,6},{6,4},{5,7},{7,5},{8,10},{10,8},{9,1... | collective-permute-start | bytes 1179656 | tf_op jit(solution)/shard_map/ppermute | solution.py:764
  468.2 5.4 %collective-permute-start.18 = (f32[128,768]{1,0:T(8,128)S(1)}, f32[128,768]{1,0:T(8,128)S(1)}, u32[]{:S(2)}, u32[]{:S(2)}) collective-permute-start(f32[128,768]{1,0:T(8,128)S(1)} %copy-done.26), channel_id=1, source_target_pairs={{0,2},{2,0},{1,3},{3,1},{4,6},{6,4},{5,7},{7,5},{8,10},{10,8},{9,1... | collective-permute-start | bytes 1179656 | tf_op jit(solution)/shard_map/ppermute | solution.py:764
  468.2 9.5 %collective-permute-start.17 = (f32[128,768]{1,0:T(8,128)}, f32[128,768]{1,0:T(8,128)S(1)}, u32[]{:S(2)}, u32[]{:S(2)}) collective-permute-start(f32[128,768]{1,0:T(8,128)} %get-tuple-element.140), channel_id=1, source_target_pairs={{0,2},{2,0},{1,3},{3,1},{4,6},{6,4},{5,7},{7,5},{8,10},{10,8},{9,1... | collective-permute-start | bytes 1179656 | tf_op jit(solution)/shard_map/ppermute | solution.py:764
  (32 other events, 571.2 us)
Sparse Core Ops, SparseCore 0:
  10.9 64.5 all-gather.7
  157.2 76.2 all-gather.9
  277.0 45.2 all-gather.11
  398.9 73.7 all-gather.13

commit v3 on v2

--- a/solution.py
+++ b/solution.py
@@ -97,65 +97,90 @@
     return jnp.where(low, both[:rows], both[rows:])
 
 
-def fill_tiles(bias_ref, tiles, first, second):
-    for h in range(LOCAL):
-        rolled = pltpu.roll(
-            jnp.broadcast_to(bias_ref[h : h + 1, :], (ROWS, 2 * ROWS)), 0, 1, stride=1, stride_axis=0
-        )
-        tiles[first, h] = rolled[:, :ROWS]
-        tiles[second, h] = rolled[:, ROWS:]
-        tiles[0, h] = jnp.broadcast_to(bias_ref[h : h + 1, 2 * ROWS - 1 :], (ROWS, ROWS))
+def tiles_kernel(bias_ref, tiles_ref):
+    def head(h, c):
+        for which in range(2):
+            row = bias_ref[pl.ds(8 * which + h, 1), :]
+            rolled = pltpu.roll(jnp.broadcast_to(row, (ROWS, 2 * ROWS)), 0, 1, stride=1, stride_axis=0)
+            first, second = (1, 2) if which == 0 else (2, 1)
+            tiles_ref[which, first, h] = rolled[:, :ROWS].astype(BF16)
+            tiles_ref[which, second, h] = rolled[:, ROWS:].astype(BF16)
+            tiles_ref[which, 0, h] = jnp.broadcast_to(row[:, 2 * ROWS - 1 :], (ROWS, ROWS)).astype(BF16)
+        return c
+
+    lax.fori_loop(0, LOCAL, head, 0)
 
 
 def lanes_of(p):
-    return pl.ds(pl.multiple_of(p * 128, 128), 128)
+    return slice(p * 128, p * 128 + 128) if isinstance(p, int) else pl.ds(pl.multiple_of(p * 128, 128), 128)
 
 
 def each_pair(body):
-    lax.fori_loop(0, PAIRS, lambda p, c: (body(p), c)[1], 0)
+    for p in range(PAIRS):
+        body(p)
 
 
 def rms_inverse(value):
     return lax.rsqrt(jnp.mean(value * value, axis=-1, keepdims=True) + EPS)
 
 
-def attend(p, queries, keys, values, visit, extra, s_scr, mx_scr, l_scr, acc_scr, qs, o_ref, low_ref, lse_ref):
-    qs[...] = split_pair(queries)
-    mx_scr[...] = jnp.full_like(mx_scr, NEG)
-
-    def scores(j):
-        at = pl.multiple_of(j * ROWS, ROWS)
-        raw = dot_nt(qs[...], keys(at))
-        for i in range(2):
-            rows = slice(i * ROWS, (i + 1) * ROWS)
-            value = raw[rows] + extra(j, at, 2 * p + i)
-            s_scr[rows, pl.ds(at, ROWS)] = value
-            mx_scr[rows] = jnp.maximum(mx_scr[rows], value)
-
-    visit(scores)
-    peak = jnp.max(mx_scr[...], axis=1, keepdims=True)
-    l_scr[...] = jnp.zeros_like(l_scr)
-    acc_scr[...] = jnp.zeros_like(acc_scr)
-
-    def weigh(j):
-        at = pl.multiple_of(j * ROWS, ROWS)
-        weights = jnp.exp(s_scr[:, pl.ds(at, ROWS)] - peak)
-        l_scr[...] += weights
-        acc_scr[...] += dot_nn(weights.astype(BF16), values(at))
-
-    visit(weigh)
-    total = jnp.sum(l_scr[...], axis=1, keepdims=True)
-    result = join_pair(acc_scr[...] / total)
-    o_ref[:, lanes_of(p)] = result
-    low_ref[:, lanes_of(p)] = result.astype(BF16)
-    both = peak + jnp.log(total)
+def together(n):
+    return PAIRS if n <= 2048 else 1
+
+
+def attend(queries, keys, values, visit_scores, visit, s_scr, mx_scr, l_scr, acc_scr, qs, o_ref, low_ref, lse_ref):
+    count = s_scr.shape[0]
+    lse_ref[...] = jnp.zeros_like(lse_ref)
     lane = iota((ROWS, 128), 1)
-    lse = jnp.where(lane == 2 * p, both[:ROWS], lse_ref[...])
-    lse_ref[...] = jnp.where(lane == 2 * p + 1, both[ROWS:], lse)
+
+    def group(g):
+        for c in range(count):
+            qs[c] = split_pair(queries(g * count + c))
+        mx_scr[...] = jnp.full_like(mx_scr, NEG)
+
+        def scores(j, extra):
+            at = pl.multiple_of(j * ROWS, ROWS)
+            raws = [dot_nt(qs[c], keys(g * count + c, at)) for c in range(count)]
+            for c in range(count):
+                for i in range(2):
+                    rows = slice(i * ROWS, (i + 1) * ROWS)
+                    value = extra(2 * (g * count + c) + i, raws[c][rows])
+                    s_scr[c, rows, pl.ds(at, ROWS)] = value
+                    mx_scr[c, rows] = jnp.maximum(mx_scr[c, rows], jnp.maximum(value[:, :128], value[:, 128:]))
+
+        visit_scores(scores)
+        for c in range(count):
+            mx_scr[c] = jnp.broadcast_to(jnp.max(mx_scr[c], axis=1, keepdims=True), mx_scr.shape[1:])
+        l_scr[...] = jnp.zeros_like(l_scr)
+        acc_scr[...] = jnp.zeros_like(acc_scr)
+
+        def weigh(j):
+            at = pl.multiple_of(j * ROWS, ROWS)
+            for c in range(count):
+                weights = jnp.exp(s_scr[c, :, pl.ds(at, ROWS)] - mx_scr[c, :, :1])
+                l_scr[c] += weights[:, :128] + weights[:, 128:]
+                acc_scr[c] += dot_nn(weights.astype(BF16), values(g * count + c, at))
+
+        visit(weigh)
+        for c in range(count):
+            p = g * count + c
+            total = jnp.sum(l_scr[c], axis=1, keepdims=True)
+            result = join_pair(acc_scr[c] / total)
+            o_ref[:, lanes_of(p)] = result
+            low_ref[:, lanes_of(p)] = result.astype(BF16)
+            both = mx_scr[c, :, :1] + jnp.log(total)
+            lse = jnp.where(lane == 2 * p, both[:ROWS], lse_ref[...])
+            lse_ref[...] = jnp.where(lane == 2 * p + 1, both[ROWS:], lse)
+
+    if count == PAIRS:
+        group(0)
+    else:
+        lax.fori_loop(0, PAIRS // count, lambda g, c: (group(g), c)[1], 0)
 
 
 ATTEND = lambda n: [
-    ((2 * ROWS, n), F32), ((2 * ROWS, ROWS), F32), ((2 * ROWS, ROWS), F32), ((2 * ROWS, 128), F32), ((2 * ROWS, 128), BF16),
+    ((together(n), 2 * ROWS, n), F32), ((together(n), 2 * ROWS, 128), F32), ((together(n), 2 * ROWS, 128), F32),
+    ((together(n), 2 * ROWS, 128), F32), ((together(n), 2 * ROWS, 128), BF16),
 ]
 
 
@@ -175,12 +200,11 @@
     return first
 
 
-def self_stage_kernel(n_parts, at_ref, len_ref, xe_ref, gain_ref, bias_ref, *refs):
+def self_stage_kernel(n_parts, at_ref, len_ref, xe_ref, gain_ref, tiles, *refs):
     parts, refs = refs[:n_parts], refs[n_parts:]
-    qkv_ref, w_ref, o_ref, low_ref, lse_ref, tiles, mask, s_scr, mx_scr, l_scr, acc_scr, qs = refs
+    qkv_ref, w_ref, o_ref, low_ref, lse_ref, s_scr, mx_scr, l_scr, acc_scr, qs = refs
     chip, side = at_ref[0], at_ref[2]
     set_rows(w_ref, parts, side)
-    fill_tiles(bias_ref, tiles, 1, 2)
     width = w_ref.shape[0]
     step = 512
 
@@ -198,31 +222,38 @@
     starts, ends = spans(len_ref)
     base = pl.multiple_of(chip * ROWS, ROWS)
     j_min = first_of(base, ends) // ROWS
+    full_from = first_of(base + ROWS - 1, ends)
     q_row = base + iota((ROWS, 1), 0)
     q_seg = seg_of(q_row, ends)
-    lse_ref[...] = jnp.zeros_like(lse_ref)
-
-    def fill_mask(j, c):
-        at = pl.multiple_of(j * ROWS, ROWS)
-        k_row = at + iota((1, ROWS), 1)
-        mask[:, pl.ds(at, ROWS)] = jnp.where((q_seg == seg_of(k_row, ends)) & (k_row <= q_row), 0.0, NEG)
-        return c
-
-    lax.fori_loop(j_min, chip + 1, fill_mask, 0)
 
     def visit(block):
         lax.fori_loop(j_min, chip + 1, lambda j, c: (block(j), c)[1], 0)
 
-    def extra(j, at, h):
-        return tiles[jnp.maximum(j - chip + 2, 0), h] + mask[:, pl.ds(at, ROWS)]
-
-    each_pair(
-        lambda p: attend(
-            p, qkv_ref[p, pl.ds(base, ROWS), :],
-            lambda at: qkv_ref[PAIRS + p, pl.ds(at, ROWS), :],
-            lambda at: qkv_ref[2 * PAIRS + p, pl.ds(at, ROWS), :],
-            visit, extra, s_scr, mx_scr, l_scr, acc_scr, qs, o_ref, low_ref, lse_ref,
-        )
+    def visit_scores(block):
+        def body(j, c):
+            at = pl.multiple_of(j * ROWS, ROWS)
+            plain = (at >= full_from) & (j < chip - 1)
+
+            @pl.when(plain)
+            def _():
+                block(j, lambda h, raw: raw + tiles[0, 0, h, :1, :1].astype(F32))
+
+            @pl.when(jnp.logical_not(plain))
+            def _():
+                k_row = at + iota((1, ROWS), 1)
+                masked = jnp.where((q_seg == seg_of(k_row, ends)) & (k_row <= q_row), 0.0, NEG)
+                tile = jnp.maximum(j - chip + 2, 0)
+                block(j, lambda h, raw: raw + (tiles[0, tile, h].astype(F32) + masked))
+
+            return c
+
+        lax.fori_loop(j_min, chip + 1, body, 0)
+
+    attend(
+        lambda p: qkv_ref[p, pl.ds(base, ROWS), :],
+        lambda p, at: qkv_ref[PAIRS + p, pl.ds(at, ROWS), :],
+        lambda p, at: qkv_ref[2 * PAIRS + p, pl.ds(at, ROWS), :],
+        visit_scores, visit, s_scr, mx_scr, l_scr, acc_scr, qs, o_ref, low_ref, lse_ref,
     )
 
 
@@ -235,7 +266,7 @@
 def cross_stage_kernel(n_parts, at_ref, len_ref, enc_ref, deal_ref, xe_ref, gain_ref, low_ref, other_ref, *refs):
     outs, mates, parts, refs = refs[:n_parts], refs[n_parts : 2 * n_parts], refs[2 * n_parts : 3 * n_parts], refs[3 * n_parts :]
     mid_ref, in_ref, q_ref, kv_ref, o_ref, low2_ref, lse_ref, so_ref, co_ref, wc_ref, refs = *refs[:10], refs[10:]
-    mask, s_scr, mx_scr, l_scr, acc_scr, qs = refs
+    s_scr, mx_scr, l_scr, acc_scr, qs = refs
     chip, core, side = at_ref[0], at_ref[1], at_ref[2]
     set_rows(wc_ref, parts, side)
     for pieces, column in ((outs, core), (mates, 1 - core)):
@@ -263,7 +294,6 @@
 
     lax.fori_loop(0, xe_ref.shape[0] // step, body, 0)
     wanted, q_pair, e_ends = cross_flags(chip, len_ref, enc_ref, deal_ref)
-    lse_ref[...] = jnp.zeros_like(lse_ref)
 
     def visit(block):
         def body(j, c):
@@ -275,19 +305,18 @@
 
         lax.fori_loop(0, kv_ref.shape[1] // ROWS, body, 0)
 
-    def fill_mask(j):
-        at = pl.multiple_of(j * ROWS, ROWS)
-        mask[:, pl.ds(at, ROWS)] = jnp.where(q_pair == seg_of(at + iota((1, ROWS), 1), e_ends), 0.0, NEG)
-
-    visit(fill_mask)
-    each_pair(
-        lambda p: attend(
-            p, q_ref[:, lanes_of(p)],
-            lambda at: kv_ref[p, pl.ds(at, ROWS), :],
-            lambda at: kv_ref[PAIRS + p, pl.ds(at, ROWS), :],
-            visit, lambda j, at, h: mask[:, pl.ds(at, ROWS)],
-            s_scr, mx_scr, l_scr, acc_scr, qs, o_ref, low2_ref, lse_ref,
-        )
+    def visit_scores(block):
+        def with_mask(j):
+            masked = jnp.where(q_pair == seg_of(j * ROWS + iota((1, ROWS), 1), e_ends), 0.0, NEG)
+            block(j, lambda h, raw: raw + masked)
+
+        visit(with_mask)
+
+    attend(
+        lambda p: q_ref[:, lanes_of(p)],
+        lambda p, at: kv_ref[p, pl.ds(at, ROWS), :],
+        lambda p, at: kv_ref[PAIRS + p, pl.ds(at, ROWS), :],
+        visit_scores, visit, s_scr, mx_scr, l_scr, acc_scr, qs, o_ref, low2_ref, lse_ref,
     )
 
 
@@ -414,14 +443,13 @@
 
 
 def self_query_grad_kernel(
-    at_ref, len_ref, bias_ref, qkv_ref, go_ref, o_ref, lse_ref, dq_ref, dist_ref,
-    tiles, qs, gs, lse_scr, delta_scr, dq_scr, ds_scr, stat_scr,
+    at_ref, len_ref, tiles, qkv_ref, go_ref, o_ref, lse_ref, dq_ref, dist_ref,
+    qs, gs, lse_scr, delta_scr, dq_scr, ds_scr, far_scr, stat_scr,
 ):
     chip = at_ref[0]
     starts, ends = spans(len_ref)
     base = pl.multiple_of(chip * ROWS, ROWS)
     first = first_of(base, ends)
-    fill_tiles(bias_ref, tiles, 1, 2)
     row_stats(go_ref, o_ref, lse_ref, gs, lse_scr, delta_scr, stat_scr)
 
     def start(p):
@@ -430,31 +458,43 @@
     each_pair(start)
     dq_scr[...] = jnp.zeros_like(dq_scr)
     ds_scr[...] = jnp.zeros_like(ds_scr)
+    far_scr[...] = jnp.zeros_like(far_scr)
+    full_from = first_of(base + ROWS - 1, ends)
     q_row = base + iota((ROWS, 1), 0)
     q_seg = seg_of(q_row, ends)
 
     def block(j, _):
         at = pl.multiple_of(j * ROWS, ROWS)
-        k_row = at + iota((1, ROWS), 1)
-        allowed = (q_seg == seg_of(k_row, ends)) & (k_row <= q_row)
-        masked = jnp.where(allowed, 0.0, NEG)
-        tile = jnp.maximum(j - chip + 2, 0)
-
-        def pair(p):
-            keys = qkv_ref[PAIRS + p, pl.ds(at, ROWS), :]
-            raw = dot_nt(qs[p], keys)
-            dprobs = dot_nt(gs[p], qkv_ref[2 * PAIRS + p, pl.ds(at, ROWS), :])
-            grads = []
-            for i in range(2):
-                rows = slice(i * ROWS, (i + 1) * ROWS)
-                value = raw[rows] + (tiles[tile, 2 * p + i] + masked)
-                probs = jnp.exp(value - lse_scr[p, rows, :1])
-                ds = (probs * (dprobs[rows] - delta_scr[p, rows, :1])).astype(BF16)
-                ds_scr[tile, 2 * p + i] += ds.astype(F32)
-                grads.append(ds)
-            dq_scr[p] += dot_nn(jnp.concatenate(grads, axis=0), keys)
-
-        each_pair(pair)
+        plain = (at >= full_from) & (j < chip - 1)
+
+        def gradients(extra, near):
+            raws = [dot_nt(qs[p], qkv_ref[PAIRS + p, pl.ds(at, ROWS), :]) for p in range(PAIRS)]
+            dprobs = [dot_nt(gs[p], qkv_ref[2 * PAIRS + p, pl.ds(at, ROWS), :]) for p in range(PAIRS)]
+            for p in range(PAIRS):
+                grads = []
+                for i in range(2):
+                    h = 2 * p + i
+                    rows = slice(i * ROWS, (i + 1) * ROWS)
+                    probs = jnp.exp(extra(h, raws[p][rows]) - lse_scr[p, rows, :1])
+                    ds = (probs * (dprobs[p][rows] - delta_scr[p, rows, :1])).astype(BF16)
+                    if near is None:
+                        far_scr[h] += jnp.sum(ds.astype(F32).reshape(ROWS // 8, 8, ROWS), axis=0)
+                    else:
+                        ds_scr[near, h] += ds.astype(F32)
+                    grads.append(ds)
+                dq_scr[p] += dot_nn(jnp.concatenate(grads, axis=0), qkv_ref[PAIRS + p, pl.ds(at, ROWS), :])
+
+        @pl.when(plain)
+        def _():
+            gradients(lambda h, raw: raw + tiles[0, 0, h, :1, :1].astype(F32), None)
+
+        @pl.when(jnp.logical_not(plain))
+        def _():
+            k_row = at + iota((1, ROWS), 1)
+            masked = jnp.where((q_seg == seg_of(k_row, ends)) & (k_row <= q_row), 0.0, NEG)
+            tile = jnp.maximum(j - chip + 2, 0)
+            gradients(lambda h, raw: raw + (tiles[0, tile, h].astype(F32) + masked), tile)
+
         return 0
 
     lax.fori_loop(first // ROWS, chip + 1, block, 0)
@@ -469,7 +509,8 @@
         while rows > 1:
             rows //= 2
             folded = folded[:rows] + pltpu.roll(folded[rows:], 2 * ROWS - rows, 1)
-        far = jnp.sum(jnp.sum(ds_scr[0, h], axis=0, keepdims=True), axis=1, keepdims=True)
+        far = jnp.sum(ds_scr[0, h], axis=0, keepdims=True) + jnp.sum(far_scr[h], axis=0, keepdims=True)
+        far = jnp.sum(far, axis=1, keepdims=True)
         dist_ref[pl.ds(h, 1), :] = folded + jnp.where(lanes == 2 * ROWS - 1, far, 0.0)
         return c
 
@@ -477,10 +518,10 @@
 
 
 def self_key_stage_kernel(
-    at_ref, len_ref, bias_ref, qkv_ref, message_ref, so_ref, dq_ref, w_ref, x_ref, gain_ref, ckv_ref, small_ref,
-    grads_ref, keep_ref, send_ref,
-    go_ref, stat_ref, tiles, ks, vs, dk_scr, dv_scr, dqkv_scr, h_scr, e_scr,
+    n_sides, at_ref, len_ref, tiles, qkv_ref, message_ref, so_ref, dq_ref, w_ref, x_ref, gain_ref, small_ref,
+    keep_ref, send_ref, *refs,
 ):
+    *outs, go_ref, stat_ref, ks, vs, dk_scr, dv_scr, dqkv_scr, h_scr, e_scr, grads_ref = refs
     chip, core = at_ref[0], at_ref[1]
     starts, ends = spans(len_ref)
     base = pl.multiple_of(chip * ROWS, ROWS)
@@ -488,7 +529,9 @@
     for end in reversed(ends[:-1]):
         last = jnp.where(base + ROWS - 1 < end, end, last)
     stop = (last - 1) // ROWS + 1
-    fill_tiles(bias_ref, tiles, 2, 1)
+    full_to = ends[-1]
+    for end in reversed(ends[:-1]):
+        full_to = jnp.where(base < end, end, full_to)
     heads = own_rows(core, HALF)
     half = ROWS // 2
 
@@ -515,28 +558,33 @@
 
     def block(i, _):
         at = pl.multiple_of(i * ROWS, ROWS)
-        q_row = at + iota((1, ROWS), 1)
-        allowed = (k_seg == seg_of(q_row, ends)) & (k_row <= q_row)
-        masked = jnp.where(allowed, 0.0, NEG)
-        tile = jnp.maximum(2 - (i - chip), 0)
-
-        def pair(p):
-            queries = qkv_ref[p, pl.ds(at, ROWS), :]
-            grads = go_ref[p, pl.ds(at, ROWS), :]
-            raw = dot_nt(ks[p], queries)
-            dprobs = dot_nt(vs[p], grads)
-            weights, dscores = [], []
-            for e in range(2):
-                rows = slice(e * ROWS, (e + 1) * ROWS)
-                h = 2 * p + e
-                value = raw[rows] + (tiles[tile, h] + masked)
-                probs = jnp.exp(value - stat_ref[i, pl.ds(h, 1), :])
-                weights.append(probs.astype(BF16))
-                dscores.append((probs * (dprobs[rows] - stat_ref[i, pl.ds(8 + h, 1), :])).astype(BF16))
-            dv_scr[p] += dot_nn(jnp.concatenate(weights, axis=0), grads)
-            dk_scr[p] += dot_nn(jnp.concatenate(dscores, axis=0), queries)
-
-        each_pair(pair)
+        plain = (at + ROWS <= full_to) & (i > chip + 1)
+
+        def gradients(extra):
+            raws = [dot_nt(ks[p], qkv_ref[p, pl.ds(at, ROWS), :]) for p in range(PAIRS)]
+            dprobs = [dot_nt(vs[p], go_ref[p, pl.ds(at, ROWS), :]) for p in range(PAIRS)]
+            for p in range(PAIRS):
+                weights, dscores = [], []
+                for e in range(2):
+                    rows = slice(e * ROWS, (e + 1) * ROWS)
+                    h = 2 * p + e
+                    probs = jnp.exp(extra(h, raws[p][rows]) - stat_ref[i, h : h + 1, :])
+                    weights.append(probs.astype(BF16))
+                    dscores.append((probs * (dprobs[p][rows] - stat_ref[i, 8 + h : 9 + h, :])).astype(BF16))
+                dv_scr[p] += dot_nn(jnp.concatenate(weights, axis=0), go_ref[p, pl.ds(at, ROWS), :])
+                dk_scr[p] += dot_nn(jnp.concatenate(dscores, axis=0), qkv_ref[p, pl.ds(at, ROWS), :])
+
+        @pl.when(plain)
+        def _():
+            gradients(lambda h, raw: raw + tiles[1, 0, h, :1, :1].astype(F32))
+
+        @pl.when(jnp.logical_not(plain))
+        def _():
+            q_row = at + iota((1, ROWS), 1)
+            masked = jnp.where((k_seg == seg_of(q_row, ends)) & (k_row <= q_row), 0.0, NEG)
+            tile = jnp.maximum(2 - (i - chip), 0)
+            gradients(lambda h, raw: raw + (tiles[1, tile, h].astype(F32) + masked))
+
         return 0
 
     lax.fori_loop(chip, stop, block, 0)
@@ -554,17 +602,17 @@
     dgain = jnp.transpose(jnp.where(iota((128, dgain.shape[1]), 0) == 0, dgain, 0.0))
     columns = grads_ref.shape[1]
     grads_ref[:, columns - 128 :] = (small_ref[...] + dgain).astype(BF16)
-    grads_ref[:, 3 * HALF : columns - 128] = ckv_ref[...]
     step = 256
     for i in range(0, h_scr.shape[1], step):
-        grads_ref[i : i + step, : 3 * HALF] = dot_tn(h_scr[:, i : i + step], dqkv_scr[...]).astype(BF16)
+        grads_ref[i : i + step, : 2 * HALF] = dot_tn(h_scr[:, i : i + step], dqkv_scr[:, HALF:]).astype(BF16)
+    give(n_sides, at_ref[2], grads_ref, outs)
 
 
 def cross_grad_stage_kernel(
-    at_ref, len_ref, enc_ref, deal_ref,
+    at_ref, len_ref, enc_ref, deal_ref, place_ref,
     e_ref, other_ref, late_ref, gain_ref, cot_ref, co_ref, q_ref, o_ref, lse_ref, kv_ref, wc_ref,
-    grad_ref, low_ref, dgain_ref, dq_ref, dkv_ref, part_ref,
-    go_ref, qs, gs, lse_scr, delta_scr, dq_scr, stat_scr,
+    grad_ref, low_ref, dgain_ref, dq_ref, keep_ref, send_ref, part_ref,
+    go_ref, qs, gs, lse_scr, delta_scr, dq_scr, stat_scr, block_scr,
 ):
     chip, core = at_ref[0], at_ref[1]
     dvalue, dgain = norm_grad(late_ref[...], gain_ref[...], e_ref[...] + other_ref[...])
@@ -582,35 +630,44 @@
     each_pair(start)
     dq_scr[...] = jnp.zeros_like(dq_scr)
 
+    half = keep_ref.shape[0] // ROWS
+
     def block(j, c):
         at = pl.multiple_of(j * ROWS, ROWS)
         hit = wanted(at)
-
-        @pl.when(hit)
-        def _():
+        upper = (place_ref[j] >= half).astype(jnp.int32)
+        to = pl.multiple_of((place_ref[j] - upper * half) * ROWS, ROWS)
+
+        def gradients(target):
             k_row = at + iota((1, ROWS), 1)
             masked = jnp.where(q_pair == seg_of(k_row, e_ends), 0.0, NEG)
-
-            def pair(p):
-                keys = kv_ref[p, pl.ds(at, ROWS), :]
-                raw = dot_nt(qs[p], keys)
-                dprobs = dot_nt(gs[p], kv_ref[PAIRS + p, pl.ds(at, ROWS), :])
+            raws = [dot_nt(qs[p], kv_ref[p, pl.ds(at, ROWS), :]) for p in range(PAIRS)]
+            dprobs = [dot_nt(gs[p], kv_ref[PAIRS + p, pl.ds(at, ROWS), :]) for p in range(PAIRS)]
+            for p in range(PAIRS):
                 weights, dscores = [], []
                 for i in range(2):
                     rows = slice(i * ROWS, (i + 1) * ROWS)
-                    probs = jnp.exp(raw[rows] + masked - lse_scr[p, rows, :1])
+                    probs = jnp.exp(raws[p][rows] + masked - lse_scr[p, rows, :1])
                     weights.append(probs.astype(BF16))
-                    dscores.append((probs * (dprobs[rows] - delta_scr[p, rows, :1])).astype(BF16))
+                    dscores.append((probs * (dprobs[p][rows] - delta_scr[p, rows, :1])).astype(BF16))
                 ds = jnp.concatenate(dscores, axis=0)
-                dq_scr[p] += dot_nn(ds, keys)
-                dkv_ref[pl.ds(at, ROWS), lanes_of(p)] = dot_tn(ds, qs[p]).astype(BF16)
-                dkv_ref[pl.ds(at, ROWS), lanes_of(PAIRS + p)] = dot_tn(jnp.concatenate(weights, axis=0), gs[p]).astype(BF16)
-
-            each_pair(pair)
+                dq_scr[p] += dot_nn(ds, kv_ref[p, pl.ds(at, ROWS), :])
+                target[:, lanes_of(p)] = dot_tn(ds, qs[p]).astype(BF16)
+                target[:, lanes_of(PAIRS + p)] = dot_tn(jnp.concatenate(weights, axis=0), gs[p]).astype(BF16)
+
+        @pl.when(hit)
+        def _():
+            gradients(block_scr)
 
         @pl.when(jnp.logical_not(hit))
         def _():
-            dkv_ref[pl.ds(at, ROWS), :] = jnp.zeros((ROWS, 2 * HALF), BF16)
+            block_scr[...] = jnp.zeros_like(block_scr)
+
+        for mine, target in ((True, keep_ref), (False, send_ref)):
+
+            @pl.when((upper == at_ref[3]) == mine)
+            def _():
+                target[pl.ds(to, ROWS), :] = block_scr[...]
 
         return c
 
@@ -651,17 +708,34 @@
         rest = rest - high.astype(F32)
 
 
-def projection_grads_kernel(at_ref, low2_ref, other2_ref, b2_ref, in_ref, dq_ref, low1_ref, other1_ref, b1_ref, out_ref):
-    core = at_ref[1]
+def projection_grads_kernel(
+    n_sides, at_ref, low2_ref, other2_ref, b2_ref, in_ref, dq2_ref, low1_ref, other1_ref, b1_ref, x_ref, gain_ref, dq1_ref, *outs
+):
+    *outs, out_ref = outs
+    core, side = at_ref[1], at_ref[2]
     lanes = pl.ds(pl.multiple_of(core * HALF, 128), HALF)
     for at, own, other, grad in ((0, low2_ref, other2_ref, b2_ref), (2 * HALF, low1_ref, other1_ref, b1_ref)):
         grads = grad[:, lanes]
-        for side, part in ((core, own), (1 - core, other)):
-            out_ref[own_rows(side, HALF), at : at + HALF] = dot_tn(part[...], grads).astype(BF16)
-    out_ref[:, HALF : 2 * HALF] = dot_tn(in_ref[...], dq_ref[...]).astype(BF16)
-
-
-def encoder_grads_kernel(at_ref, dkv_ref, e_ref, wc_ref, grads_ref, keep_ref, send_ref, low_scr, e_scr):
+        for which, part in ((core, own), (1 - core, other)):
+            out_ref[own_rows(which, HALF), at : at + HALF] = dot_tn(part[...], grads).astype(BF16)
+    out_ref[:, HALF : 2 * HALF] = dot_tn(in_ref[...], dq2_ref[...]).astype(BF16)
+    wide = x_ref[...].astype(F32)
+    normed = (wide * rms_inverse(wide) * gain_ref[...]).astype(BF16)
+    out_ref[:, 3 * HALF :] = dot_tn(normed, dq1_ref[...]).astype(BF16)
+    give(n_sides, side, out_ref, outs)
+
+
+def give(n_sides, side, value, outs):
+    if n_sides == 2:
+        rows = value.shape[0] // 2
+        outs[0][...] = value[own_rows(side, rows), :]
+        outs[1][...] = value[own_rows(1 - side, rows), :]
+    else:
+        outs[0][...] = value[...]
+
+
+def encoder_grads_kernel(n_sides, at_ref, dkv_ref, e_ref, wc_ref, keep_ref, send_ref, *outs):
+    *outs, low_scr, e_scr, grads_ref = outs
     core = at_ref[1]
     half = ROWS // 2
     low_scr[...] = dkv_ref[...].astype(BF16)
@@ -669,6 +743,7 @@
     keep_ref[...] = e_scr[own_rows(core, half), :]
     send_ref[...] = e_scr[own_rows(1 - core, half), :]
     grads_ref[...] = dot_tn(e_ref[...], low_scr[...]).astype(BF16)
+    give(n_sides, at_ref[2], grads_ref, outs)
 
 
 def token_grads_kernel(at_ref, e_ref, other_ref, x_ref, gain_ref, grad_ref, out_ref):
@@ -676,35 +751,47 @@
     out_ref[...] = grad_ref[own_rows(at_ref[1], out_ref.shape[0]), :] + dvalue
 
 
-def finish_columns_kernel(at_ref, own_ref, other_ref, *outs):
-    core = at_ref[1]
-    for i, out in enumerate(outs):
-        columns = slice(i * HALF, (i + 1) * HALF)
-        out[:, pl.ds(pl.multiple_of(core * HALF, 128), HALF)] = own_ref[:, columns].astype(F32)
-        out[:, pl.ds(pl.multiple_of((1 - core) * HALF, 128), HALF)] = other_ref[:, columns].astype(F32)
-
-
-def finish_ffn_kernel(order, parts_ref, outer_ref, inner_ref):
+def finish_late_kernel(count, at_ref, place_ref, own_ref, other_ref, *outs):
+    *outs, small = outs
+    core, place = at_ref[1], place_ref[0]
+    rows = own_ref.shape[0] // count
+    columns = slice(len(outs) * HALF, len(outs) * HALF + 128)
+    for i in range(count):
+        part = slice(i * rows, (i + 1) * rows)
+        to = pl.ds(pl.multiple_of((place ^ i) * rows, rows), rows)
+        for j, out in enumerate(outs):
+            lanes = slice(j * HALF, (j + 1) * HALF)
+            out[to, own_lanes(core)] = own_ref[part, lanes].astype(F32)
+            out[to, own_lanes(1 - core)] = other_ref[part, lanes].astype(F32)
+        small[to, :] = own_ref[part, columns].astype(F32) + other_ref[part, columns].astype(F32)
+
+
+def own_lanes(core):
+    return pl.ds(pl.multiple_of(core * HALF, 128), HALF)
+
+
+def finish_kernel(order, parts_ref, outer_ref, inner_ref, *outs):
     rows = parts_ref.shape[1]
+    width = outer_ref.shape[1]
     side = inner_ref.shape[0]
-    width = outer_ref.shape[1]
     unit = inner_ref.shape[1] // 4
-    for i, (core, place) in enumerate(order):
-        at = place * rows
+    for i in range(parts_ref.shape[0]):
+        core, at = i % 2, (i // 2) * rows
         for half in range(2):
             top = (2 * core + half) * side + at
             outer_ref[top : top + rows, :] = parts_ref[i, :, half * width : (half + 1) * width].astype(F32)
             lanes = slice((2 * half + core) * unit, (2 * half + core + 1) * unit)
             inner_ref[at : at + rows, lanes] = parts_ref[i, :, 2 * width + half * unit : 2 * width + (half + 1) * unit].astype(F32)
-
-
-def finish_gathered_kernel(order, parts_ref, *outs):
+    finish_columns_kernel(order, 4 * width, parts_ref, *outs)
+
+
+def finish_columns_kernel(order, skip, parts_ref, *outs):
     rows = parts_ref.shape[1]
     for i, (core, place) in enumerate(order):
+        at = slice(place * rows, (place + 1) * rows)
         for j, out in enumerate(outs):
-            out[place * rows : (place + 1) * rows, core * HALF : (core + 1) * HALF] = parts_ref[
-                i, :, j * HALF : (j + 1) * HALF
-            ].astype(F32)
+            columns = slice(skip + j * HALF, skip + (j + 1) * HALF)
+            out[at, core * HALF : (core + 1) * HALF] = parts_ref[i, :, columns].astype(F32)
 
 
 def pack_kernel(groups, core_ref, *refs):
@@ -731,11 +818,12 @@
         out_specs=[VMEM] * len(outs),
         scratch_shapes=[pltpu.VMEM(s, d) for s, d in scratch],
         compiler_params=pltpu.CompilerParams(vmem_limit_bytes=VMEM_LIMIT),
-        cost_estimate=pl.CostEstimate(flops=flops, transcendentals=0, bytes_accessed=moved),
+        cost_estimate=pl.CostEstimate(flops=1, transcendentals=0, bytes_accessed=1),
     )(*scalars, *arrays)
 
 
 TILES = ((3, LOCAL, ROWS, ROWS), F32)
+FAR = ((LOCAL, 8, ROWS), F32)
 STACK = ((PAIRS, 2 * ROWS, 128), BF16)
 COLUMN = ((PAIRS, 2 * ROWS, 128), F32)
 LANE = ((ROWS, 128), F32)
@@ -787,34 +875,49 @@
     return lax.ppermute(value, axis, [(i, i ^ (1 << bit)) for i in range(lax.axis_size(axis))])
 
 
-def halve(value, axis, bit):
+def parted(terms, axis, bit):
     side = (lax.axis_index(axis) >> bit) & 1
-    keep = lax.dynamic_index_in_dim(value, side, 0, keepdims=False).astype(F32)
-    send = lax.dynamic_index_in_dim(value, 1 - side, 0, keepdims=False).astype(BF16)
-    return keep + swap_bit(send, axis, bit).astype(F32)
+    rows = terms[0].shape[0] // 2
+
+    def half(which):
+        return [lax.dynamic_slice_in_dim(t, which * rows, rows, 0) for t in terms]
+
+    return half(side), total(half(1 - side)).astype(BF16)
+
+
+def halve(terms, axis, bit):
+    keep, send = parted(terms, axis, bit)
+    return keep + [swap_bit(send, axis, bit)]
+
+
+def total(terms):
+    return sum(t.astype(F32) for t in terms[1:]) + terms[0].astype(F32)
 
 
 def steps_of(*axes):
     return [(axis, bit) for axis in axes for bit in bits_of(axis)]
 
 
-def scatter(value, steps):
+def scatter(terms, steps):
     for axis, bit in steps:
-        value = halve(value.reshape((2, value.shape[0] // 2) + value.shape[1:]), axis, bit)
-    return value
+        terms = halve(terms, axis, bit)
+    return terms
 
 
 def scatter_fsdp(terms):
     return scatter(terms, [("fsdp", bit) for bit in reversed(bits_of("fsdp"))])
 
 
-def scatter_chips(value):
+def places(steps):
     nz, ny = lax.axis_size("z"), lax.axis_size("y")
-    value = value.reshape((nz, ny, value.shape[0] // (nz * ny)) + value.shape[1:])
-    value = jnp.swapaxes(value, 0, 1)
-    value = value.reshape((nz * ny,) + value.shape[2:])
-    steps = [(axis, bit) for axis in ("y", "z") for bit in reversed(bits_of(axis))]
-    return scatter(value, steps)[0]
+    found = []
+    for z in range(nz):
+        for y in range(ny):
+            place = 0
+            for axis, bit in steps:
+                place = 2 * place + (((z if axis == "z" else y) >> bit) & 1)
+            found.append(place)
+    return found
 
 
 def after(value, *earlier):
@@ -832,7 +935,9 @@
     fsdp = lax.axis_index("fsdp")
     n_fsdp = lax.axis_size("fsdp")
     chip = lax.axis_index(CHIPS)
-    at = jnp.stack([chip, core, fsdp]).astype(jnp.int32)
+    steps = steps_of("y", "z")
+    y_side = (lax.axis_index("y") >> steps[0][1]) & 1
+    at = jnp.stack([chip, core, fsdp, y_side]).astype(jnp.int32)
     core_ref = core.reshape(1).astype(jnp.int32)
     rows, width = tokens.shape
     n = 2 * rows * lax.axis_size(CHIPS)
@@ -881,14 +986,14 @@
     table = lax.dynamic_slice_in_dim(table, core * LOCAL, LOCAL, 1).astype(F32)
     onehots = np.concatenate([QK_ONEHOT, KQ_ONEHOT], axis=0)
     biases = jnp.einsum("bh,tb->ht", table, onehots, precision=lax.Precision.HIGHEST)
-    biases = jnp.pad(biases, ((0, 2), (0, 0)))
-    bias_qk, bias_kq = biases[:, : 2 * ROWS], biases[:, 2 * ROWS :]
+    biases = jnp.pad(biases.reshape(LOCAL, 2, 2 * ROWS).swapaxes(0, 1), ((0, 0), (0, 2), (0, 0)))
+    (tiles,) = call(tiles_kernel, (), (biases.reshape(16, 2 * ROWS),), [((2, *TILES[0]), BF16)], [], 1)
 
     xe = gather_rows(jnp.concatenate([tokens, encoded], axis=1))
     qkv, w_qkv, attn_self, low_self, lse_self = call(
-        functools.partial(self_stage_kernel, len(w_qkv)), (at, tgt_lengths), (xe, gain_self, bias_qk, *w_qkv),
+        functools.partial(self_stage_kernel, len(w_qkv)), (at, tgt_lengths), (xe, gain_self, tiles, *w_qkv),
         [((3 * PAIRS, n, 128), BF16), ((width, 3 * HALF), BF16), ((ROWS, HALF), F32), ((ROWS, HALF), BF16), LANE],
-        [TILES, ((ROWS, n), F32), *ATTEND(n)],
+        ATTEND(n),
         2 * n * width * 3 * HALF + 4 * ROWS * n * HALF,
     )
     low_self_other = swap_core(low_self)
@@ -900,7 +1005,7 @@
             wide, flat, ((ROWS, HALF), BF16), ((2 * PAIRS, n, 128), BF16), ((ROWS, HALF), F32), ((ROWS, HALF), BF16), LANE,
             ((width, width), BF16), ((width, width), BF16), ((width, 3 * HALF), BF16),
         ],
-        [((ROWS, n), F32), *ATTEND(n)],
+        ATTEND(n),
         2 * n * width * 2 * HALF + 4 * ROWS * n * HALF,
     )
     low_cross_other = swap_core(low_cross)
@@ -914,48 +1019,59 @@
         8 * ROWS * width * hidden_half,
     )
     e_ffn_other = swap_core(e_ffn)
-    ffn_out = (
-        [((side, 4 * width), F32), ((side, 4 * width), BF16)]
-        if n_fsdp == 2
-        else [((hidden_half, width), F32), ((width, hidden_half), F32)]
-    )
-    first = call(
-        functools.partial(ffn_grads_kernel, n_fsdp), (at,), (hidden, cot, in_ffn, d_pre), ffn_out, [],
-        4 * ROWS * width * hidden_half,
-    )
-    if n_fsdp == 2:
-        first_other = lax.ppermute(first[1], "fsdp", [(0, 1), (1, 0)])
-        e_ffn = after(e_ffn, first[1])
     output = out_keep + swap_core(out_send)
 
-    grad_late, late_low, d_gain_ffn, dq_cross, dkv_part, e_cross = call(
-        cross_grad_stage_kernel, (at, tgt_lengths, enc_lengths, deal),
+    place = places(steps)
+    place_ref = jnp.asarray(np.array(place, np.int32))
+    grad_late, late_low, d_gain_ffn, dq_cross, dkv_keep, dkv_send, e_cross = call(
+        cross_grad_stage_kernel, (at, tgt_lengths, enc_lengths, deal, place_ref),
         (e_ffn, e_ffn_other, x_late, gain_ffn, cot, w_co, q_cross, attn_cross, lse_cross, kv_cross, w_cross),
-        [wide, flat, ((1, width), F32), ((ROWS, HALF), BF16), ((n, 2 * HALF), BF16), wide],
-        [((ROWS, HALF), BF16), STACK, STACK, COLUMN, COLUMN, COLUMN, LANE],
+        [wide, flat, ((1, width), F32), ((ROWS, HALF), BF16), ((n // 2, 2 * HALF), BF16), ((n // 2, 2 * HALF), BF16), wide],
+        [((ROWS, HALF), BF16), STACK, STACK, COLUMN, COLUMN, COLUMN, LANE, ((ROWS, 2 * HALF), BF16)],
         10 * ROWS * n * HALF,
     )
     e_cross_other = swap_core(e_cross)
+    dkv_got = swap_bit(dkv_send, *steps[0])
 
     grad_mid, mid_low, d_gain_cross, go_self, message = call(
         self_grad_start_kernel, (at,), (e_cross, e_cross_other, x_mid, gain_cross, grad_late, w_so, attn_self, lse_self),
         [wide, flat, ((1, width), F32), ((ROWS, HALF), BF16), ((rows + 16, width), BF16)], [LANE],
         2 * ROWS * width * HALF,
     )
+    ffn_out = (
+        [((side, 4 * width), BF16), ((side, 4 * width), BF16)]
+        if n_fsdp == 2
+        else [((hidden_half, width), F32), ((width, hidden_half), F32)]
+    )
+    first = call(
+        functools.partial(ffn_grads_kernel, n_fsdp), (at,), (hidden, cot, in_ffn, after(d_pre, message)), ffn_out, [],
+        4 * ROWS * width * hidden_half,
+    )
+    if n_fsdp == 2:
+        first_other = lax.ppermute(first[1], "fsdp", [(0, 1), (1, 0)])
+        go_self = after(go_self, first[1])
     message = lax.all_gather(message, GROUP, axis=0)
-    (second,) = call(
-        projection_grads_kernel, (at,),
-        (low_cross, low_cross_other, late_low, in_cross, dq_cross, low_self, low_self_other, mid_low),
-        [((width, 3 * HALF), BF16)], [], 6 * ROWS * width * HALF,
-    )
-    dq_self, dist = call(
-        self_query_grad_kernel, (at, tgt_lengths), (bias_qk, qkv, after(go_self, second), attn_self, lse_self),
-        [((ROWS, HALF), BF16), ((8, 2 * ROWS), F32)],
-        [TILES, STACK, STACK, COLUMN, COLUMN, COLUMN, TILES, LANE],
-        6 * ROWS * n * HALF,
-    )
     x_chip = lax.dynamic_slice(xe, (chip * ROWS, 0), (ROWS, width))
     e_chip = lax.dynamic_slice(xe, (chip * ROWS, width), (ROWS, width))
+    dq_self, dist = call(
+        self_query_grad_kernel, (at, tgt_lengths), (tiles, qkv, go_self, attn_self, lse_self),
+        [((ROWS, HALF), BF16), ((8, 2 * ROWS), F32)],
+        [STACK, STACK, COLUMN, COLUMN, COLUMN, TILES, FAR, LANE],
+        6 * ROWS * n * HALF,
+    )
+    def given(columns):
+        return [((width // 2, columns), BF16)] * 2 if n_fsdp == 2 else [((width, columns), BF16)]
+
+    def over_fsdp(parts):
+        if n_fsdp == 2:
+            return [parts[0], lax.ppermute(parts[1], "fsdp", [(0, 1), (1, 0)])]
+        return scatter_fsdp(parts)
+
+    second = call(
+        functools.partial(projection_grads_kernel, n_fsdp), (at,),
+        (low_cross, low_cross_other, late_low, in_cross, dq_cross, low_self, low_self_other, mid_low, x_chip, gain_self, dq_self),
+        given(4 * HALF), [((width, 4 * HALF), BF16)], 8 * ROWS * width * HALF,
+    )
     d_table = jnp.einsum("ht,tb->bh", dist[:LOCAL], QK_ONEHOT, precision=lax.Precision.HIGHEST)
     d_table = jnp.zeros((BUCKETS, 2, LOCAL), F32).at[:, core].set(d_table).reshape(n_fsdp, -1, HEADS)
     d_table = jnp.pad(d_table, ((0, 0), (0, side - d_table.shape[1]), (0, 0))).reshape(width, HEADS)
@@ -963,86 +1079,105 @@
     small = [none, 0.5 * d_gain_cross.reshape(width, 1), 0.5 * d_gain_ffn.reshape(width, 1), d_table]
     small = jnp.pad(jnp.concatenate(small, axis=1), ((0, 0), (0, 128 - 3 - HEADS)))
 
-    dkv_cross = scatter_chips(dkv_part)
-    d_ckv, enc_keep, enc_send = call(
-        encoder_grads_kernel, (at,), (dkv_cross, e_chip, w_cross),
-        [((width, 2 * HALF), BF16), half_rows, half_rows], [((ROWS, 2 * HALF), BF16), wide],
-        8 * ROWS * width * HALF,
-    )
-    enc_grad = enc_keep + swap_core(enc_send)
-
-    steps = steps_of("y", "z")
     if n_fsdp == 2:
-        first = first[0] + first_other.astype(F32)
+        first = [first[0], first_other]
     else:
         outer = first[0].reshape(n_fsdp, 2, side, width)
         first = jnp.concatenate([outer[:, 0], outer[:, 1], first[1].reshape(n_fsdp, side, hidden_half)], axis=2)
-        first = scatter_fsdp(first)[0]
-    second = scatter_fsdp(after(second, first).reshape(n_fsdp, side, -1))[0]
-    first = scatter(first, steps[:1])
-    second = scatter(second, steps[:1])
-
-    d_qkv, e_keep, e_send = call(
-        self_key_stage_kernel, (at, tgt_lengths),
-        (bias_kq, qkv, after(message, dq_self), w_so, dq_self, w_qkv, x_chip, gain_self, d_ckv, small),
-        [((width, 5 * HALF + 128), BF16), half_rows, half_rows],
+        first = scatter_fsdp([first.reshape(width, -1)])
+    *y_steps, z_near, z_far = steps
+    dkv_cross = scatter([dkv_keep, dkv_got], y_steps[1:])
+    dkv_keep, dkv_sent = parted(after(dkv_cross, second[-1]), *z_near)
+    dkv_near = swap_bit(dkv_sent, *z_near)
+    first = total(after(first, dkv_sent)).astype(BF16)
+    second = over_fsdp(after(second, first))
+
+    e_keep, e_send, *fourth = call(
+        functools.partial(self_key_stage_kernel, n_fsdp), (at, tgt_lengths),
+        (tiles, qkv, after(message, first), w_so, dq_self, w_qkv, x_chip, gain_self, small),
+        [half_rows, half_rows, *given(2 * HALF + 128)],
         [
-            ((PAIRS, n, 128), BF16), ((n // ROWS, 16, ROWS), F32), TILES, STACK, STACK, COLUMN, COLUMN,
-            ((ROWS, 3 * HALF), BF16), flat, wide,
+            ((PAIRS, n, 128), BF16), ((n // ROWS, 16, ROWS), F32), STACK, STACK, COLUMN, COLUMN,
+            ((ROWS, 3 * HALF), BF16), flat, wide, ((width, 2 * HALF + 128), BF16),
         ],
         8 * ROWS * n * HALF,
     )
+    first = lax.psum_scatter(after(first, message), CHIPS, scatter_dimension=0, tiled=True)
+    fourth_sent = fourth[-1]
+    fourth = over_fsdp(fourth)
+    dkv_keep, dkv_sent = parted(dkv_keep + [after(dkv_near, fourth_sent)], *z_far)
+    dkv_far = swap_bit(dkv_sent, *z_far)
+    second_keep, second_sent = parted(after(second, dkv_sent), *y_steps[0])
+    second_got = swap_bit(second_sent, *y_steps[0])
+    enc_keep, enc_send, *third = call(
+        functools.partial(encoder_grads_kernel, n_fsdp), (at,),
+        (total(dkv_keep + [after(dkv_far, second_sent)]), e_chip, w_cross),
+        [half_rows, half_rows, *given(2 * HALF)],
+        [((ROWS, 2 * HALF), BF16), wide, ((width, 2 * HALF), BF16)], 8 * ROWS * width * HALF,
+    )
+    third_sent = third[-1]
+    third = over_fsdp(third)
     (grad_tokens,) = call(
-        token_grads_kernel, (at,), (e_keep, swap_core(e_send), tokens, gain_self, grad_mid),
+        token_grads_kernel, (at,), (e_keep, swap_core(after(e_send, third_sent)), tokens, gain_self, grad_mid),
         [half_rows], [], 10 * rows * width,
     )
-
-    def reduced(joined):
-        count = n_fsdp * lax.axis_size(CHIPS)
-        joined = joined.reshape(count, -1, joined.shape[1])
-        terms = lax.all_to_all(joined, ("fsdp",) + CHIPS, 0, 0, tiled=True)
-        total = jnp.sum(terms.astype(F32), axis=0).astype(BF16)
-        copies = jnp.broadcast_to(total[None], (lax.axis_size(CHIPS),) + total.shape)
-        own = lax.all_to_all(copies, CHIPS, 0, 0, tiled=True).reshape(-1, joined.shape[2])
-        return own, swap_core(own)
-
-    third = reduced(d_qkv)
-    first = scatter(first, steps[1:]).astype(BF16)
-    second = scatter(second, steps[1:]).astype(BF16)
-    first = lax.all_gather(first, GROUP, axis=0)
-    second = lax.all_gather(second, GROUP, axis=0)
-
-    nz, ny = lax.axis_size("z"), lax.axis_size("y")
-    order = []
-    for z in range(nz):
-        for y in range(ny):
-            place = 0
-            for axis, bit in steps:
-                place = 2 * place + (((z if axis == "z" else y) >> bit) & 1)
-            order += [(0, place), (1, place)]
+    enc_grad = enc_keep + swap_core(after(enc_send, third_sent))
+
+    second_got, third, fourth = after((second_got, third, fourth), grad_tokens, enc_grad)
+    second = scatter(second_keep + [second_got], y_steps[1:])
+    second_keep, second_sent = parted(second, *z_near)
+    second_got = swap_bit(second_sent, *z_near)
+    late = [jnp.concatenate([total(third), total(after(fourth, second_sent))], axis=1)]
+    late_keep, late_sent = parted(late, *y_steps[0])
+    late_got = swap_bit(late_sent, *y_steps[0])
+    first = after(first, late_sent)
+    second_keep, second_sent = parted(second_keep + [after(second_got, late_sent)], *z_far)
+    second_got = swap_bit(second_sent, *z_far)
+    late = scatter(late_keep + [after(late_got, second_sent)], y_steps[1:])
+    late_keep, late_sent = parted(late, *z_near)
+    late_got = swap_bit(late_sent, *z_near)
+    second = total(second_keep + [after(second_got, late_sent)]).astype(BF16)
+    late = total(halve(late_keep + [after(late_got, second)], *z_far)).astype(BF16)
+    early = lax.all_gather(jnp.concatenate([first, second], axis=1), GROUP, axis=0)
+    for axis, bit in reversed(steps):
+        late = jnp.concatenate([late, swap_bit(late, axis, bit)], axis=0)
+    late_other = swap_core(late)
+    early = after(early, late_other)
+
     matrix = ((side, width), F32)
-    g_co, g_cq, g_so = call(
-        functools.partial(finish_gathered_kernel, order), (), (second,), [matrix] * 3, [], 6 * side * width
-    )
-    g_sq, g_sk, g_sv, g_ck, g_cv = call(finish_columns_kernel, (at,), third, [matrix] * 5, [], 10 * side * width)
-    if n_fsdp == 2:
-        g_outer, g_inner = call(
-            functools.partial(finish_ffn_kernel, order), (), (first,),
-            [(ffn_outer.shape, F32), (ffn_inner.shape, F32)], [], 8 * side * width,
+    own_place = place_ref[chip].reshape(1)
+    if side // len(place) % 8 == 0:
+        g_ck, g_cv, g_sk, g_sv, small = call(
+            functools.partial(finish_late_kernel, len(place)), (at, own_place), (late, late_other),
+            [matrix] * 4 + [((side, 128), F32)], [], 8 * side * width,
         )
     else:
-        places = np.argsort([2 * place + c for c, place in order])
-        first = first[places].reshape(nz * ny, 2, -1, first.shape[2])
-        pair = jnp.swapaxes(first, 0, 1).reshape(2, side, -1).astype(F32)
+        blocks = jnp.stack([late, late_other]).reshape(2, len(place), side // len(place), -1)
+        blocks = jnp.take(blocks, own_place[0] ^ jnp.arange(len(place), dtype=jnp.int32), axis=1)
+        blocks = jnp.where(core == 0, blocks, blocks[::-1]).astype(F32).reshape(2, side, -1)
+        g_ck, g_cv, g_sk, g_sv = (
+            jnp.swapaxes(blocks[:, :, i : i + HALF], 0, 1).reshape(side, width) for i in range(0, 4 * HALF, HALF)
+        )
+        small = jnp.sum(blocks[:, :, 4 * HALF :], axis=0)
+    order = [(c, p) for p in place for c in range(2)]
+    if n_fsdp == 2:
+        g_outer, g_inner, g_co, g_cq, g_so, g_sq = call(
+            functools.partial(finish_kernel, order), (), (early,),
+            [(ffn_outer.shape, F32), (ffn_inner.shape, F32), *[matrix] * 4], [], 8 * side * width,
+        )
+    else:
+        pair = jnp.swapaxes(early.reshape(len(place), 2, -1, early.shape[2]), 0, 1).reshape(2, side, -1).astype(F32)
         g_outer = pair[:, :, : 2 * width].reshape(2, side, 2, width)
         g_outer = jnp.swapaxes(g_outer, 1, 2).reshape(ffn_outer.shape)
-        g_inner = jnp.transpose(pair[:, :, 2 * width :].reshape(2, side, n_fsdp, unit), (1, 2, 0, 3))
+        g_inner = jnp.transpose(pair[:, :, 2 * width : 4 * width].reshape(2, side, n_fsdp, unit), (1, 2, 0, 3))
         g_inner = g_inner.reshape(ffn_inner.shape)
-    vectors = third[0][:, -128:].astype(F32) + third[1][:, -128:].astype(F32)
+        g_co, g_cq, g_so, g_sq = call(
+            functools.partial(finish_columns_kernel, order, 4 * width), (), (early,), [matrix] * 4, [], 8 * side * width
+        )
 
     return (
         output, grad_tokens, enc_grad,
-        vectors[:, 0], vectors[:, 1], vectors[:, 2], vectors[: bias_table.shape[0], 3 : 3 + HEADS],
+        small[:, 0], small[:, 1], small[:, 2], small[: bias_table.shape[0], 3 : 3 + HEADS],
         g_sq, g_sk, g_sv, g_so, g_cq, g_ck, g_cv, g_co, g_inner, g_outer,
     )
 

time: 501 us -> 429 us (0.86)
  blocking collectives: 68.1 us -> 0 us
  starting transfers between devices: 52.4 us -> 19.3 us
  Pallas kernels: 126 us -> 138 us
  waiting for transfers between devices: 200 us -> 208 us
  other arithmetic: 20 us -> 25.6 us
    all_to_all x1 -> x0, blocking collectives: 68.1 us -> none  [reduced(): lax.all_to_all(copies, CHIPS, 0, 0, tiled=True).reshape(-1, joined.shape[2])]
    ppermute x10 -> x12, starting transfers between devices: 37.4 us -> 3.07 us  [swap_bit(): lax.ppermute(value, axis, [(i, i ^ 1 << bit) for i in range(lax.axis_size...]
    ppermute x10 -> x12, waiting for transfers between devices: 120 us -> 143 us  [swap_bit(): lax.ppermute(value, axis, [(i, i ^ 1 << bit) for i in range(lax.axis_size...]
    ppermute x6, waiting for transfers between devices: 53.8 us -> 39 us  [gather_fsdp(): return [own, lax.ppermute(own, 'fsdp', [(0, 1), (1, 0)])]]
    convert_element_type x2 -> x11, other arithmetic: 1.43 us -> 14.3 us  [the longest x8 10.6 us: parted(): return (half(side), total(half(1 - side)).astype(BF16))]
    pallas_call x14, Pallas kernels: 118 us -> 130 us  [call(): pl.pallas_call(kernel, out_shape=[jax.ShapeDtypeStruct(s, d) for s, d in...]
    ppermute x1, waiting for transfers between devices: 13.7 us -> 3.93 us  [on_device(): first_other = lax.ppermute(first[1], 'fsdp', [(0, 1), (1, 0)])]
    add x10 -> x4, other arithmetic: 12.9 us -> 4.6 us  [the longest x3 3.81 us: total(): return sum((t.astype(F32) for t in terms[1:])) + terms[0].astype(F32)]
  transfers between devices with their start and end apart: 33 -> 37, of which waited for: 13 -> 23; matrix products, arithmetic and copies ran while one was open for 6% -> 8% of each run, Pallas kernels for 22% -> 23%
where the time goes in v3:
time: 429 us; the launch traced here: 425 us
  waiting for transfers between devices  208 us (48%)
  Pallas kernels  138 us (32%)
  other arithmetic  25.6 us (6%)
  starting transfers between devices  19.3 us (4%)
  local copies, waits for them, and re-layouts  17.6 us (4%)
  between operations  14.2 us (3%)
    ppermute x12, waiting for transfers between devices, swap_bit(): lax.ppermute(value, axis, [(i, i ^ 1 << bit) for i in range(lax.axis_size...  143 us
    pallas_call x14, Pallas kernels, call(): pl.pallas_call(kernel, out_shape=[jax.ShapeDtypeStruct(s, d) for s, d in...  130 us
    ppermute x6, waiting for transfers between devices, gather_fsdp(): return [own, lax.ppermute(own, 'fsdp', [(0, 1), (1, 0)])]  39 us
    convert_element_type x8, other arithmetic, parted(): return (half(side), total(half(1 - side)).astype(BF16))  10.6 us
    ppermute x11, waiting for transfers between devices, swap_core(): return lax.ppermute(value, 'core', [(0, 1), (1, 0)])  9.45 us
    ppermute x6, starting transfers between devices, gather_fsdp(): return [own, lax.ppermute(own, 'fsdp', [(0, 1), (1, 0)])]  9.3 us
  transfers between devices with their start and end apart: 37, of which 23 were waited for; matrix products, arithmetic and copies ran while one was open for 8% of the time, Pallas kernels for 23%

profile of v3, /device:TPU:0, one launch (start us, length us, event | category | flops | bytes accessed | tf_op | source)
XLA Modules:
  0.0 424.9 jit_solution(17707996447809240778)
XLA Ops:
  9.2 5.3 %shard_map.353 = (bf16[384,768]{1,0:T(8,128)(2,1)}, bf16[384,1152]{1,0:T(8,128)(2,1)}, bf16[384,1536]{1,0:T(8,128)(2,1)}, bf16[768,768]{1,0:T(8,128)(2,1)}) custom-call(s32[1]{0:T(128)} %bitcast.1.core_ref, f32[384,768]{1,0:T(8,128)} %refs_0_.3, f32[384,768]{1,0:T(8,128)} %refs_1_.3, f32[384,768]{1,0:T(8,128)} %refs_2_.3, f32[384,768]{1,0:T(8,128)} %refs_3_.1, ...), custom_call_target="tpu_custom_call" | custom-call | tf_op jit(solution)/shard_map/pallas_call | solution.py:834
  14.4 2.9 collective-permute-start.6
  22.4 15.7 %collective-permute-done.6.refs_5_ = bf16[384,1152]{1,0:T(8,128)(2,1)S(1)} collective-permute-done((bf16[384,1152]{1,0:T(8,128)(2,1)}, bf16[384,1152]{1,0:T(8,128)(2,1)S(1)}, u32[]{:S(2)}, u32[]{:S(2)}) %collective-permute-start.6) | collective-permute-done | bytes 884768 | tf_op jit(solution)/shard_map/ppermute | solution.py:859
  41.0 9.8 %collective-permute-done = bf16[1,1344]{1,0:T(2,128)(2,1)S(1)} collective-permute-done((bf16[1,1344]{1,0:T(2,128)(2,1)S(1)}, bf16[1,1344]{1,0:T(2,128)(2,1)S(1)}, u32[]{:S(2)}, u32[]{:S(2)}) %collective-permute-start) | collective-permute-done | bytes 2720 | tf_op jit(solution)/shard_map/ppermute | solution.py:859
  58.3 3.8 shard_map.350.tiles
  62.8 7.1 %collective-permute-done.1.refs_1_ = bf16[384,1152]{1,0:T(8,128)(2,1)} collective-permute-done((bf16[384,1152]{1,0:T(8,128)(2,1)}, bf16[384,1152]{1,0:T(8,128)(2,1)}, u32[]{:S(2)}, u32[]{:S(2)}) %collective-permute-start.1) | collective-permute-done | bytes 884768 | tf_op jit(solution)/shard_map/ppermute | solution.py:859
  69.9 5.6 %all-gather.6.cloned.1.call-done.xe_ref = bf16[2048,1536]{1,0:T(8,128)(2,1)} async-done(((bf16[128,1536]{1,0:T(8,128)(2,1)}), bf16[2048,1536]{1,0:T(8,128)(2,1)}) %all-gather.6.cloned.1.call-update) | async-done | bytes 6291472 | tf_op jit(solution)/shard_map/all_gather | solution.py:867
  75.5 14.4 %shard_map.352 = (bf16[9,2048,128]{2,1,0:T(8,128)(2,1)}, bf16[768,1152]{1,0:T(8,128)(2,1)}, f32[256,384]{1,0:T(8,128)}, bf16[256,384]{1,0:T(8,128)(2,1)}, f32[256,128]{1,0:T(8,128)}) custom-call(s32[4]{0:T(128)} %pad_add_fusion.at_ref, s32[1,6]{1,0:T(1,128)} %len_ref.9, bf16[2048,1536]{1,0:T(8,128)(2,1)} %all-gather.6.cloned.1.call-done.xe_ref, ...), custom_call_target="tpu_custom_call" | custom-call | flops 1 | bytes 1 | tf_op jit(solution)/shard_map/pallas_call | solution.py:814
  92.3 20.0 %shard_map.354 = (f32[256,768]{1,0:T(8,128)}, bf16[256,768]{1,0:T(8,128)(2,1)}, bf16[256,384]{1,0:T(8,128)(2,1)}, bf16[6,2048,128]{2,1,0:T(8,128)(2,1)}, f32[256...) custom-call(s32[4]{0:T(128)} %pad_add_fusion.at_ref, ...), custom_call_target="tpu_custom_call" | custom-call | flops 1 | bytes 1 | tf_op jit(solution)/shard_map/pallas_call | solution.py:814
  113.2 6.4 %collective-permute-done.10.refs_3_ = bf16[768,768]{1,0:T(8,128)(2,1)} collective-permute-done((bf16[768,768]{1,0:T(8,128)(2,1)S(1)}, bf16[768,768]{1,0:T(8,128)(2,1)}, u32[]{:S(2)}, u32[]{:S(2)}) %collective-permute-start.10) | collective-permute-done | bytes 1179680 | tf_op jit(solution)/shard_map/ppermute | solution.py:859
  120.3 8.6 %shard_map.355 = (f32[256,768]{1,0:T(8,128)}, bf16[256,768]{1,0:T(8,128)(2,1)}, bf16[256,1536]{1,0:T(8,128)(2,1)}, bf16[256,1536]{1,0:T(8,128)(2,1)}, bf16[256,7...) custom-call(s32[4]{0:T(128)} %pad_add_fusion.at_ref, ...), custom_call_target="tpu_custom_call" | custom-call | flops 1 | bytes 1 | tf_op jit(solution)/shard_map/pallas_call | solution.py:814
  132.3 19.5 %shard_map.356 = (f32[256,768]{1,0:T(8,128)}, bf16[256,768]{1,0:T(8,128)(2,1)}, f32[1,768]{1,0:T(1,128)}, bf16[256,384]{1,0:T(8,128)(2,1)}, bf16[1024,768]{1,0:T...) custom-call(s32[4]{0:T(128)} %pad_add_fusion.at_ref, s32[1,6]{1,0:T(1,128)} %len_ref.9, s32[1,6]{1,0:T(1,128)} %enc_ref.3, ...), custom_call_target="tpu_custom_call" | custom-call | flops 1 | bytes 1 | tf_op jit(solution)/shard_map/pallas_call | solution.py:814
  155.2 4.1 shard_map.357
  159.4 5.7 %shard_map.358 = (bf16[384,3072]{1,0:T(8,128)(2,1)}, bf16[384,3072]{1,0:T(8,128)(2,1)}) custom-call(s32[4]{0:T(128)} %pad_add_fusion.at_ref, bf16[256,1536]{1,0:T(8,128)(2,1)} %get-tuple-element.151.hid_ref, bf16[256,768]{1,0:T(8,128)(2,1)} %get-tuple-element.139.cot_ref, bf16[256,768]{1,0:T(8,128)(2,1)} %get-tuple-element.152.in_ref, ...), custom_call_target="tpu_custom_call" | custom-call | flops 1 | bytes 1 | tf_op jit(solution)/shard_map/pallas_call | solution.py:814
  169.6 9.4 %shard_map.359 = (bf16[256,384]{1,0:T(8,128)(2,1)}, f32[8,512]{1,0:T(8,128)}) custom-call(s32[4]{0:T(128)} %pad_add_fusion.at_ref, s32[1,6]{1,0:T(1,128)} %len_ref.9, bf16[2,3,6,256,256]{4,3,2,1,0:T(8,128)(2,1)} %shard_map.350.tiles, bf16[9,2048,128]{2,1,0:T(8,128)(2,1)} %get-tuple-element.136.qkv_ref, bf16[256,384]{1,0:T(8,128)(2,1)} %get-tuple-element.164.go_ref, ...), custom_call_target="tpu_custom_call" | custom-call | flops 1 | bytes 1 | tf_op jit(solution)/shard_map/pallas_call | solution.py:814
  179.0 4.4 %shard_map.360 = (bf16[384,1536]{1,0:T(8,128)(2,1)}, bf16[384,1536]{1,0:T(8,128)(2,1)}) custom-call(s32[4]{0:T(128)} %pad_add_fusion.at_ref, bf16[256,384]{1,0:T(8,128)(2,1)} %get-tuple-element.128.low_ref.low2_ref, bf16[256,384]{1,0:T(8,128)(2,1)} %copy-done.12, bf16[256,768]{1,0:T(8,128)(2,1)} %get-tuple-element.159.b2_ref, ...), custom_call_target="tpu_custom_call" | custom-call | flops 1 | bytes 1 | tf_op jit(solution)/shard_map/pallas_call | solution.py:814
  183.4 29.9 %collective-permute-done.15 = bf16[1024,768]{1,0:T(8,128)(2,1)} collective-permute-done((bf16[1024,768]{1,0:T(8,128)(2,1)}, bf16[1024,768]{1,0:T(8,128)(2,1)}, u32[]{:S(2)}, u32[]{:S(2)}) %collective-permute-start.15) | collective-permute-done | bytes 1572896 | tf_op jit(solution)/shard_map/ppermute | solution.py:875
  214.6 3.9 collective-permute-done.14
  224.9 20.9 %shard_map.361 = (f32[128,768]{1,0:T(8,128)}, f32[128,768]{1,0:T(8,128)}, bf16[384,896]{1,0:T(8,128)(2,1)}, bf16[384,896]{1,0:T(8,128)(2,1)}) custom-call(s32[4]{0:T(128)} %pad_add_fusion.at_ref, s32[1,6]{1,0:T(1,128)} %len_ref.9, bf16[2,3,6,256,256]{4,3,2,1,0:T(8,128)(2,1)} %shard_map.350.tiles, bf16[9,2048,128]{2,1,0:T(8,128)(2,1)} %get-tuple-element.136.qkv_ref, ...), custom_call_target="tpu_custom_call" | custom-call | flops 1 | bytes 1 | tf_op jit(solution)/shard_map/pallas_call | solution.py:814
  245.8 14.1 %collective-permute-done.16 = bf16[512,768]{1,0:T(8,128)(2,1)} collective-permute-done((bf16[512,768]{1,0:T(8,128)(2,1)S(1)}, bf16[512,768]{1,0:T(8,128)(2,1)}, u32[]{:S(2)}, u32[]{:S(2)}) %collective-permute-start.16) | collective-permute-done | bytes 786464 | tf_op jit(solution)/shard_map/ppermute | solution.py:875
  264.3 12.0 %collective-permute-done.17 = bf16[256,768]{1,0:T(8,128)(2,1)} collective-permute-done((bf16[256,768]{1,0:T(8,128)(2,1)}, bf16[256,768]{1,0:T(8,128)(2,1)}, u32[]{:S(2)}, u32[]{:S(2)}) %collective-permute-start.17) | collective-permute-done | bytes 393248 | tf_op jit(solution)/shard_map/ppermute | solution.py:875
  278.7 3.8 shard_map.362
  289.7 6.6 %collective-permute-done.22 = bf16[384,768]{1,0:T(8,128)(2,1)} collective-permute-done((bf16[384,768]{1,0:T(8,128)(2,1)}, bf16[384,768]{1,0:T(8,128)(2,1)}, u32[]{:S(2)}, u32[]{:S(2)}) %collective-permute-start.22) | collective-permute-done | bytes 589856 | tf_op jit(solution)/shard_map/ppermute | solution.py:1067
  301.3 7.6 %collective-permute-done.25 = bf16[96,1536]{1,0:T(8,128)(2,1)S(1)} collective-permute-done((bf16[96,1536]{1,0:T(8,128)(2,1)}, bf16[96,1536]{1,0:T(8,128)(2,1)S(1)}, u32[]{:S(2)}, u32[]{:S(2)}) %collective-permute-start.25) | collective-permute-done | bytes 294944 | tf_op jit(solution)/shard_map/ppermute | solution.py:875
  315.2 3.2 collective-permute-done.27
  321.6 8.6 %collective-permute-done.26 = bf16[96,1664]{1,0:T(8,128)(2,1)S(1)} collective-permute-done((bf16[96,1664]{1,0:T(8,128)(2,1)}, bf16[96,1664]{1,0:T(8,128)(2,1)S(1)}, u32[]{:S(2)}, u32[]{:S(2)}) %collective-permute-start.26) | collective-permute-done | bytes 319520 | tf_op jit(solution)/shard_map/ppermute | solution.py:875
  330.4 20.3 %collective-permute-done.28 = bf16[48,1664]{1,0:T(8,128)(2,1)S(1)} collective-permute-done((bf16[48,1664]{1,0:T(8,128)(2,1)S(1)}, bf16[48,1664]{1,0:T(8,128)(2,1)S(1)}, u32[]{:S(2)}, u32[]{:S(2)}) %collective-permute-start.28) | collective-permute-done | bytes 159776 | tf_op jit(solution)/shard_map/ppermute | solution.py:875
  350.9 8.9 %collective-permute-done.29 = bf16[48,1664]{1,0:T(8,128)(2,1)S(1)} collective-permute-done((bf16[48,1664]{1,0:T(8,128)(2,1)S(1)}, bf16[48,1664]{1,0:T(8,128)(2,1)S(1)}, u32[]{:S(2)}, u32[]{:S(2)}) %collective-permute-start.29) | collective-permute-done | bytes 159776 | tf_op jit(solution)/shard_map/ppermute | solution.py:875
  359.9 23.9 %collective-permute-done.30 = bf16[96,1664]{1,0:T(8,128)(2,1)S(1)} collective-permute-done((bf16[96,1664]{1,0:T(8,128)(2,1)S(1)}, bf16[96,1664]{1,0:T(8,128)(2,1)S(1)}, u32[]{:S(2)}, u32[]{:S(2)}) %collective-permute-start.30) | collective-permute-done | bytes 319520 | tf_op jit(solution)/shard_map/ppermute | solution.py:875
  384.0 12.3 %collective-permute-done.31 = bf16[192,1664]{1,0:T(8,128)(2,1)S(1)} collective-permute-done((bf16[192,1664]{1,0:T(8,128)(2,1)S(1)}, bf16[192,1664]{1,0:T(8,128)(2,1)S(1)}, u32[]{:S(2)}, u32[]{:S(2)}) %collective-permute-start.31) | collective-permute-done | bytes 639008 | tf_op jit(solution)/shard_map/ppermute | solution.py:875
  401.7 4.9 %shard_map.364 = (f32[384,768]{1,0:T(8,128)}, f32[384,768]{1,0:T(8,128)}, f32[384,768]{1,0:T(8,128)}, f32[384,768]{1,0:T(8,128)}, f32[384,128]{1,0:T(8,128)}) custom-call(s32[4]{0:T(128)} %pad_add_fusion.at_ref, s32[1]{0:T(128)} %dynamic_slice.162.place_ref, bf16[384,1664]{1,0:T(8,128)(2,1)} %copy-done, bf16[384,1664]{1,0:T(8,128)(2,1)} %copy-done.4), custom_call_target="tpu_custom_call" | custom-call | flops 1 | bytes 1 | tf_op jit(solution)/shard_map/pallas_call | solution.py:814
  410.0 8.4 %shard_map.365 = (f32[1536,768]{1,0:T(8,128)}, f32[384,3072]{1,0:T(8,128)}, f32[384,768]{1,0:T(8,128)}, f32[384,768]{1,0:T(8,128)}, f32[384,768]{1,0:T(8,128)}, /*index=5*/f32[384,768]{1,0:T(8,128)}) custom-call(bf16[16,48,4608]{2,1,0:T(8,128)(2,1)} %bitcast.45), custom_call_target="tpu_custom_call" | custom-call | flops 1 | bytes 1 | tf_op jit(solution)/shard_map/pallas_call | solution.py:814
  (187 shorter events, 78.6 us)
Async XLA Ops:
  7.2 68.3 %all-gather.6.cloned.1.call-start = ((), (), s32[]{:S(2)}) async-start(), calls=%async_computation.1 | async-start | bytes 6684672 | tf_op jit(solution)/shard_map/all_gather | solution.py:867
  9.1 213.5 %all-gather.8.cloned.1.call-start = ((), (), s32[]{:S(2)}) async-start(), calls=%async_computation.3 | async-start | bytes 3760128 | tf_op jit(solution)/shard_map/all_gather | solution.py:1053
  14.4 23.6 %collective-permute-start.6 = (bf16[384,1152]{1,0:T(8,128)(2,1)}, bf16[384,1152]{1,0:T(8,128)(2,1)S(1)}, u32[]{:S(2)}, u32[]{:S(2)}) collective-permute-start(bf16[384,1152]{1,0:T(8,128)(2,1)} %get-tuple-element.126.refs_4_), channel_id=1, source_target_pairs={{0,1},{1,0},{2,3},{3,2},{4,5},{5,4},{6,7},{7,6},{8,9},{9,8},{10,11... | collective-permute-start | bytes 2654216 | tf_op jit(solution)/shard_map/ppermute | solution.py:859
  17.4 39.7 %collective-permute-start.3 = (bf16[384,768]{1,0:T(8,128)(2,1)}, bf16[384,768]{1,0:T(8,128)(2,1)}, u32[]{:S(2)}, u32[]{:S(2)}) collective-permute-start(bf16[384,768]{1,0:T(8,128)(2,1)} %get-tuple-element.125.refs_0_), channel_id=1, source_target_pairs={{0,1},{1,0},{2,3},{3,2},{4,5},{5,4},{6,7},{7,6},{8,9},{9,8},{10,11... | collective-permute-start | bytes 1769480 | tf_op jit(solution)/shard_map/ppermute | solution.py:859
  17.7 33.2 %collective-permute-start = (bf16[1,1344]{1,0:T(2,128)(2,1)S(1)}, bf16[1,1344]{1,0:T(2,128)(2,1)S(1)}, u32[]{:S(2)}, u32[]{:S(2)}) collective-permute-start(bf16[1,1344]{1,0:T(2,128)(2,1)S(1)} %constant_dynamic-update-slice_fusion), channel_id=1, source_target_pairs={{0,1},{1,0},{2,3},{3,2},{4,5},{5,4},{6,7},{7,6},{8,9},{9,8},{10,11... | collective-permute-start | bytes 8072 | tf_op jit(solution)/shard_map/ppermute | solution.py:859
  19.7 71.0 %collective-permute-start.4 = (bf16[384,768]{1,0:T(8,128)(2,1)}, bf16[384,768]{1,0:T(8,128)(2,1)}, u32[]{:S(2)}, u32[]{:S(2)}) collective-permute-start(bf16[384,768]{1,0:T(8,128)(2,1)} %get-tuple-element.125.refs_0_), channel_id=1, source_target_pairs={{0,2},{2,0},{1,3},{3,1},{4,6},{6,4},{5,7},{7,5},{8,10},{10,8},{9,1... | collective-permute-start | bytes 1769480 | tf_op jit(solution)/shard_map/ppermute | solution.py:852
  22.2 47.7 %collective-permute-start.1 = (bf16[384,1152]{1,0:T(8,128)(2,1)}, bf16[384,1152]{1,0:T(8,128)(2,1)}, u32[]{:S(2)}, u32[]{:S(2)}) collective-permute-start(bf16[384,1152]{1,0:T(8,128)(2,1)} %shard_map.351.refs_0_), channel_id=1, source_target_pairs={{0,1},{1,0},{2,3},{3,2},{4,5},{5,4},{6,7},{7,6},{8,9},{9,8},{10,11... | collective-permute-start | bytes 2654216 | tf_op jit(solution)/shard_map/ppermute | solution.py:859
  39.0 74.2 %collective-permute-start.9 = (bf16[384,1536]{1,0:T(8,128)(2,1)S(1)}, bf16[384,1536]{1,0:T(8,128)(2,1)S(1)}, u32[]{:S(2)}, u32[]{:S(2)}) collective-permute-start(bf16[384,1536]{1,0:T(8,128)(2,1)S(1)} %copy-done.6), channel_id=1, source_target_pairs={{0,1},{1,0},{2,3},{3,2},{4,5},{5,4},{6,7},{7,6},{8,9},{9,8},{10,11... | collective-permute-start | bytes 3538952 | tf_op jit(solution)/shard_map/ppermute | solution.py:859
  51.4 68.2 %collective-permute-start.10 = (bf16[768,768]{1,0:T(8,128)(2,1)S(1)}, bf16[768,768]{1,0:T(8,128)(2,1)}, u32[]{:S(2)}, u32[]{:S(2)}) collective-permute-start(bf16[768,768]{1,0:T(8,128)(2,1)S(1)} %copy-done.7), channel_id=1, source_target_pairs={{0,1},{1,0},{2,3},{3,2},{4,5},{5,4},{6,7},{7,6},{8,9},{9,8},{10,11... | collective-permute-start | bytes 3538952 | tf_op jit(solution)/shard_map/ppermute | solution.py:859
  57.1 33.9 %collective-permute-start.5 = (bf16[384,768]{1,0:T(8,128)(2,1)}, bf16[384,768]{1,0:T(8,128)(2,1)}, u32[]{:S(2)}, u32[]{:S(2)}) collective-permute-start(bf16[384,768]{1,0:T(8,128)(2,1)} %collective-permute-done.3.refs_1_), channel_id=1, source_target_pairs={{0,2},{2,0},{1,3},{3,1},{4,6},{6,4},{5,7},{7,5},{8,10},{10,8},{9,1... | collective-permute-start | bytes 1769480 | tf_op jit(solution)/shard_map/ppermute | solution.py:852
  90.8 22.4 %collective-permute-start.8 = (bf16[128,768]{1,0:T(8,128)(2,1)S(1)}, bf16[128,768]{1,0:T(8,128)(2,1)S(1)}, u32[]{:S(2)}, u32[]{:S(2)}) collective-permute-start(bf16[128,768]{1,0:T(8,128)(2,1)S(1)} %copy-done.21), channel_id=1, source_target_pairs={{0,2},{2,0},{1,3},{3,1},{4,6},{6,4},{5,7},{7,5},{8,10},{10,8},{9,1... | collective-permute-start | bytes 589832 | tf_op jit(solution)/shard_map/ppermute | solution.py:852
  112.3 7.4 %collective-permute-start.7 = (bf16[256,384]{1,0:T(8,128)(2,1)}, bf16[256,384]{1,0:T(8,128)(2,1)S(1)}, u32[]{:S(2)}, u32[]{:S(2)}) collective-permute-start(bf16[256,384]{1,0:T(8,128)(2,1)} %get-tuple-element.128.low_ref.low2_ref), channel_id=1, source_target_pairs={{0,2},{2,0},{1,3},{3,1},{4,6},{6,4},{5,7},{7,5},{8,10},{10,8},{9,1... | collective-permute-start | bytes 589832 | tf_op jit(solution)/shard_map/ppermute | solution.py:852
  159.4 160.4 %reduce-scatter.2.cloned.1.call-start = ((), (), s32[]{:S(2)}) async-start(), calls=%async_computation.2 | async-start | bytes 2654208 | tf_op jit(solution)/shard_map/reduce_scatter | solution.py:1105
  165.1 53.5 %collective-permute-start.14 = (bf16[384,3072]{1,0:T(8,128)(2,1)}, bf16[384,3072]{1,0:T(8,128)(2,1)S(1)}, u32[]{:S(2)}, u32[]{:S(2)}) collective-permute-start(bf16[384,3072]{1,0:T(8,128)(2,1)} %get-tuple-element.156), channel_id=1, source_target_pairs={{0,1},{1,0},{2,3},{3,2},{4,5},{5,4},{6,7},{7,6},{8,9},{9,8},{10,11... | collective-permute-start | bytes 7077896 | tf_op jit(solution)/shard_map/ppermute | solution.py:1051
  166.8 46.5 %collective-permute-start.15 = (bf16[1024,768]{1,0:T(8,128)(2,1)}, bf16[1024,768]{1,0:T(8,128)(2,1)}, u32[]{:S(2)}, u32[]{:S(2)}) collective-permute-start(bf16[1024,768]{1,0:T(8,128)(2,1)} %get-tuple-element.158), channel_id=1, source_target_pairs={{0,4},{4,0},{1,5},{5,1},{2,6},{6,2},{3,7},{7,3},{8,12},{12,8},{9,1... | collective-permute-start | bytes 4718600 | tf_op jit(solution)/shard_map/ppermute | solution.py:875
  220.8 41.4 %collective-permute-start.18 = (bf16[384,1536]{1,0:T(8,128)(2,1)}, bf16[384,1536]{1,0:T(8,128)(2,1)}, u32[]{:S(2)}, u32[]{:S(2)}) collective-permute-start(bf16[384,1536]{1,0:T(8,128)(2,1)} %get-tuple-element.182), channel_id=1, source_target_pairs={{0,1},{1,0},{2,3},{3,2},{4,5},{5,4},{6,7},{7,6},{8,9},{9,8},{10,11... | collective-permute-start | bytes 3538952 | tf_op jit(solution)/shard_map/ppermute | solution.py:1067
  222.6 187.4 %all-gather.10.cloned.1.call-start = ((), (), s32[]{:S(2)}) async-start(), calls=%async_computation.4 | async-start | bytes 7520256 | tf_op jit(solution)/shard_map/all_gather | solution.py:1141
  222.7 37.2 %collective-permute-start.16 = (bf16[512,768]{1,0:T(8,128)(2,1)S(1)}, bf16[512,768]{1,0:T(8,128)(2,1)}, u32[]{:S(2)}, u32[]{:S(2)}) collective-permute-start(bf16[512,768]{1,0:T(8,128)(2,1)S(1)} %add_convert_fusion.1), channel_id=1, source_target_pairs={{0,8},{8,0},{16,24},{24,16},{1,9},{9,1},{17,25},{25,17},{2,10},{10... | collective-permute-start | bytes 2359304 | tf_op jit(solution)/shard_map/ppermute | solution.py:875
  262.0 14.2 %collective-permute-start.17 = (bf16[256,768]{1,0:T(8,128)(2,1)}, bf16[256,768]{1,0:T(8,128)(2,1)}, u32[]{:S(2)}, u32[]{:S(2)}) collective-permute-start(bf16[256,768]{1,0:T(8,128)(2,1)} %add_convert_fusion.3), channel_id=1, source_target_pairs={{0,16},{8,24},{16,0},{24,8},{1,17},{9,25},{17,1},{25,9},{2,18},{10... | collective-permute-start | bytes 1179656 | tf_op jit(solution)/shard_map/ppermute | solution.py:875
  262.0 27.7 %collective-permute-start.23 = (bf16[384,896]{1,0:T(8,128)(2,1)}, bf16[384,896]{1,0:T(8,128)(2,1)S(1)}, u32[]{:S(2)}, u32[]{:S(2)}) collective-permute-start(bf16[384,896]{1,0:T(8,128)(2,1)} %get-tuple-element.178), channel_id=1, source_target_pairs={{0,1},{1,0},{2,3},{3,2},{4,5},{5,4},{6,7},{7,6},{8,9},{9,8},{10,11... | collective-permute-start | bytes 2064392 | tf_op jit(solution)/shard_map/ppermute | solution.py:1067
  264.3 25.4 %collective-permute-start.21 = (bf16[192,1536]{1,0:T(8,128)(2,1)}, bf16[192,1536]{1,0:T(8,128)(2,1)}, u32[]{:S(2)}, u32[]{:S(2)}) collective-permute-start(bf16[192,1536]{1,0:T(8,128)(2,1)} %add_convert_fusion.2), channel_id=1, source_target_pairs={{0,4},{4,0},{1,5},{5,1},{2,6},{6,2},{3,7},{7,3},{8,12},{12,8},{9,1... | collective-permute-start | bytes 1769480 | tf_op jit(solution)/shard_map/ppermute | solution.py:875
  282.5 13.7 %collective-permute-start.22 = (bf16[384,768]{1,0:T(8,128)(2,1)}, bf16[384,768]{1,0:T(8,128)(2,1)}, u32[]{:S(2)}, u32[]{:S(2)}) collective-permute-start(bf16[384,768]{1,0:T(8,128)(2,1)} %get-tuple-element.186), channel_id=1, source_target_pairs={{0,1},{1,0},{2,3},{3,2},{4,5},{5,4},{6,7},{7,6},{8,9},{9,8},{10,11... | collective-permute-start | bytes 1769480 | tf_op jit(solution)/shard_map/ppermute | solution.py:1067
  283.5 5.4 %collective-permute-start.20 = (f32[128,768]{1,0:T(8,128)}, f32[128,768]{1,0:T(8,128)S(1)}, u32[]{:S(2)}, u32[]{:S(2)}) collective-permute-start(f32[128,768]{1,0:T(8,128)} %get-tuple-element.191), channel_id=1, source_target_pairs={{0,2},{2,0},{1,3},{3,1},{4,6},{6,4},{5,7},{7,5},{8,10},{10,8},{9,1... | collective-permute-start | bytes 1179656 | tf_op jit(solution)/shard_map/ppermute | solution.py:852
  300.6 13.8 %collective-permute-start.24 = (bf16[192,1664]{1,0:T(8,128)(2,1)}, bf16[192,1664]{1,0:T(8,128)(2,1)S(1)}, u32[]{:S(2)}, u32[]{:S(2)}) collective-permute-start(bf16[192,1664]{1,0:T(8,128)(2,1)} %fusion.1), channel_id=1, source_target_pairs={{0,4},{4,0},{1,5},{5,1},{2,6},{6,2},{3,7},{7,3},{8,12},{12,8},{9,1... | collective-permute-start | bytes 1916936 | tf_op jit(solution)/shard_map/ppermute | solution.py:875
  300.6 8.3 %collective-permute-start.25 = (bf16[96,1536]{1,0:T(8,128)(2,1)}, bf16[96,1536]{1,0:T(8,128)(2,1)S(1)}, u32[]{:S(2)}, u32[]{:S(2)}) collective-permute-start(bf16[96,1536]{1,0:T(8,128)(2,1)} %add_convert_fusion.4), channel_id=1, source_target_pairs={{0,8},{8,0},{16,24},{24,16},{1,9},{9,1},{17,25},{25,17},{2,10},{10... | collective-permute-start | bytes 884744 | tf_op jit(solution)/shard_map/ppermute | solution.py:875
  310.2 8.2 %collective-permute-start.27 = (bf16[48,1536]{1,0:T(8,128)(2,1)S(1)}, bf16[48,1536]{1,0:T(8,128)(2,1)S(1)}, u32[]{:S(2)}, u32[]{:S(2)}) collective-permute-start(bf16[48,1536]{1,0:T(8,128)(2,1)S(1)} %add_convert_fusion.6), channel_id=1, source_target_pairs={{0,16},{8,24},{16,0},{24,8},{1,17},{9,25},{17,1},{25,9},{2,18},{10... | collective-permute-start | bytes 442376 | tf_op jit(solution)/shard_map/ppermute | solution.py:875
  321.5 8.7 %collective-permute-start.26 = (bf16[96,1664]{1,0:T(8,128)(2,1)}, bf16[96,1664]{1,0:T(8,128)(2,1)S(1)}, u32[]{:S(2)}, u32[]{:S(2)}) collective-permute-start(bf16[96,1664]{1,0:T(8,128)(2,1)} %fusion.6), channel_id=1, source_target_pairs={{0,8},{8,0},{16,24},{24,16},{1,9},{9,1},{17,25},{25,17},{2,10},{10... | collective-permute-start | bytes 958472 | tf_op jit(solution)/shard_map/ppermute | solution.py:875
  330.3 20.4 %collective-permute-start.28 = (bf16[48,1664]{1,0:T(8,128)(2,1)S(1)}, bf16[48,1664]{1,0:T(8,128)(2,1)S(1)}, u32[]{:S(2)}, u32[]{:S(2)}) collective-permute-start(bf16[48,1664]{1,0:T(8,128)(2,1)S(1)} %fusion.12), channel_id=1, source_target_pairs={{0,16},{8,24},{16,0},{24,8},{1,17},{9,25},{17,1},{25,9},{2,18},{10... | collective-permute-start | bytes 479240 | tf_op jit(solution)/shard_map/ppermute | solution.py:875
  350.8 9.0 %collective-permute-start.29 = (bf16[48,1664]{1,0:T(8,128)(2,1)S(1)}, bf16[48,1664]{1,0:T(8,128)(2,1)S(1)}, u32[]{:S(2)}, u32[]{:S(2)}) collective-permute-start(bf16[48,1664]{1,0:T(8,128)(2,1)S(1)} %fusion.9), channel_id=1, source_target_pairs={{0,16},{8,24},{16,0},{24,8},{1,17},{9,25},{17,1},{25,9},{2,18},{10... | collective-permute-start | bytes 479240 | tf_op jit(solution)/shard_map/ppermute | solution.py:875
  359.8 24.0 %collective-permute-start.30 = (bf16[96,1664]{1,0:T(8,128)(2,1)S(1)}, bf16[96,1664]{1,0:T(8,128)(2,1)S(1)}, u32[]{:S(2)}, u32[]{:S(2)}) collective-permute-start(bf16[96,1664]{1,0:T(8,128)(2,1)S(1)} %pad_maximum_fusion.4), channel_id=1, source_target_pairs={{0,8},{8,0},{16,24},{24,16},{1,9},{9,1},{17,25},{25,17},{2,10},{10... | collective-permute-start | bytes 958472 | tf_op jit(solution)/shard_map/ppermute | solution.py:875
  383.9 12.4 %collective-permute-start.31 = (bf16[192,1664]{1,0:T(8,128)(2,1)S(1)}, bf16[192,1664]{1,0:T(8,128)(2,1)S(1)}, u32[]{:S(2)}, u32[]{:S(2)}) collective-permute-start(bf16[192,1664]{1,0:T(8,128)(2,1)S(1)} %pad_maximum_fusion.1), channel_id=1, source_target_pairs={{0,4},{4,0},{1,5},{5,1},{2,6},{6,2},{3,7},{7,3},{8,12},{12,8},{9,1... | collective-permute-start | bytes 1916936 | tf_op jit(solution)/shard_map/ppermute | solution.py:875
  396.4 4.3 %collective-permute-start.32 = (bf16[384,1664]{1,0:T(8,128)(2,1)S(1)}, bf16[384,1664]{1,0:T(8,128)(2,1)S(1)}, u32[]{:S(2)}, u32[]{:S(2)}) collective-permute-start(bf16[384,1664]{1,0:T(8,128)(2,1)S(1)} %pad_maximum_fusion.own_ref), channel_id=1, source_target_pairs={{0,2},{2,0},{1,3},{3,1},{4,6},{6,4},{5,7},{7,5},{8,10},{10,8},{9,1... | collective-permute-start | bytes 3833864 | tf_op jit(solution)/shard_map/ppermute | solution.py:852
  (39 other events, 332.2 us)
Sparse Core Ops, SparseCore 0:
  10.9 64.5 all-gather.5
  159.5 55.3 all-gather.7
  222.7 81.7 reduce-scatter.1
  321.6 85.8 all-gather.9
